TPU v7x, 32 devices: a whole 2x2x4 slice. The times are simulated.
32 devices in a mesh: groups: 2 (over y), row: 4 (over z), col: 4 (over x, core).
Axes of the slice: x: 2, y: 2, z: 4, core: 2. Of those that a mesh axis runs over, the one named last changes fastest.
Arguments:
- right_side: float32 [4096, 512], P(('groups', 'row')), parts along dimension 0, may hold values from -6 to 6
- prev_factor: float32 [4096, 4096], P(('groups', 'row'), 'col'), parts along dimension 0, may hold values from -0.09375 to 0.09375
- prev_solution: float32 [8192, 512], P(('groups', 'col'), 'row'), parts along dimension 0, may hold values from -6 to 6
- window_factor: float32 [4096, 1536], P(('groups', 'row')), parts along dimension 0, may hold values from -2 to 2
Outputs:
- panel: float32 [4096, 512], P(('groups', 'row'), 'col'), parts along dimension 0
There are 2 independent parts, one for each index of `groups`. A program takes and returns all parts, laid end to end along the dimension named above; each array names one. Nothing has to cross between parts.
All inputs are finite; a program needn't handle non-finite values.
Results may differ from a plain program's by a relative error of at most 0.0001.
Values sent between devices are 32-bit elements; how exact they have to be, the bound alone decides.
No kernel may reach another device: no remote copies, remote signals or barrier semaphores. Data moves between devices by JAX's collectives and lax.ppermute only.
A program may use at most 64 MiB of HBM per device.

v0:
```python
import jax
import jax.numpy as jnp
from jax import lax
from jax.sharding import PartitionSpec as P

NRHS = 512
STEPS = 6


def spread(array, axis, root):
    mine = lax.axis_index(axis) == root
    return lax.psum(jnp.where(mine, array, jnp.zeros_like(array)), axis)


def advance(resid, tiles, order, step, slot, is_root, sender):
    local = resid[slot]

    def solve_tile():
        return jnp.dot(
            tiles[slot, :, step, :],
            local,
            precision=lax.Precision.HIGHEST,
            preferred_element_type=jnp.float32,
        )

    def empty_tile():
        return jnp.zeros_like(local)

    mine = lax.cond(is_root, solve_tile, empty_tile)
    solved = sender(mine)
    update = jnp.einsum(
        "sij,jn->sin", tiles[:, :, step, :], solved, precision=lax.Precision.HIGHEST
    )
    later = (order > step)[:, None, None]
    resid = jnp.where(later, resid - update, resid)
    resid = jnp.where((order == step)[:, None, None], solved[None], resid)
    return resid


def body(right_side, prev_factor, prev_solution, window_factor):
    row_count = lax.axis_size("row")
    row_index = lax.axis_index("row")
    col_count = lax.axis_size("col")
    col_index = lax.axis_index("col")
    blocks = window_factor.shape[1] // STEPS
    slots = right_side.shape[0] // blocks
    partial_value = jnp.dot(
        prev_factor,
        lax.all_gather(prev_solution, "row", axis=1, tiled=True),
        precision=lax.Precision.HIGHEST,
        preferred_element_type=jnp.float32,
    )
    tiles = window_factor.reshape(slots, blocks, STEPS, blocks)
    order = jnp.arange(slots, dtype=jnp.int32) * row_count + row_index
    prior = lax.psum(partial_value, "col")
    resid = (right_side - prior).reshape(slots, blocks, -1)
    for step in range(STEPS):
        root = step % row_count
        resid = advance(
            resid,
            tiles,
            order,
            step,
            step // row_count,
            row_index == root,
            lambda solved: spread(solved, "row", root),
        )
    width = NRHS // col_count
    return lax.dynamic_slice_in_dim(resid.reshape(slots * blocks, -1), col_index * width, width, 1)


def solution(mesh):
    in_specs = (
        P(("groups", "row"), None),
        P(("groups", "row"), "col"),
        P(("groups", "col"), "row"),
        P(("groups", "row"), None),
    )
    out_specs = P(("groups", "row"), "col")
    return jax.shard_map(body, mesh=mesh, in_specs=in_specs, out_specs=out_specs, check_vma=False)
```

profile of v0, /device:TPU:0, one launch (start us, length us, event | category | flops | bytes accessed | tf_op | source)
XLA Modules:
  0.0 414.7 jit_solution(410126882840946337)
XLA Ops:
  7.3 50.6 %all-gather.2.cloned.1.call-done = f32[1024,512]{1,0:T(8,128)} async-done(((f32[1024,128]{1,0:T(8,128)}), f32[1024,512]{1,0:T(8,128)}) %all-gather.2.cloned.1.call-update) | async-done | bytes 2097168 | tf_op jit(solution)/shard_map/all_gather | solution.py:49
  57.9 6.1 %fusion.48 = f32[512,512]{1,0:T(8,128)} fusion(f32[512,1024]{1,0:T(8,128)S(1)} %copy-done, f32[1024,512]{1,0:T(8,128)} %all-gather.2.cloned.1.call-done), kind=kOutput, calls=%fused_computation.80 | convolution fusion | flops 3221225472 | bytes 5242880 | tf_op jit(solution)/shard_map/dot_general | solution.py:47
  64.1 3.5 copy.11
  67.6 3.8 reshape.56
  71.4 27.1 %all-reduce.8.cloned.1.call-done = f32[512,512]{1,0:T(8,128)} async-done(((f32[512,512]{1,0:T(8,128)}), f32[512,512]{1,0:T(8,128)}) %all-reduce.8.cloned.1.call-update) | async-done | bytes 1048592 | tf_op jit(solution)/shard_map/psum | solution.py:55
  98.5 2.8 sub.21
  101.3 8.1 %conditional.6 = (f32[256,512]{1,0:T(8,128)}) conditional(s32[]{:T(128)} %convert_element_type.15, () %tuple.46, (f32[2,256,6,256]{1,0,3,2:T(2,128)S(1)}, f32[512,512]{1,0:T(8,128)}) %tuple.47), branch_computations={%region_1.0_spmd, %region_2.0_spmd} | conditional | flops 402653184 | bytes 8126472 | solution.py:29
  101.3 3.9 copy.12
  107.0 2.5 fusion
  115.8 31.5 %all-reduce.10.cloned.1.call-done = f32[256,512]{1,0:T(8,128)} async-done(((f32[256,512]{1,0:T(8,128)}), f32[256,512]{1,0:T(8,128)}) %all-reduce.10.cloned.1.call-update) | async-done | bytes 524304 | tf_op jit(solution)/shard_map/psum | solution.py:12
  147.4 3.7 fusion.34
  155.0 43.6 %all-reduce.12.cloned.1.call-done = f32[256,512]{1,0:T(8,128)} async-done(((f32[256,512]{1,0:T(8,128)}), f32[256,512]{1,0:T(8,128)}) %all-reduce.12.cloned.1.call-update) | async-done | bytes 524304 | tf_op jit(solution)/shard_map/psum | solution.py:12
  198.6 3.7 fusion.33
  206.2 44.4 %all-reduce.14.cloned.1.call-done = f32[256,512]{1,0:T(8,128)} async-done(((f32[256,512]{1,0:T(8,128)}), f32[256,512]{1,0:T(8,128)}) %all-reduce.14.cloned.1.call-update) | async-done | bytes 524304 | tf_op jit(solution)/shard_map/psum | solution.py:12
  250.5 3.7 fusion.32
  258.1 44.7 %all-reduce.16.cloned.1.call-done = f32[256,512]{1,0:T(8,128)} async-done(((f32[256,512]{1,0:T(8,128)}), f32[256,512]{1,0:T(8,128)}) %all-reduce.16.cloned.1.call-update) | async-done | bytes 524304 | tf_op jit(solution)/shard_map/psum | solution.py:12
  302.8 3.7 fusion.31
  306.6 8.2 %conditional.10 = (f32[256,512]{1,0:T(8,128)}) conditional(s32[]{:T(128)} %convert_element_type.15, () %tuple.42, (f32[2,256,6,256]{1,0,3,2:T(2,128)S(1)}, f32[2,256,512]{2,1,0:T(8,128)}) %tuple.51), branch_computations={%region_13.14_spmd, %region_14.15_spmd} | conditional | flops 402653184 | bytes 8126472 | solution.py:29
  306.6 3.9 copy.20
  312.4 2.5 fusion.19
  318.8 34.5 %all-reduce.18.cloned.1.call-done = f32[256,512]{1,0:T(8,128)} async-done(((f32[256,512]{1,0:T(8,128)}), f32[256,512]{1,0:T(8,128)}) %all-reduce.18.cloned.1.call-update) | async-done | bytes 524304 | tf_op jit(solution)/shard_map/psum | solution.py:12
  353.3 3.7 fusion.30
  361.1 43.5 %all-reduce.20.cloned.1.call-done = f32[256,512]{1,0:T(8,128)} async-done(((f32[256,512]{1,0:T(8,128)}), f32[256,512]{1,0:T(8,128)}) %all-reduce.20.cloned.1.call-update) | async-done | bytes 524304 | tf_op jit(solution)/shard_map/psum | solution.py:12
  404.7 2.5 fusion.29
  (52 shorter events, 34.5 us)
Async XLA Ops:
  6.5 51.4 %copy-start = (f32[512,1024]{1,0:T(8,128)S(1)}, f32[512,1024]{1,0:T(8,128)}, u32[]{:S(2)}) copy-start(f32[512,1024]{1,0:T(8,128)} %param.17) | copy-start | bytes 6291460
  6.5 51.4 %all-gather.2.cloned.1.call-start = ((), (), s32[]{:S(2)}) async-start(), calls=%async_computation | async-start | bytes 2621440 | tf_op jit(solution)/shard_map/all_gather | solution.py:49
  7.3 91.3 %all-reduce.8.cloned.1.call-start = ((), (), s32[]{:S(2)}) async-start(), calls=%async_computation.1 | async-start | bytes 2097152 | tf_op jit(solution)/shard_map/psum | solution.py:55
  64.0 83.4 %all-reduce.10.cloned.1.call-start = ((), (), s32[]{:S(2)}) async-start(), calls=%async_computation.2 | async-start | bytes 1048576 | tf_op jit(solution)/shard_map/psum | solution.py:12
  111.3 87.3 %all-reduce.12.cloned.1.call-start = ((), (), s32[]{:S(2)}) async-start(), calls=%async_computation.3 | async-start | bytes 1048576 | tf_op jit(solution)/shard_map/psum | solution.py:12
  152.9 97.7 %all-reduce.14.cloned.1.call-start = ((), (), s32[]{:S(2)}) async-start(), calls=%async_computation.4 | async-start | bytes 1048576 | tf_op jit(solution)/shard_map/psum | solution.py:12
  204.1 98.8 %all-reduce.16.cloned.1.call-start = ((), (), s32[]{:S(2)}) async-start(), calls=%async_computation.5 | async-start | bytes 1048576 | tf_op jit(solution)/shard_map/psum | solution.py:12
  256.0 97.3 %all-reduce.18.cloned.1.call-start = ((), (), s32[]{:S(2)}) async-start(), calls=%async_computation.6 | async-start | bytes 1048576 | tf_op jit(solution)/shard_map/psum | solution.py:12
  316.7 87.9 %all-reduce.20.cloned.1.call-start = ((), (), s32[]{:S(2)}) async-start(), calls=%async_computation.7 | async-start | bytes 1048576 | tf_op jit(solution)/shard_map/psum | solution.py:12
  357.9 46.7 %copy-start.2 = (f32[2,256,512]{2,1,0:T(8,128)S(1)}, f32[2,256,512]{2,1,0:T(8,128)}, u32[]{:S(2)}) copy-start(f32[2,256,512]{2,1,0:T(8,128)} %fusion.30) | copy-start | bytes 3145732
  357.9 49.9 %copy-start.1 = (f32[512,1024]{1,0:T(8,128)S(1)}, f32[512,1024]{1,0:T(8,128)}, u32[]{:S(2)}) copy-start(f32[512,1024]{1,0:T(8,128)} %param.17) | copy-start | bytes 6291460
Sparse Core Ops, SparseCore 0:
  8.9 48.9 all-gather.1
  64.1 34.3 all-reduce.7
  111.4 35.8 all-reduce.9
  153.0 45.5 all-reduce.11
  204.2 46.2 all-reduce.13
  256.1 46.6 all-reduce.15
  316.9 36.4 all-reduce.17
  358.9 45.6 all-reduce.19
where the time goes:
time: 416 us; the launch traced here: 415 us
  waiting for transfers between devices  321 us (77%)
  local copies, waits for them, and re-layouts  37.9 us (9%)
  matrix products  32.2 us (8%)
  between operations  13.5 us (3%)
  other arithmetic  9.93 us (2%)
    psum x6, waiting for transfers between devices, spread(): return lax.psum(jnp.where(mine, array, jnp.zeros_like(array)), axis)  242 us
    all_gather x1, waiting for transfers between devices, body(): lax.all_gather(prev_solution, 'row', axis=1, tiled=True)  50.6 us
    psum x1, waiting for transfers between devices, body(): prior = lax.psum(partial_value, 'col')  27.1 us
    dot_general x6, matrix products, advance(): jnp.einsum('sij,jn->sin', tiles[:, :, step, :], solved, precision=lax.Pre...  21.2 us
    unnamed x13, local copies, waits for them, and re-layouts  16.1 us
    another operation x6, local copies, waits for them, and re-layouts  11.3 us
  transfers between devices with their start and end apart: 8, of which 8 were waited for; matrix products, arithmetic and copies ran while one was open for 5% of the time, Pallas kernels for 0%

commit v1 on v0

v1 whole, which is shorter than its diff:
```python
import jax
import jax.numpy as jnp
from jax import lax
from jax.sharding import PartitionSpec as P

NRHS = 512
STEPS = 6
HIGH = lax.Precision.HIGH


def mul(a, b):
    return jnp.dot(a, b, precision=HIGH, preferred_element_type=jnp.float32)


def general(right_side, prev_factor, prev_solution, window_factor):
    row_count = lax.axis_size("row")
    row_index = lax.axis_index("row")
    col_count = lax.axis_size("col")
    col_index = lax.axis_index("col")
    blocks = window_factor.shape[1] // STEPS
    slots = right_side.shape[0] // blocks
    width = NRHS // col_count
    partial_value = mul(prev_factor, lax.all_gather(prev_solution, "row", axis=1, tiled=True))
    prior = lax.psum_scatter(partial_value, "col", scatter_dimension=1, tiled=True)
    mine = lax.dynamic_slice_in_dim(right_side, col_index * width, width, 1)
    resid = (mine - prior).reshape(slots, blocks, width)
    tiles = window_factor.reshape(slots, blocks, STEPS, blocks)
    order = jnp.arange(slots, dtype=jnp.int32) * row_count + row_index
    for step in range(STEPS):
        root = step % row_count
        solved = mul(tiles[step // row_count, :, step, :], resid[step // row_count])
        solved = lax.psum(jnp.where(row_index == root, solved, jnp.zeros_like(solved)), "row")
        update = jnp.einsum("sij,jn->sin", tiles[:, :, step, :], solved, precision=HIGH)
        resid = jnp.where((order > step)[:, None, None], resid - update, resid)
        resid = jnp.where((order == step)[:, None, None], solved[None], resid)
    return resid.reshape(slots * blocks, width)


def gather_row(piece, chunks):
    row_index = lax.axis_index("row")
    rows = piece.shape[0] // chunks
    up = down = [piece[i * rows : (i + 1) * rows] for i in range(chunks)]
    ups, downs = [], []
    for hop in range(3):
        up = [lax.ppermute(c, "row", [(i, i + 1) for i in range(hop, 3)]) for c in up]
        down = [lax.ppermute(c, "row", [(i + 1, i) for i in range(0, 3 - hop)]) for c in down]
        ups.append(up)
        downs.append(down)
    got = [piece]
    for s in range(1, 4):
        got.append(
            jnp.concatenate(
                [jnp.where(row_index >= s, u, d) for u, d in zip(ups[s - 1], downs[3 - s])], 0
            )
        )
    return got


def line4(right_side, prev_factor, prev_solution, window_factor):
    row_index = lax.axis_index("row")
    col_index = lax.axis_index("col")
    core, side = col_index % 2, col_index // 2
    blocks = window_factor.shape[1] // STEPS
    width = NRHS // 4
    rows = right_side.shape[0]

    got = gather_row(prev_solution, 2)
    parts = jnp.stack([mul(prev_factor, g) for g in got])

    def part(owner):
        return lax.dynamic_index_in_dim(parts, (row_index - owner) % 4, 0, keepdims=False)

    away = jnp.stack([part(1 - core), part(3 - core)])
    keep = jnp.stack([part(core), part(2 + core)])
    keep = keep + lax.ppermute(away, "col", [(0, 1), (1, 0), (2, 3), (3, 2)])
    other = lax.dynamic_index_in_dim(keep, 1 - side, 0, keepdims=False)
    own = lax.dynamic_index_in_dim(keep, side, 0, keepdims=False)
    prior = own + lax.ppermute(other, "col", [(0, 2), (2, 0), (1, 3), (3, 1)])
    mine = lax.dynamic_slice_in_dim(right_side, col_index * width, width, 1)
    resid = mine - prior

    def tile(slot, step):
        return window_factor[slot * blocks : (slot + 1) * blocks, step * blocks : (step + 1) * blocks]

    low, high = resid[:blocks], resid[blocks:]
    at = {}
    done = {}
    for step in range(STEPS):
        root, slot = step % 4, step // 4
        value = low if slot == 0 else high
        for k in range(step):
            value = value - mul(tile(slot, k), at[k, root])
        solved = mul(tile(slot, step), value)
        done[step] = solved
        for d in [(root + 1) % 4, (root + 2) % 4, (root + 3) % 4]:
            if d + 4 > step:
                at[step, d] = lax.ppermute(solved, "row", [(root, d)])
        at[step, root] = solved
    tails = [high, high]
    for i, d in enumerate((2, 3)):
        for k in range(STEPS):
            tails[i] = tails[i] - mul(tile(1, k), at[k, d])
    low = lax.select_n(row_index, *[done[k] for k in range(4)])
    high = lax.select_n(row_index, done[4], done[5], tails[0], tails[1])
    return jnp.concatenate([low, high], 0)


def body(right_side, prev_factor, prev_solution, window_factor):
    blocks = window_factor.shape[1] // STEPS
    slots = right_side.shape[0] // blocks
    if lax.axis_size("row") == 4 and lax.axis_size("col") == 4 and slots == 2:
        return line4(right_side, prev_factor, prev_solution, window_factor)
    return general(right_side, prev_factor, prev_solution, window_factor)


def solution(mesh):
    in_specs = (
        P(("groups", "row"), None),
        P(("groups", "row"), "col"),
        P(("groups", "col"), "row"),
        P(("groups", "row"), None),
    )
    out_specs = P(("groups", "row"), "col")
    return jax.shard_map(body, mesh=mesh, in_specs=in_specs, out_specs=out_specs, check_vma=False)
```

time: 416 us -> 114 us (0.27)
  the two profiles are of different devices: /device:TPU:0 before, /device:TPU:16 now
where the time goes in v1:
time: 114 us; the launch traced here: 113 us
  starting transfers between devices  46.8 us (41%)
  waiting for transfers between devices  36.9 us (32%)
  matrix products  21.7 us (19%)
  local copies, waits for them, and re-layouts  3.54 us (3%)
  other arithmetic  3.12 us (3%)
    ppermute x17, waiting for transfers between devices, line4(): at[step, d] = lax.ppermute(solved, 'row', [(root, d)])  24.5 us
    dot_general x37, matrix products, mul(): return jnp.dot(a, b, precision=HIGH, preferred_element_type=jnp.float32)  21.7 us
    ppermute x17, starting transfers between devices, line4(): at[step, d] = lax.ppermute(solved, 'row', [(root, d)])  16.6 us
    ppermute x6, starting transfers between devices, gather_row(): lax.ppermute(c, 'row', [(i, i + 1) for i in range(hop, 3)])  15.2 us
    ppermute x6, starting transfers between devices, gather_row(): lax.ppermute(c, 'row', [(i + 1, i) for i in range(0, 3 - hop)])  13.4 us
    ppermute x1, waiting for transfers between devices, line4(): prior = own + lax.ppermute(other, 'col', [(0, 2), (2, 0), (1, 3), (3, 1)])  5.61 us
    ppermute x6, waiting for transfers between devices, gather_row(): lax.ppermute(c, 'row', [(i, i + 1) for i in range(hop, 3)])  3.96 us
  transfers between devices with their start and end apart: 31, of which 9 were waited for; matrix products, arithmetic and copies ran while one was open for 20% of the time, Pallas kernels for 0%

profile of v1, /device:TPU:16, one launch (start us, length us, event | category | flops | bytes accessed | tf_op | source)
XLA Modules:
  0.0 112.9 jit_solution(10517690374775347888)
XLA Ops:
  1.2 3.5 %collective-permute-start.4 = (f32[512,128]{1,0:T(8,128)S(1)}, f32[512,128]{1,0:T(8,128)S(1)}, u32[]{:S(2)}, u32[]{:S(2)}) collective-permute-start(f32[512,128]{1,0:T(8,128)S(1)} %get-tuple-element.12), channel_id=1, source_target_pairs={{0,4},{4,8},{8,12},{1,5},{5,9},{9,13},{2,6},{6,10},{10,14},{3,7},{... | collective-permute-start | bytes 786440 | tf_op jit(solution)/shard_map/ppermute | solution.py:45
  4.7 1.9 %collective-permute-start = (f32[512,128]{1,0:T(8,128)S(1)}, f32[512,128]{1,0:T(8,128)S(1)}, u32[]{:S(2)}, u32[]{:S(2)}) collective-permute-start(f32[512,128]{1,0:T(8,128)S(1)} %get-tuple-element.11), channel_id=1, source_target_pairs={{0,4},{4,8},{8,12},{1,5},{5,9},{9,13},{2,6},{6,10},{10,14},{3,7},{... | collective-permute-start | bytes 786440 | tf_op jit(solution)/shard_map/ppermute | solution.py:45
  6.6 3.9 %collective-permute-start.5 = (f32[512,128]{1,0:T(8,128)S(1)}, f32[512,128]{1,0:T(8,128)S(1)}, u32[]{:S(2)}, u32[]{:S(2)}) collective-permute-start(f32[512,128]{1,0:T(8,128)S(1)} %get-tuple-element.12), channel_id=1, source_target_pairs={{4,0},{8,4},{12,8},{5,1},{9,5},{13,9},{6,2},{10,6},{14,10},{7,3},{... | collective-permute-start | bytes 786440 | tf_op jit(solution)/shard_map/ppermute | solution.py:46
  10.6 2.4 %collective-permute-start.1 = (f32[512,128]{1,0:T(8,128)S(1)}, f32[512,128]{1,0:T(8,128)S(1)}, u32[]{:S(2)}, u32[]{:S(2)}) collective-permute-start(f32[512,128]{1,0:T(8,128)S(1)} %get-tuple-element.11), channel_id=1, source_target_pairs={{4,0},{8,4},{12,8},{5,1},{9,5},{13,9},{6,2},{10,6},{14,10},{7,3},{... | collective-permute-start | bytes 786440 | tf_op jit(solution)/shard_map/ppermute | solution.py:46
  13.0 3.5 %collective-permute-start.9 = (f32[512,128]{1,0:T(8,128)S(1)}, f32[512,128]{1,0:T(8,128)}, u32[]{:S(2)}, u32[]{:S(2)}) collective-permute-start(f32[512,128]{1,0:T(8,128)S(1)} %collective-permute-done.4), channel_id=1, source_target_pairs={{4,8},{8,12},{5,9},{9,13},{6,10},{10,14},{7,11},{11,15},{20,24},{2... | collective-permute-start | bytes 786440 | tf_op jit(solution)/shard_map/ppermute | solution.py:45
  17.3 3.5 %collective-permute-start.8 = (f32[512,128]{1,0:T(8,128)S(1)}, f32[512,128]{1,0:T(8,128)}, u32[]{:S(2)}, u32[]{:S(2)}) collective-permute-start(f32[512,128]{1,0:T(8,128)S(1)} %collective-permute-done), channel_id=1, source_target_pairs={{4,8},{8,12},{5,9},{9,13},{6,10},{10,14},{7,11},{11,15},{20,24},{2... | collective-permute-start | bytes 786440 | tf_op jit(solution)/shard_map/ppermute | solution.py:45
  20.8 3.7 %collective-permute-start.6 = (f32[512,128]{1,0:T(8,128)S(1)}, f32[512,128]{1,0:T(8,128)}, u32[]{:S(2)}, u32[]{:S(2)}) collective-permute-start(f32[512,128]{1,0:T(8,128)S(1)} %collective-permute-done.5), channel_id=1, source_target_pairs={{4,0},{8,4},{5,1},{9,5},{6,2},{10,6},{7,3},{11,7},{20,16},{24,20},... | collective-permute-start | bytes 786440 | tf_op jit(solution)/shard_map/ppermute | solution.py:46
  24.6 2.0 %collective-permute-start.2 = (f32[512,128]{1,0:T(8,128)S(1)}, f32[512,128]{1,0:T(8,128)}, u32[]{:S(2)}, u32[]{:S(2)}) collective-permute-start(f32[512,128]{1,0:T(8,128)S(1)} %collective-permute-done.1), channel_id=1, source_target_pairs={{4,0},{8,4},{5,1},{9,5},{6,2},{10,6},{7,3},{11,7},{20,16},{24,20},... | collective-permute-start | bytes 786440 | tf_op jit(solution)/shard_map/ppermute | solution.py:46
  26.6 2.0 %convolution_bitcast_fusion.3 = f32[1,512,128]{2,1,0:T(8,128)S(1)} fusion(f32[512,1024]{1,0:T(8,128)S(1)} %copy-done, f32[1024,128]{1,0:T(8,128)} %param.6), kind=kOutput, calls=%fused_computation.3 | convolution fusion | flops 402653184 | bytes 2883584 | tf_op jit(solution)/shard_map/dot_general | solution.py:12
  28.7 1.3 %collective-permute-start.11 = (f32[512,128]{1,0:T(8,128)}, f32[512,128]{1,0:T(8,128)S(1)}, u32[]{:S(2)}, u32[]{:S(2)}) collective-permute-start(f32[512,128]{1,0:T(8,128)} %collective-permute-done.9), channel_id=1, source_target_pairs={{8,12},{9,13},{10,14},{11,15},{24,28},{25,29},{26,30},{27,31}} | collective-permute-start | bytes 786440 | tf_op jit(solution)/shard_map/ppermute | solution.py:45
  30.0 1.6 %collective-permute-start.10 = (f32[512,128]{1,0:T(8,128)}, f32[512,128]{1,0:T(8,128)S(1)}, u32[]{:S(2)}, u32[]{:S(2)}) collective-permute-start(f32[512,128]{1,0:T(8,128)} %collective-permute-done.8), channel_id=1, source_target_pairs={{8,12},{9,13},{10,14},{11,15},{24,28},{25,29},{26,30},{27,31}} | collective-permute-start | bytes 786440 | tf_op jit(solution)/shard_map/ppermute | solution.py:45
  37.0 2.8 %collective-permute-done.10 = f32[512,128]{1,0:T(8,128)S(1)} collective-permute-done((f32[512,128]{1,0:T(8,128)}, f32[512,128]{1,0:T(8,128)S(1)}, u32[]{:S(2)}, u32[]{:S(2)}) %collective-permute-start.10) | collective-permute-done | bytes 262176 | tf_op jit(solution)/shard_map/ppermute | solution.py:45
  42.9 2.1 %collective-permute-done.12 = f32[2,512,128]{2,1,0:T(8,128)S(1)} collective-permute-done((f32[2,512,128]{2,1,0:T(8,128)}, f32[2,512,128]{2,1,0:T(8,128)S(1)}, u32[]{:S(2)}, u32[]{:S(2)}) %collective-permute-start.12) | collective-permute-done | bytes 524320 | tf_op jit(solution)/shard_map/ppermute | solution.py:75
  45.3 1.6 %collective-permute-start.13 = (f32[512,128]{0,1:T(8,128)S(1)}, f32[512,128]{0,1:T(8,128)S(1)}, u32[]{:S(2)}, u32[]{:S(2)}) collective-permute-start(f32[512,128]{0,1:T(8,128)S(1)} %copy.14), channel_id=1, source_target_pairs={{0,2},{2,0},{1,3},{3,1},{4,6},{6,4},{5,7},{7,5},{8,10},{10,8},{9,1... | collective-permute-start | bytes 786440 | tf_op jit(solution)/shard_map/ppermute | solution.py:78
  48.1 5.6 %collective-permute-done.13 = f32[512,128]{0,1:T(8,128)S(1)} collective-permute-done((f32[512,128]{0,1:T(8,128)S(1)}, f32[512,128]{0,1:T(8,128)S(1)}, u32[]{:S(2)}, u32[]{:S(2)}) %collective-permute-start.13) | collective-permute-done | bytes 262176 | tf_op jit(solution)/shard_map/ppermute | solution.py:78
  55.7 1.6 %collective-permute-start.15 = (f32[256,128]{0,1:T(8,128)S(1)}, f32[256,128]{0,1:T(8,128)S(1)}, u32[]{:S(2)}, u32[]{:S(2)}) collective-permute-start(f32[256,128]{0,1:T(8,128)S(1)} %bitcast.186), channel_id=1, source_target_pairs={{0,8},{1,9},{2,10},{3,11},{16,24},{17,25},{18,26},{19,27}} | collective-permute-start | bytes 393224 | tf_op jit(solution)/shard_map/ppermute | solution.py:97
  60.5 1.3 %collective-permute-start.16 = (f32[256,128]{0,1:T(8,128)S(1)}, f32[256,128]{0,1:T(8,128)S(1)}, u32[]{:S(2)}, u32[]{:S(2)}) collective-permute-start(f32[256,128]{0,1:T(8,128)S(1)} %bitcast.182), channel_id=1, source_target_pairs={{4,8},{5,9},{6,10},{7,11},{20,24},{21,25},{22,26},{23,27}} | collective-permute-start | bytes 393224 | tf_op jit(solution)/shard_map/ppermute | solution.py:97
  64.4 15.0 %collective-permute-done.16 = f32[256,128]{0,1:T(8,128)S(1)} collective-permute-done((f32[256,128]{0,1:T(8,128)S(1)}, f32[256,128]{0,1:T(8,128)S(1)}, u32[]{:S(2)}, u32[]{:S(2)}) %collective-permute-start.16) | collective-permute-done | bytes 131104 | tf_op jit(solution)/shard_map/ppermute | solution.py:97
  83.2 1.3 %collective-permute-start.19 = (f32[256,128]{0,1:T(8,128)S(1)}, f32[256,128]{0,1:T(8,128)S(1)}, u32[]{:S(2)}, u32[]{:S(2)}) collective-permute-start(f32[256,128]{0,1:T(8,128)S(1)} %bitcast.179), channel_id=1, source_target_pairs={{8,12},{9,13},{10,14},{11,15},{24,28},{25,29},{26,30},{27,31}} | collective-permute-start | bytes 393224 | tf_op jit(solution)/shard_map/ppermute | solution.py:97
  84.5 1.3 %collective-permute-start.21 = (f32[256,128]{0,1:T(8,128)S(1)}, f32[256,128]{0,1:T(8,128)S(1)}, u32[]{:S(2)}, u32[]{:S(2)}) collective-permute-start(f32[256,128]{0,1:T(8,128)S(1)} %bitcast.180), channel_id=1, source_target_pairs={{8,0},{9,1},{10,2},{11,3},{24,16},{25,17},{26,18},{27,19}} | collective-permute-start | bytes 393224 | tf_op jit(solution)/shard_map/ppermute | solution.py:97
  86.5 1.3 %collective-permute-start.23 = (f32[256,128]{0,1:T(8,128)S(1)}, f32[256,128]{0,1:T(8,128)S(1)}, u32[]{:S(2)}, u32[]{:S(2)}) collective-permute-start(f32[256,128]{0,1:T(8,128)S(1)} %bitcast.181), channel_id=1, source_target_pairs={{8,4},{9,5},{10,6},{11,7},{24,20},{25,21},{26,22},{27,23}} | collective-permute-start | bytes 393224 | tf_op jit(solution)/shard_map/ppermute | solution.py:97
  99.8 1.3 %collective-permute-start.28 = (f32[256,128]{0,1:T(8,128)S(1)}, f32[256,128]{0,1:T(8,128)S(1)}, u32[]{:S(2)}, u32[]{:S(2)}) collective-permute-start(f32[256,128]{0,1:T(8,128)S(1)} %convolution_bitcast_fusion.16), channel_id=1, source_target_pairs={{4,8},{5,9},{6,10},{7,11},{20,24},{21,25},{22,26},{23,27}} | collective-permute-start | bytes 393224 | tf_op jit(solution)/shard_map/ppermute | solution.py:97
  101.1 6.1 %collective-permute-done.27 = f32[256,128]{0,1:T(8,128)S(1)} collective-permute-done((f32[256,128]{0,1:T(8,128)S(1)}, f32[256,128]{0,1:T(8,128)S(1)}, u32[]{:S(2)}, u32[]{:S(2)}) %collective-permute-start.27) | collective-permute-done | bytes 131104 | tf_op jit(solution)/shard_map/ppermute | solution.py:97
  108.2 3.3 %collective-permute-done.28 = f32[256,128]{0,1:T(8,128)S(1)} collective-permute-done((f32[256,128]{0,1:T(8,128)S(1)}, f32[256,128]{0,1:T(8,128)S(1)}, u32[]{:S(2)}, u32[]{:S(2)}) %collective-permute-start.28) | collective-permute-done | bytes 131104 | tf_op jit(solution)/shard_map/ppermute | solution.py:97
  (98 shorter events, 38.2 us)
Async XLA Ops:
  1.2 11.7 %collective-permute-start.4 = (f32[512,128]{1,0:T(8,128)S(1)}, f32[512,128]{1,0:T(8,128)S(1)}, u32[]{:S(2)}, u32[]{:S(2)}) collective-permute-start(f32[512,128]{1,0:T(8,128)S(1)} %get-tuple-element.12), channel_id=1, source_target_pairs={{0,4},{4,8},{8,12},{1,5},{5,9},{9,13},{2,6},{6,10},{10,14},{3,7},{... | collective-permute-start | bytes 786440 | tf_op jit(solution)/shard_map/ppermute | solution.py:45
  4.7 12.6 %collective-permute-start = (f32[512,128]{1,0:T(8,128)S(1)}, f32[512,128]{1,0:T(8,128)S(1)}, u32[]{:S(2)}, u32[]{:S(2)}) collective-permute-start(f32[512,128]{1,0:T(8,128)S(1)} %get-tuple-element.11), channel_id=1, source_target_pairs={{0,4},{4,8},{8,12},{1,5},{5,9},{9,13},{2,6},{6,10},{10,14},{3,7},{... | collective-permute-start | bytes 786440 | tf_op jit(solution)/shard_map/ppermute | solution.py:45
  6.6 14.2 %collective-permute-start.5 = (f32[512,128]{1,0:T(8,128)S(1)}, f32[512,128]{1,0:T(8,128)S(1)}, u32[]{:S(2)}, u32[]{:S(2)}) collective-permute-start(f32[512,128]{1,0:T(8,128)S(1)} %get-tuple-element.12), channel_id=1, source_target_pairs={{4,0},{8,4},{12,8},{5,1},{9,5},{13,9},{6,2},{10,6},{14,10},{7,3},{... | collective-permute-start | bytes 786440 | tf_op jit(solution)/shard_map/ppermute | solution.py:46
  10.6 14.0 %collective-permute-start.1 = (f32[512,128]{1,0:T(8,128)S(1)}, f32[512,128]{1,0:T(8,128)S(1)}, u32[]{:S(2)}, u32[]{:S(2)}) collective-permute-start(f32[512,128]{1,0:T(8,128)S(1)} %get-tuple-element.11), channel_id=1, source_target_pairs={{4,0},{8,4},{12,8},{5,1},{9,5},{13,9},{6,2},{10,6},{14,10},{7,3},{... | collective-permute-start | bytes 786440 | tf_op jit(solution)/shard_map/ppermute | solution.py:46
  13.0 15.8 %collective-permute-start.9 = (f32[512,128]{1,0:T(8,128)S(1)}, f32[512,128]{1,0:T(8,128)}, u32[]{:S(2)}, u32[]{:S(2)}) collective-permute-start(f32[512,128]{1,0:T(8,128)S(1)} %collective-permute-done.4), channel_id=1, source_target_pairs={{4,8},{8,12},{5,9},{9,13},{6,10},{10,14},{7,11},{11,15},{20,24},{2... | collective-permute-start | bytes 786440 | tf_op jit(solution)/shard_map/ppermute | solution.py:45
  17.3 12.7 %collective-permute-start.8 = (f32[512,128]{1,0:T(8,128)S(1)}, f32[512,128]{1,0:T(8,128)}, u32[]{:S(2)}, u32[]{:S(2)}) collective-permute-start(f32[512,128]{1,0:T(8,128)S(1)} %collective-permute-done), channel_id=1, source_target_pairs={{4,8},{8,12},{5,9},{9,13},{6,10},{10,14},{7,11},{11,15},{20,24},{2... | collective-permute-start | bytes 786440 | tf_op jit(solution)/shard_map/ppermute | solution.py:45
  20.8 10.8 %collective-permute-start.6 = (f32[512,128]{1,0:T(8,128)S(1)}, f32[512,128]{1,0:T(8,128)}, u32[]{:S(2)}, u32[]{:S(2)}) collective-permute-start(f32[512,128]{1,0:T(8,128)S(1)} %collective-permute-done.5), channel_id=1, source_target_pairs={{4,0},{8,4},{5,1},{9,5},{6,2},{10,6},{7,3},{11,7},{20,16},{24,20},... | collective-permute-start | bytes 786440 | tf_op jit(solution)/shard_map/ppermute | solution.py:46
  24.6 8.8 %collective-permute-start.2 = (f32[512,128]{1,0:T(8,128)S(1)}, f32[512,128]{1,0:T(8,128)}, u32[]{:S(2)}, u32[]{:S(2)}) collective-permute-start(f32[512,128]{1,0:T(8,128)S(1)} %collective-permute-done.1), channel_id=1, source_target_pairs={{4,0},{8,4},{5,1},{9,5},{6,2},{10,6},{7,3},{11,7},{20,16},{24,20},... | collective-permute-start | bytes 786440 | tf_op jit(solution)/shard_map/ppermute | solution.py:46
  28.7 8.3 %collective-permute-start.11 = (f32[512,128]{1,0:T(8,128)}, f32[512,128]{1,0:T(8,128)S(1)}, u32[]{:S(2)}, u32[]{:S(2)}) collective-permute-start(f32[512,128]{1,0:T(8,128)} %collective-permute-done.9), channel_id=1, source_target_pairs={{8,12},{9,13},{10,14},{11,15},{24,28},{25,29},{26,30},{27,31}} | collective-permute-start | bytes 786440 | tf_op jit(solution)/shard_map/ppermute | solution.py:45
  30.0 9.8 %collective-permute-start.10 = (f32[512,128]{1,0:T(8,128)}, f32[512,128]{1,0:T(8,128)S(1)}, u32[]{:S(2)}, u32[]{:S(2)}) collective-permute-start(f32[512,128]{1,0:T(8,128)} %collective-permute-done.8), channel_id=1, source_target_pairs={{8,12},{9,13},{10,14},{11,15},{24,28},{25,29},{26,30},{27,31}} | collective-permute-start | bytes 786440 | tf_op jit(solution)/shard_map/ppermute | solution.py:45
  45.3 8.4 %collective-permute-start.13 = (f32[512,128]{0,1:T(8,128)S(1)}, f32[512,128]{0,1:T(8,128)S(1)}, u32[]{:S(2)}, u32[]{:S(2)}) collective-permute-start(f32[512,128]{0,1:T(8,128)S(1)} %copy.14), channel_id=1, source_target_pairs={{0,2},{2,0},{1,3},{3,1},{4,6},{6,4},{5,7},{7,5},{8,10},{10,8},{9,1... | collective-permute-start | bytes 786440 | tf_op jit(solution)/shard_map/ppermute | solution.py:78
  55.7 25.0 %collective-permute-start.15 = (f32[256,128]{0,1:T(8,128)S(1)}, f32[256,128]{0,1:T(8,128)S(1)}, u32[]{:S(2)}, u32[]{:S(2)}) collective-permute-start(f32[256,128]{0,1:T(8,128)S(1)} %bitcast.186), channel_id=1, source_target_pairs={{0,8},{1,9},{2,10},{3,11},{16,24},{17,25},{18,26},{19,27}} | collective-permute-start | bytes 393224 | tf_op jit(solution)/shard_map/ppermute | solution.py:97
  57.3 32.1 %collective-permute-start.17 = (f32[256,128]{0,1:T(8,128)S(1)}, f32[256,128]{0,1:T(8,128)S(1)}, u32[]{:S(2)}, u32[]{:S(2)}) collective-permute-start(f32[256,128]{0,1:T(8,128)S(1)} %bitcast.187), channel_id=1, source_target_pairs={{0,12},{1,13},{2,14},{3,15},{16,28},{17,29},{18,30},{19,31}} | collective-permute-start | bytes 393224 | tf_op jit(solution)/shard_map/ppermute | solution.py:97
  60.5 19.0 %collective-permute-start.16 = (f32[256,128]{0,1:T(8,128)S(1)}, f32[256,128]{0,1:T(8,128)S(1)}, u32[]{:S(2)}, u32[]{:S(2)}) collective-permute-start(f32[256,128]{0,1:T(8,128)S(1)} %bitcast.182), channel_id=1, source_target_pairs={{4,8},{5,9},{6,10},{7,11},{20,24},{21,25},{22,26},{23,27}} | collective-permute-start | bytes 393224 | tf_op jit(solution)/shard_map/ppermute | solution.py:97
  61.8 24.7 %collective-permute-start.18 = (f32[256,128]{0,1:T(8,128)S(1)}, f32[256,128]{0,1:T(8,128)S(1)}, u32[]{:S(2)}, u32[]{:S(2)}) collective-permute-start(f32[256,128]{0,1:T(8,128)S(1)} %bitcast.183), channel_id=1, source_target_pairs={{4,12},{5,13},{6,14},{7,15},{20,28},{21,29},{22,30},{23,31}} | collective-permute-start | bytes 393224 | tf_op jit(solution)/shard_map/ppermute | solution.py:97
  62.5 26.3 %collective-permute-start.20 = (f32[256,128]{0,1:T(8,128)S(1)}, f32[256,128]{0,1:T(8,128)S(1)}, u32[]{:S(2)}, u32[]{:S(2)}) collective-permute-start(f32[256,128]{0,1:T(8,128)S(1)} %bitcast.184), channel_id=1, source_target_pairs={{4,0},{5,1},{6,2},{7,3},{20,16},{21,17},{22,18},{23,19}} | collective-permute-start | bytes 393224 | tf_op jit(solution)/shard_map/ppermute | solution.py:97
  84.5 9.1 %collective-permute-start.21 = (f32[256,128]{0,1:T(8,128)S(1)}, f32[256,128]{0,1:T(8,128)S(1)}, u32[]{:S(2)}, u32[]{:S(2)}) collective-permute-start(f32[256,128]{0,1:T(8,128)S(1)} %bitcast.180), channel_id=1, source_target_pairs={{8,0},{9,1},{10,2},{11,3},{24,16},{25,17},{26,18},{27,19}} | collective-permute-start | bytes 393224 | tf_op jit(solution)/shard_map/ppermute | solution.py:97
  86.5 7.4 %collective-permute-start.23 = (f32[256,128]{0,1:T(8,128)S(1)}, f32[256,128]{0,1:T(8,128)S(1)}, u32[]{:S(2)}, u32[]{:S(2)}) collective-permute-start(f32[256,128]{0,1:T(8,128)S(1)} %bitcast.181), channel_id=1, source_target_pairs={{8,4},{9,5},{10,6},{11,7},{24,20},{25,21},{26,22},{27,23}} | collective-permute-start | bytes 393224 | tf_op jit(solution)/shard_map/ppermute | solution.py:97
  90.7 7.2 %collective-permute-start.24 = (f32[256,128]{0,1:T(8,128)S(1)}, f32[256,128]{0,1:T(8,128)S(1)}, u32[]{:S(2)}, u32[]{:S(2)}) collective-permute-start(f32[256,128]{0,1:T(8,128)S(1)} %bitcast.189), channel_id=1, source_target_pairs={{12,4},{13,5},{14,6},{15,7},{28,20},{29,21},{30,22},{31,23}} | collective-permute-start | bytes 393224 | tf_op jit(solution)/shard_map/ppermute | solution.py:97
  91.7 20.1 %collective-permute-start.26 = (f32[256,128]{0,1:T(8,128)S(1)}, f32[256,128]{0,1:T(8,128)S(1)}, u32[]{:S(2)}, u32[]{:S(2)}) collective-permute-start(f32[256,128]{0,1:T(8,128)S(1)} %bitcast.190), channel_id=1, source_target_pairs={{12,8},{13,9},{14,10},{15,11},{28,24},{29,25},{30,26},{31,27}} | collective-permute-start | bytes 393224 | tf_op jit(solution)/shard_map/ppermute | solution.py:97
  95.9 12.0 %collective-permute-start.29 = (f32[256,128]{0,1:T(8,128)S(1)}, f32[256,128]{0,1:T(8,128)S(1)}, u32[]{:S(2)}, u32[]{:S(2)}) collective-permute-start(f32[256,128]{0,1:T(8,128)S(1)} %convolution_bitcast_fusion.22), channel_id=1, source_target_pairs={{0,12},{1,13},{2,14},{3,15},{16,28},{17,29},{18,30},{19,31}} | collective-permute-start | bytes 393224 | tf_op jit(solution)/shard_map/ppermute | solution.py:97
  96.5 10.7 %collective-permute-start.27 = (f32[256,128]{0,1:T(8,128)S(1)}, f32[256,128]{0,1:T(8,128)S(1)}, u32[]{:S(2)}, u32[]{:S(2)}) collective-permute-start(f32[256,128]{0,1:T(8,128)S(1)} %convolution_bitcast_fusion.22), channel_id=1, source_target_pairs={{0,8},{1,9},{2,10},{3,11},{16,24},{17,25},{18,26},{19,27}} | collective-permute-start | bytes 393224 | tf_op jit(solution)/shard_map/ppermute | solution.py:97
  99.1 8.4 %collective-permute-start.30 = (f32[256,128]{0,1:T(8,128)S(1)}, f32[256,128]{0,1:T(8,128)S(1)}, u32[]{:S(2)}, u32[]{:S(2)}) collective-permute-start(f32[256,128]{0,1:T(8,128)S(1)} %convolution_bitcast_fusion.16), channel_id=1, source_target_pairs={{4,12},{5,13},{6,14},{7,15},{20,28},{21,29},{22,30},{23,31}} | collective-permute-start | bytes 393224 | tf_op jit(solution)/shard_map/ppermute | solution.py:97
  99.8 11.6 %collective-permute-start.28 = (f32[256,128]{0,1:T(8,128)S(1)}, f32[256,128]{0,1:T(8,128)S(1)}, u32[]{:S(2)}, u32[]{:S(2)}) collective-permute-start(f32[256,128]{0,1:T(8,128)S(1)} %convolution_bitcast_fusion.16), channel_id=1, source_target_pairs={{4,8},{5,9},{6,10},{7,11},{20,24},{21,25},{22,26},{23,27}} | collective-permute-start | bytes 393224 | tf_op jit(solution)/shard_map/ppermute | solution.py:97
  (9 other events, 85.2 us)

commit v2 on v1

v2 whole, which is shorter than its diff:
```python
import jax
import jax.numpy as jnp
from jax import lax
from jax.experimental import pallas as pl
from jax.experimental.pallas import tpu as pltpu
from jax.sharding import PartitionSpec as P

NRHS = 512
STEPS = 6
HIGH = lax.Precision.HIGH


def mul(a, b):
    return jnp.dot(a, b, precision=HIGH, preferred_element_type=jnp.float32)


def general(right_side, prev_factor, prev_solution, window_factor):
    row_count = lax.axis_size("row")
    row_index = lax.axis_index("row")
    col_count = lax.axis_size("col")
    col_index = lax.axis_index("col")
    blocks = window_factor.shape[1] // STEPS
    slots = right_side.shape[0] // blocks
    width = NRHS // col_count
    partial_value = mul(prev_factor, lax.all_gather(prev_solution, "row", axis=1, tiled=True))
    prior = lax.psum_scatter(partial_value, "col", scatter_dimension=1, tiled=True)
    mine = lax.dynamic_slice_in_dim(right_side, col_index * width, width, 1)
    resid = (mine - prior).reshape(slots, blocks, width)
    tiles = window_factor.reshape(slots, blocks, STEPS, blocks)
    order = jnp.arange(slots, dtype=jnp.int32) * row_count + row_index
    for step in range(STEPS):
        root = step % row_count
        solved = mul(tiles[step // row_count, :, step, :], resid[step // row_count])
        solved = lax.psum(jnp.where(row_index == root, solved, jnp.zeros_like(solved)), "row")
        update = jnp.einsum("sij,jn->sin", tiles[:, :, step, :], solved, precision=HIGH)
        resid = jnp.where((order > step)[:, None, None], resid - update, resid)
        resid = jnp.where((order == step)[:, None, None], solved[None], resid)
    return resid.reshape(slots * blocks, width)


def gather_row(piece, chunks):
    rows = piece.shape[0] // chunks
    up = down = [piece[i * rows : (i + 1) * rows] for i in range(chunks)]
    ups, downs = [], []
    for hop in range(3):
        up = [lax.ppermute(c, "row", [(i, i + 1) for i in range(hop, 3)]) for c in up]
        down = [lax.ppermute(c, "row", [(i + 1, i) for i in range(0, 3 - hop)]) for c in down]
        ups.append(up)
        downs.append(down)
    return ups, downs


def pick(pred, ones, others):
    return [jnp.where(pred, a, b) for a, b in zip(ones, others)]


def prior_block(prev_factor, prev_solution):
    row_index = lax.axis_index("row")
    col_index = lax.axis_index("col")
    core, side = col_index % 2, col_index // 2
    ups, downs = gather_row(prev_solution, 2)
    half = prev_solution.shape[0] // 2
    whole = [prev_solution[:half], prev_solution[half:]]
    second = pick(row_index >= 2, ups[1], downs[1])
    front = pick(row_index >= 1, ups[0], downs[2])
    back = pick(row_index >= 3, ups[2], downs[0])
    factor, whole[0], whole[1], second[0], second[1] = lax.optimization_barrier(
        (prev_factor, whole[0], whole[1], second[0], second[1])
    )
    mine_first = row_index // 2 == side
    mine_late = ((row_index + 3) % 4) // 2 == side

    def products(flag, one, two):
        close = jnp.concatenate(pick(flag, one, two), 0)
        far = jnp.concatenate(pick(flag, two, one), 0)
        return mul(factor, close), mul(factor, far)

    early = products(mine_first, whole, second)
    late = products(mine_late, front, back)
    keeps_early = core == row_index % 2
    away = jnp.stack([jnp.where(keeps_early, b, a) for a, b in zip(early, late)])
    keep = jnp.stack([jnp.where(keeps_early, a, b) for a, b in zip(early, late)])
    keep = keep + lax.ppermute(away, "col", [(0, 1), (1, 0), (2, 3), (3, 2)])
    return keep[0], lax.ppermute(keep[1], "col", [(0, 2), (2, 0), (1, 3), (3, 1)]), second[0]


BLOCK = 256
HALF = BLOCK // 2
WIDTH = 128
VMEM_SPEC = pl.BlockSpec(memory_space=pltpu.VMEM)
ANY_SPEC = pl.BlockSpec(memory_space=pl.ANY)


def near(x):
    return pltpu.with_memory_space_constraint(x, pltpu.VMEM)


def after(x, *earlier):
    return lax.optimization_barrier((x, *earlier))[0]


def split(x):
    high = x.astype(jnp.bfloat16)
    return high, (x - high.astype(jnp.float32)).astype(jnp.bfloat16)


def wide(x):
    return jnp.concatenate(split(x), 1)


def product(tile, pair):
    high, low = split(tile)
    both = jnp.dot(high, pair, preferred_element_type=jnp.float32)
    both = both + jnp.dot(low, pair, preferred_element_type=jnp.float32)
    return both[:, :WIDTH] + both[:, WIDTH:]


def columns(k):
    return slice(k * BLOCK, (k + 1) * BLOCK)


LOW, TOP = slice(0, BLOCK), slice(BLOCK, 2 * BLOCK)


def call(kernel, shapes, scratch=(), specs=None):
    def run(*args):
        spaces = specs or [VMEM_SPEC] * len(args)
        args = [a if s is ANY_SPEC else near(a) for a, s in zip(args, spaces)]
        return pl.pallas_call(
            kernel,
            out_shape=[pltpu.VMEM(s, jnp.float32) for s in shapes],
            in_specs=spaces,
            out_specs=[VMEM_SPEC] * len(shapes),
            scratch_shapes=list(scratch),
            compiler_params=pltpu.CompilerParams(vmem_limit_bytes=32 * 1024 * 1024),
        )(*args)

    return run


def load_kernel(factor, side, factor_out, side_out, *rest):
    sent, sem = rest[:-1], rest[-1]
    col_index = lax.axis_index("col")
    low = pl.ds(pl.multiple_of((col_index % 2) * HALF, HALF), HALF)
    top = pl.ds(pl.multiple_of(BLOCK + (col_index % 2) * HALF, HALF), HALF)
    mine = pl.ds(pl.multiple_of(col_index * WIDTH, WIDTH), WIDTH)
    sources = [
        factor,
        side.at[:, mine],
        factor.at[low, pl.ds(0, 4 * BLOCK)],
        factor.at[top, pl.ds(BLOCK, 4 * BLOCK)],
        factor.at[top, pl.ds(2 * BLOCK, 4 * BLOCK)],
        factor.at[top, pl.ds(0, 6 * BLOCK)],
    ]
    copies = [
        pltpu.make_async_copy(s, d, sem.at[i])
        for i, (s, d) in enumerate(zip(sources, (factor_out, side_out, *sent)))
    ]
    for copy in copies:
        copy.start()
    for copy in copies:
        copy.wait()


def first_kernel(side, one, two, factor, low, top):
    low[...] = side[LOW, :] - (one[LOW, :] + two[LOW, :])
    top[...] = side[TOP, :] - (one[TOP, :] + two[TOP, :])

    @pl.when(lax.axis_index("row") == 0)
    def _():
        low[...] = product(factor[LOW, columns(0)], wide(low[...]))
        top[...] = top[...] - product(factor[TOP, columns(0)], wide(low[...]))


def second_kernel(solved, low_in, top_in, factor, low, top):
    @pl.when(lax.axis_index("row") == 1)
    def _():
        pair = wide(solved[...])
        value = low_in[...] - product(factor[LOW, columns(0)], pair)
        low[...] = product(factor[LOW, columns(1)], wide(value))
        value = top_in[...] - product(factor[TOP, columns(0)], pair)
        top[...] = value - product(factor[TOP, columns(1)], wide(low[...]))


def halves():
    core = lax.axis_index("col") % 2
    own = pl.ds(pl.multiple_of(core * HALF, HALF), HALF)
    other = pl.ds(pl.multiple_of((1 - core) * HALF, HALF), HALF)
    return own, other


def third_kernel(solved, low, top, low3, top3, factor, own3, other3, own7, other7, state):
    @pl.when(lax.axis_index("row") == 2)
    def _():
        own, other = halves()
        pair = wide(solved[...])
        state[0] = low[...] - product(factor[LOW, columns(0)], pair)
        state[2] = top[...] - product(factor[TOP, columns(0)], pair)
        state[1] = low3[...]
        state[3] = top3[...]
        for at, mine, theirs in ((1, own3, other3), (3, own7, other7)):
            state[at, own, :] = state[at, own, :] - product(mine[:, columns(0)], pair)
            state[at, other, :] = state[at, other, :] - product(theirs[:, columns(0)], pair)


def fourth_kernel(
    state, solved, value4, value5, factor, own3, other3, own4, other4, own5, other5, own7, other7,
    kept, block4, block5, sent, value,
):
    @pl.when(lax.axis_index("row") == 2)
    def _():
        own, other = halves()
        spots = {3: value.at[0], 4: value.at[1], 5: value.at[2], 7: value.at[3], 6: value.at[4]}
        tiles = {
            3: (own3, other3, 0),
            4: (own4, other4, 1),
            5: (own5, other5, 2),
            7: (own7, other7, 0),
        }

        def update(block, k, pair):
            ref = spots[block]
            if block == 6:
                ref[...] = ref[...] - product(factor[TOP, columns(k)], pair)
                return
            mine, theirs, skip = tiles[block]
            ref[own, :] = ref[own, :] - product(mine[:, columns(k - skip)], pair)
            ref[other, :] = ref[other, :] - product(theirs[:, columns(k - skip)], pair)

        pair = wide(solved[...])
        start = state[0] - product(factor[LOW, columns(1)], pair)
        kept[LOW, :] = product(factor[LOW, columns(2)], wide(start))
        value[0] = state[1]
        value[1] = value4[...]
        value[2] = value5[...]
        value[3] = state[3]
        value[4] = state[2]
        for block in (3, 4, 6, 7):
            update(block, 1, pair)
        outs = {2: kept.at[LOW, :], 3: sent.at[LOW, :], 4: block4, 5: block5}
        for k in range(2, 6):
            if k > 2:
                pair = wide(spots[k][...])
                mine, theirs, skip = tiles[k]
                outs[k][own, :] = product(mine[:, columns(k - skip)], pair)
                outs[k][other, :] = product(theirs[:, columns(k - skip)], pair)
            pair = wide(outs[k][...])
            for block in (3, 4, 5, 6, 7):
                if block > k:
                    update(block, k, pair)
        kept[TOP, :] = spots[6][...]
        sent[TOP, :] = spots[7][...]


def line4(right_side, prev_factor, prev_solution, window_factor):
    row_index = lax.axis_index("row")
    one, two, early = prior_block(prev_factor, prev_solution)

    def move(x, *pairs):
        return lax.ppermute(x, "row", list(pairs))

    def swap(x):
        return lax.ppermute(x, "col", [(0, 1), (1, 0), (2, 3), (3, 2)])

    half, size, six = (HALF, 4 * BLOCK), (BLOCK, WIDTH), (HALF, 6 * BLOCK)
    factor, side, send3, send4, send5, send7 = call(
        load_kernel,
        [window_factor.shape, (2 * BLOCK, WIDTH), half, half, half, six],
        [pltpu.SemaphoreType.DMA((6,))],
        [ANY_SPEC, ANY_SPEC],
    )(after(window_factor, early), right_side)
    own3 = move(send3, (3, 2))
    own5 = move(send5, (1, 2))
    own4 = move(send4, (0, 2))
    own7 = move(send7, (3, 2))

    low, top = call(first_kernel, [size, size])(side, one, two, factor)
    first = move(low, (0, 1), (3, 2))
    second = move(low, (0, 2))
    value4 = move(top, (0, 2))
    top3 = move(top, (3, 2))
    other3, other4, other5, other7 = [swap(after(x, low)) for x in (own3, own4, own5, own7)]
    low1, top1 = call(second_kernel, [size, size])(first, low, top, factor)
    third = move(low1, (1, 2))
    value5 = move(top1, (1, 2))
    (state,) = call(third_kernel, [(4, *size)])(
        after(second, low1), low, top, first, top3, factor, own3, other3, own7, other7
    )
    kept, block4, block5, sent = call(
        fourth_kernel, [(2 * BLOCK, WIDTH), size, size, (2 * BLOCK, WIDTH)], [pltpu.VMEM((5, *size), jnp.float32)]
    )(state, third, value4, value5, factor, own3, other3, own4, other4, own5, other5, own7, other7)
    last = move(sent, (2, 3))
    block5 = move(block5, (2, 1))
    block4 = move(block4, (2, 0))
    lows = lax.select_n(row_index, low, low1, kept[:BLOCK], last[:BLOCK])
    tops = lax.select_n(row_index, block4, block5, kept[BLOCK:], last[BLOCK:])
    return jnp.concatenate([lows, tops], 0)


def body(right_side, prev_factor, prev_solution, window_factor):
    blocks = window_factor.shape[1] // STEPS
    slots = right_side.shape[0] // blocks
    if lax.axis_size("row") == 4 and lax.axis_size("col") == 4 and slots == 2:
        return line4(right_side, prev_factor, prev_solution, window_factor)
    return general(right_side, prev_factor, prev_solution, window_factor)


def solution(mesh):
    in_specs = (
        P(("groups", "row"), None),
        P(("groups", "row"), "col"),
        P(("groups", "col"), "row"),
        P(("groups", "row"), None),
    )
    out_specs = P(("groups", "row"), "col")
    return jax.shard_map(body, mesh=mesh, in_specs=in_specs, out_specs=out_specs, check_vma=False)
```

time: 114 us -> 129 us (1.13)
  the two profiles are of different devices: /device:TPU:16 before, /device:TPU:0 now
where the time goes in v2:
time: 129 us; the launch traced here: 128 us
  starting transfers between devices  67.9 us (53%)
  waiting for transfers between devices  48.2 us (37%)
  other arithmetic  3.97 us (3%)
  matrix products  3.95 us (3%)
  local copies, waits for them, and re-layouts  2.29 us (2%)
    ppermute x13, starting transfers between devices, move(): return lax.ppermute(x, 'row', list(pairs))  44.3 us
    ppermute x13, waiting for transfers between devices, move(): return lax.ppermute(x, 'row', list(pairs))  25.2 us
    ppermute x6, waiting for transfers between devices, gather_row(): lax.ppermute(c, 'row', [(i + 1, i) for i in range(0, 3 - hop)])  21.2 us
    ppermute x6, starting transfers between devices, gather_row(): lax.ppermute(c, 'row', [(i, i + 1) for i in range(hop, 3)])  13.6 us
    ppermute x6, starting transfers between devices, gather_row(): lax.ppermute(c, 'row', [(i + 1, i) for i in range(0, 3 - hop)])  7.73 us
    dot_general x4, matrix products, mul(): return jnp.dot(a, b, precision=HIGH, preferred_element_type=jnp.float32)  3.95 us
    select_n x5, other arithmetic, pick(): return [jnp.where(pred, a, b) for a, b in zip(ones, others)]  3.11 us
  transfers between devices with their start and end apart: 31, of which 12 were waited for; matrix products, arithmetic and copies ran while one was open for 2% of the time, Pallas kernels for 1%

profile of v2, /device:TPU:0, one launch (start us, length us, event | category | flops | bytes accessed | tf_op | source)
XLA Modules:
  0.0 128.0 jit_solution(8701195566455562982)
XLA Ops:
  1.2 4.9 %collective-permute-start.4 = (f32[512,128]{1,0:T(8,128)S(1)}, f32[512,128]{1,0:T(8,128)S(1)}, u32[]{:S(2)}, u32[]{:S(2)}) collective-permute-start(f32[512,128]{1,0:T(8,128)S(1)} %get-tuple-element.35), channel_id=1, source_target_pairs={{0,4},{4,8},{8,12},{1,5},{5,9},{9,13},{2,6},{6,10},{10,14},{3,7},{... | collective-permute-start | bytes 786440 | tf_op jit(solution)/shard_map/ppermute | solution.py:46
  6.2 1.3 %collective-permute-start.6 = (f32[512,128]{1,0:T(8,128)S(1)}, f32[512,128]{1,0:T(8,128)S(1)}, u32[]{:S(2)}, u32[]{:S(2)}) collective-permute-start(f32[512,128]{1,0:T(8,128)S(1)} %get-tuple-element.35), channel_id=1, source_target_pairs={{4,0},{8,4},{12,8},{5,1},{9,5},{13,9},{6,2},{10,6},{14,10},{7,3},{... | collective-permute-start | bytes 786440 | tf_op jit(solution)/shard_map/ppermute | solution.py:47
  7.5 4.6 %collective-permute-start = (f32[512,128]{1,0:T(8,128)S(1)}, f32[512,128]{1,0:T(8,128)S(1)}, u32[]{:S(2)}, u32[]{:S(2)}) collective-permute-start(f32[512,128]{1,0:T(8,128)S(1)} %get-tuple-element.34), channel_id=1, source_target_pairs={{0,4},{4,8},{8,12},{1,5},{5,9},{9,13},{2,6},{6,10},{10,14},{3,7},{... | collective-permute-start | bytes 786440 | tf_op jit(solution)/shard_map/ppermute | solution.py:46
  12.0 1.3 %collective-permute-start.2 = (f32[512,128]{1,0:T(8,128)S(1)}, f32[512,128]{1,0:T(8,128)}, u32[]{:S(2)}, u32[]{:S(2)}) collective-permute-start(f32[512,128]{1,0:T(8,128)S(1)} %get-tuple-element.34), channel_id=1, source_target_pairs={{4,0},{8,4},{12,8},{5,1},{9,5},{13,9},{6,2},{10,6},{14,10},{7,3},{... | collective-permute-start | bytes 786440 | tf_op jit(solution)/shard_map/ppermute | solution.py:47
  13.4 1.4 %collective-permute-start.5 = (f32[512,128]{1,0:T(8,128)S(1)}, f32[512,128]{1,0:T(8,128)}, u32[]{:S(2)}, u32[]{:S(2)}) collective-permute-start(f32[512,128]{1,0:T(8,128)S(1)} %collective-permute-done.4), channel_id=1, source_target_pairs={{4,8},{8,12},{5,9},{9,13},{6,10},{10,14},{7,11},{11,15},{20,24},{2... | collective-permute-start | bytes 786440 | tf_op jit(solution)/shard_map/ppermute | solution.py:46
  14.7 1.3 %collective-permute-done.6 = f32[512,128]{1,0:T(8,128)S(1)} collective-permute-done((f32[512,128]{1,0:T(8,128)S(1)}, f32[512,128]{1,0:T(8,128)S(1)}, u32[]{:S(2)}, u32[]{:S(2)}) %collective-permute-start.6) | collective-permute-done | bytes 262176 | tf_op jit(solution)/shard_map/ppermute | solution.py:47
  17.4 1.4 %collective-permute-start.1 = (f32[512,128]{1,0:T(8,128)S(1)}, f32[512,128]{1,0:T(8,128)}, u32[]{:S(2)}, u32[]{:S(2)}) collective-permute-start(f32[512,128]{1,0:T(8,128)S(1)} %collective-permute-done), channel_id=1, source_target_pairs={{4,8},{8,12},{5,9},{9,13},{6,10},{10,14},{7,11},{11,15},{20,24},{2... | collective-permute-start | bytes 786440 | tf_op jit(solution)/shard_map/ppermute | solution.py:46
  18.7 2.9 %collective-permute-done.2 = f32[512,128]{1,0:T(8,128)} collective-permute-done((f32[512,128]{1,0:T(8,128)S(1)}, f32[512,128]{1,0:T(8,128)}, u32[]{:S(2)}, u32[]{:S(2)}) %collective-permute-start.2) | collective-permute-done | bytes 262176 | tf_op jit(solution)/shard_map/ppermute | solution.py:47
  23.0 4.2 %collective-permute-done.7 = f32[512,128]{1,0:T(8,128)} collective-permute-done((f32[512,128]{1,0:T(8,128)S(1)}, f32[512,128]{1,0:T(8,128)}, u32[]{:S(2)}, u32[]{:S(2)}) %collective-permute-start.7) | collective-permute-done | bytes 262176 | tf_op jit(solution)/shard_map/ppermute | solution.py:47
  28.2 5.8 %collective-permute-done.3 = f32[512,128]{1,0:T(8,128)} collective-permute-done((f32[512,128]{1,0:T(8,128)}, f32[512,128]{1,0:T(8,128)}, u32[]{:S(2)}, u32[]{:S(2)}) %collective-permute-start.3) | collective-permute-done | bytes 262176 | tf_op jit(solution)/shard_map/ppermute | solution.py:47
  36.0 1.3 %collective-permute-start.8 = (f32[512,128]{1,0:T(8,128)}, f32[512,128]{1,0:T(8,128)S(1)}, u32[]{:S(2)}, u32[]{:S(2)}) collective-permute-start(f32[512,128]{1,0:T(8,128)} %collective-permute-done.3), channel_id=1, source_target_pairs={{4,0},{5,1},{6,2},{7,3},{20,16},{21,17},{22,18},{23,19}} | collective-permute-start | bytes 786440 | tf_op jit(solution)/shard_map/ppermute | solution.py:47
  41.0 5.2 %collective-permute-done.8 = f32[512,128]{1,0:T(8,128)S(1)} collective-permute-done((f32[512,128]{1,0:T(8,128)}, f32[512,128]{1,0:T(8,128)S(1)}, u32[]{:S(2)}, u32[]{:S(2)}) %collective-permute-start.8) | collective-permute-done | bytes 262176 | tf_op jit(solution)/shard_map/ppermute | solution.py:47
  47.2 1.8 %collective-permute-done.10 = f32[512,128]{1,0:T(8,128)S(1)} collective-permute-done((f32[512,128]{1,0:T(8,128)}, f32[512,128]{1,0:T(8,128)S(1)}, u32[]{:S(2)}, u32[]{:S(2)}) %collective-permute-start.10) | collective-permute-done | bytes 262176 | tf_op jit(solution)/shard_map/ppermute | solution.py:47
  53.5 1.5 %collective-permute-start.13 = (f32[512,128]{1,0:T(8,128)S(1)}, f32[512,128]{1,0:T(8,128)S(1)}, u32[]{:S(2)}, u32[]{:S(2)}) collective-permute-start(f32[512,128]{1,0:T(8,128)S(1)} %get-tuple-element.61), channel_id=1, source_target_pairs={{0,2},{2,0},{1,3},{3,1},{4,6},{6,4},{5,7},{7,5},{8,10},{10,8},{9,1... | collective-permute-start | bytes 786440 | tf_op jit(solution)/shard_map/ppermute | solution.py:84
  56.5 3.3 %collective-permute-start.24 = (f32[128,1024]{1,0:T(8,128)S(1)}, f32[128,1024]{1,0:T(8,128)S(1)}, u32[]{:S(2)}, u32[]{:S(2)}) collective-permute-start(f32[128,1024]{1,0:T(8,128)S(1)} %get-tuple-element.47), channel_id=1, source_target_pairs={{0,8},{1,9},{2,10},{3,11},{16,24},{17,25},{18,26},{19,27}} | collective-permute-start | bytes 1572872 | tf_op jit(solution)/shard_map/ppermute | solution.py:260
  59.8 1.9 %collective-permute-done.13.two = f32[512,128]{1,0:T(8,128)S(1)} collective-permute-done((f32[512,128]{1,0:T(8,128)S(1)}, f32[512,128]{1,0:T(8,128)S(1)}, u32[]{:S(2)}, u32[]{:S(2)}) %collective-permute-start.13) | collective-permute-done | bytes 262176 | tf_op jit(solution)/shard_map/ppermute | solution.py:84
  64.2 7.5 %collective-permute-done.24.own4 = f32[128,1024]{1,0:T(8,128)S(1)} collective-permute-done((f32[128,1024]{1,0:T(8,128)S(1)}, f32[128,1024]{1,0:T(8,128)S(1)}, u32[]{:S(2)}, u32[]{:S(2)}) %collective-permute-start.24) | collective-permute-done | bytes 524320 | tf_op jit(solution)/shard_map/ppermute | solution.py:260
  71.7 1.4 %collective-permute-done.14.solved.low3 = f32[256,128]{1,0:T(8,128)S(1)} collective-permute-done((f32[256,128]{1,0:T(8,128)S(1)}, f32[256,128]{1,0:T(8,128)S(1)}, u32[]{:S(2)}, u32[]{:S(2)}) %collective-permute-start.14) | collective-permute-done | bytes 131104 | tf_op jit(solution)/shard_map/ppermute | solution.py:260
  73.1 20.9 %collective-permute-start.15 = (f32[256,128]{1,0:T(8,128)S(1)}, f32[256,128]{1,0:T(8,128)S(1)}, u32[]{:S(2)}, u32[]{:S(2)}) collective-permute-start(f32[256,128]{1,0:T(8,128)S(1)} %get-tuple-element.38.low_in.low), channel_id=1, source_target_pairs={{0,8},{1,9},{2,10},{3,11},{16,24},{17,25},{18,26},{19,27}} | collective-permute-start | bytes 393224 | tf_op jit(solution)/shard_map/ppermute | solution.py:260
  94.0 2.6 %collective-permute-done.15.solved = f32[256,128]{1,0:T(8,128)S(1)} collective-permute-done((f32[256,128]{1,0:T(8,128)S(1)}, f32[256,128]{1,0:T(8,128)S(1)}, u32[]{:S(2)}, u32[]{:S(2)}) %collective-permute-start.15) | collective-permute-done | bytes 131104 | tf_op jit(solution)/shard_map/ppermute | solution.py:260
  97.3 11.4 %collective-permute-start.22 = (f32[256,128]{1,0:T(8,128)S(1)}, f32[256,128]{1,0:T(8,128)S(1)}, u32[]{:S(2)}, u32[]{:S(2)}) collective-permute-start(f32[256,128]{1,0:T(8,128)S(1)} %get-tuple-element.39.top_in.top), channel_id=1, source_target_pairs={{0,8},{1,9},{2,10},{3,11},{16,24},{17,25},{18,26},{19,27}} | collective-permute-start | bytes 393224 | tf_op jit(solution)/shard_map/ppermute | solution.py:260
  112.0 1.3 %collective-permute-start.29 = (f32[256,128]{1,0:T(8,128)S(1)}, f32[256,128]{1,0:T(8,128)S(1)}, u32[]{:S(2)}, u32[]{:S(2)}) collective-permute-start(f32[256,128]{1,0:T(8,128)S(1)} %get-tuple-element.53), channel_id=1, source_target_pairs={{8,0},{9,1},{10,2},{11,3},{24,16},{25,17},{26,18},{27,19}} | collective-permute-start | bytes 393224 | tf_op jit(solution)/shard_map/ppermute | solution.py:260
  113.3 1.3 %collective-permute-start.30 = (f32[256,128]{1,0:T(8,128)S(1)}, f32[256,128]{1,0:T(8,128)}, u32[]{:S(2)}, u32[]{:S(2)}) collective-permute-start(f32[256,128]{1,0:T(8,128)S(1)} %get-tuple-element.54), channel_id=1, source_target_pairs={{8,4},{9,5},{10,6},{11,7},{24,20},{25,21},{26,22},{27,23}} | collective-permute-start | bytes 393224 | tf_op jit(solution)/shard_map/ppermute | solution.py:260
  114.6 12.6 %collective-permute-done.29 = f32[256,128]{1,0:T(8,128)S(1)} collective-permute-done((f32[256,128]{1,0:T(8,128)S(1)}, f32[256,128]{1,0:T(8,128)S(1)}, u32[]{:S(2)}, u32[]{:S(2)}) %collective-permute-start.29) | collective-permute-done | bytes 131104 | tf_op jit(solution)/shard_map/ppermute | solution.py:260
  (64 shorter events, 24.5 us)
Async XLA Ops:
  1.2 12.1 %collective-permute-start.4 = (f32[512,128]{1,0:T(8,128)S(1)}, f32[512,128]{1,0:T(8,128)S(1)}, u32[]{:S(2)}, u32[]{:S(2)}) collective-permute-start(f32[512,128]{1,0:T(8,128)S(1)} %get-tuple-element.35), channel_id=1, source_target_pairs={{0,4},{4,8},{8,12},{1,5},{5,9},{9,13},{2,6},{6,10},{10,14},{3,7},{... | collective-permute-start | bytes 786440 | tf_op jit(solution)/shard_map/ppermute | solution.py:46
  6.2 9.9 %collective-permute-start.6 = (f32[512,128]{1,0:T(8,128)S(1)}, f32[512,128]{1,0:T(8,128)S(1)}, u32[]{:S(2)}, u32[]{:S(2)}) collective-permute-start(f32[512,128]{1,0:T(8,128)S(1)} %get-tuple-element.35), channel_id=1, source_target_pairs={{4,0},{8,4},{12,8},{5,1},{9,5},{13,9},{6,2},{10,6},{14,10},{7,3},{... | collective-permute-start | bytes 786440 | tf_op jit(solution)/shard_map/ppermute | solution.py:47
  7.5 9.9 %collective-permute-start = (f32[512,128]{1,0:T(8,128)S(1)}, f32[512,128]{1,0:T(8,128)S(1)}, u32[]{:S(2)}, u32[]{:S(2)}) collective-permute-start(f32[512,128]{1,0:T(8,128)S(1)} %get-tuple-element.34), channel_id=1, source_target_pairs={{0,4},{4,8},{8,12},{1,5},{5,9},{9,13},{2,6},{6,10},{10,14},{3,7},{... | collective-permute-start | bytes 786440 | tf_op jit(solution)/shard_map/ppermute | solution.py:46
  12.0 9.5 %collective-permute-start.2 = (f32[512,128]{1,0:T(8,128)S(1)}, f32[512,128]{1,0:T(8,128)}, u32[]{:S(2)}, u32[]{:S(2)}) collective-permute-start(f32[512,128]{1,0:T(8,128)S(1)} %get-tuple-element.34), channel_id=1, source_target_pairs={{4,0},{8,4},{12,8},{5,1},{9,5},{13,9},{6,2},{10,6},{14,10},{7,3},{... | collective-permute-start | bytes 786440 | tf_op jit(solution)/shard_map/ppermute | solution.py:47
  13.4 9.6 %collective-permute-start.5 = (f32[512,128]{1,0:T(8,128)S(1)}, f32[512,128]{1,0:T(8,128)}, u32[]{:S(2)}, u32[]{:S(2)}) collective-permute-start(f32[512,128]{1,0:T(8,128)S(1)} %collective-permute-done.4), channel_id=1, source_target_pairs={{4,8},{8,12},{5,9},{9,13},{6,10},{10,14},{7,11},{11,15},{20,24},{2... | collective-permute-start | bytes 786440 | tf_op jit(solution)/shard_map/ppermute | solution.py:46
  16.1 11.1 %collective-permute-start.7 = (f32[512,128]{1,0:T(8,128)S(1)}, f32[512,128]{1,0:T(8,128)}, u32[]{:S(2)}, u32[]{:S(2)}) collective-permute-start(f32[512,128]{1,0:T(8,128)S(1)} %collective-permute-done.6), channel_id=1, source_target_pairs={{4,0},{8,4},{5,1},{9,5},{6,2},{10,6},{7,3},{11,7},{20,16},{24,20},... | collective-permute-start | bytes 786440 | tf_op jit(solution)/shard_map/ppermute | solution.py:47
  17.4 10.8 %collective-permute-start.1 = (f32[512,128]{1,0:T(8,128)S(1)}, f32[512,128]{1,0:T(8,128)}, u32[]{:S(2)}, u32[]{:S(2)}) collective-permute-start(f32[512,128]{1,0:T(8,128)S(1)} %collective-permute-done), channel_id=1, source_target_pairs={{4,8},{8,12},{5,9},{9,13},{6,10},{10,14},{7,11},{11,15},{20,24},{2... | collective-permute-start | bytes 786440 | tf_op jit(solution)/shard_map/ppermute | solution.py:46
  21.6 12.4 %collective-permute-start.3 = (f32[512,128]{1,0:T(8,128)}, f32[512,128]{1,0:T(8,128)}, u32[]{:S(2)}, u32[]{:S(2)}) collective-permute-start(f32[512,128]{1,0:T(8,128)} %collective-permute-done.2), channel_id=1, source_target_pairs={{4,0},{8,4},{5,1},{9,5},{6,2},{10,6},{7,3},{11,7},{20,16},{24,20},... | collective-permute-start | bytes 786440 | tf_op jit(solution)/shard_map/ppermute | solution.py:47
  36.0 10.1 %collective-permute-start.8 = (f32[512,128]{1,0:T(8,128)}, f32[512,128]{1,0:T(8,128)S(1)}, u32[]{:S(2)}, u32[]{:S(2)}) collective-permute-start(f32[512,128]{1,0:T(8,128)} %collective-permute-done.3), channel_id=1, source_target_pairs={{4,0},{5,1},{6,2},{7,3},{20,16},{21,17},{22,18},{23,19}} | collective-permute-start | bytes 786440 | tf_op jit(solution)/shard_map/ppermute | solution.py:47
  37.3 8.8 %collective-permute-start.9 = (f32[512,128]{1,0:T(8,128)}, f32[512,128]{1,0:T(8,128)S(1)}, u32[]{:S(2)}, u32[]{:S(2)}) collective-permute-start(f32[512,128]{1,0:T(8,128)} %collective-permute-done.1), channel_id=1, source_target_pairs={{8,12},{9,13},{10,14},{11,15},{24,28},{25,29},{26,30},{27,31}} | collective-permute-start | bytes 786440 | tf_op jit(solution)/shard_map/ppermute | solution.py:46
  38.0 11.0 %collective-permute-start.10 = (f32[512,128]{1,0:T(8,128)}, f32[512,128]{1,0:T(8,128)S(1)}, u32[]{:S(2)}, u32[]{:S(2)}) collective-permute-start(f32[512,128]{1,0:T(8,128)} %collective-permute-done.7), channel_id=1, source_target_pairs={{4,0},{5,1},{6,2},{7,3},{20,16},{21,17},{22,18},{23,19}} | collective-permute-start | bytes 786440 | tf_op jit(solution)/shard_map/ppermute | solution.py:47
  39.3 9.7 %collective-permute-start.11 = (f32[512,128]{1,0:T(8,128)}, f32[512,128]{1,0:T(8,128)S(1)}, u32[]{:S(2)}, u32[]{:S(2)}) collective-permute-start(f32[512,128]{1,0:T(8,128)} %collective-permute-done.5), channel_id=1, source_target_pairs={{8,12},{9,13},{10,14},{11,15},{24,28},{25,29},{26,30},{27,31}} | collective-permute-start | bytes 786440 | tf_op jit(solution)/shard_map/ppermute | solution.py:46
  52.7 9.5 %collective-permute-start.19 = (f32[128,1536]{1,0:T(8,128)S(1)}, f32[128,1536]{1,0:T(8,128)S(1)}, u32[]{:S(2)}, u32[]{:S(2)}) collective-permute-start(f32[128,1536]{1,0:T(8,128)S(1)} %get-tuple-element.44), channel_id=1, source_target_pairs={{12,8},{13,9},{14,10},{15,11},{28,24},{29,25},{30,26},{31,27}} | collective-permute-start | bytes 2359304 | tf_op jit(solution)/shard_map/ppermute | solution.py:260
  56.5 15.2 %collective-permute-start.24 = (f32[128,1024]{1,0:T(8,128)S(1)}, f32[128,1024]{1,0:T(8,128)S(1)}, u32[]{:S(2)}, u32[]{:S(2)}) collective-permute-start(f32[128,1024]{1,0:T(8,128)S(1)} %get-tuple-element.47), channel_id=1, source_target_pairs={{0,8},{1,9},{2,10},{3,11},{16,24},{17,25},{18,26},{19,27}} | collective-permute-start | bytes 1572872 | tf_op jit(solution)/shard_map/ppermute | solution.py:260
  62.2 47.3 %collective-permute-start.20 = (f32[128,1536]{1,0:T(8,128)S(1)}, f32[128,1536]{1,0:T(8,128)S(1)}, u32[]{:S(2)}, u32[]{:S(2)}) collective-permute-start(f32[128,1536]{1,0:T(8,128)S(1)} %collective-permute-done.19.own7), channel_id=1, source_target_pairs={{0,1},{1,0},{2,3},{3,2},{4,5},{5,4},{6,7},{7,6},{8,9},{9,8},{10,11... | collective-permute-start | bytes 2359304 | tf_op jit(solution)/shard_map/ppermute | solution.py:263
  62.3 46.5 %collective-permute-start.18 = (f32[128,1024]{1,0:T(8,128)S(1)}, f32[128,1024]{1,0:T(8,128)S(1)}, u32[]{:S(2)}, u32[]{:S(2)}) collective-permute-start(f32[128,1024]{1,0:T(8,128)S(1)} %collective-permute-done.17.own3), channel_id=1, source_target_pairs={{0,1},{1,0},{2,3},{3,2},{4,5},{5,4},{6,7},{7,6},{8,9},{9,8},{10,11... | collective-permute-start | bytes 1572872 | tf_op jit(solution)/shard_map/ppermute | solution.py:263
  62.8 10.3 %collective-permute-start.14 = (f32[256,128]{1,0:T(8,128)S(1)}, f32[256,128]{1,0:T(8,128)S(1)}, u32[]{:S(2)}, u32[]{:S(2)}) collective-permute-start(f32[256,128]{1,0:T(8,128)S(1)} %get-tuple-element.38.low_in.low), channel_id=1, source_target_pairs={{0,4},{12,8},{1,5},{13,9},{2,6},{14,10},{3,7},{15,11},{16,20},{28,... | collective-permute-start | bytes 393224 | tf_op jit(solution)/shard_map/ppermute | solution.py:260
  64.1 47.2 %collective-permute-start.27 = (f32[128,1024]{1,0:T(8,128)S(1)}, f32[128,1024]{1,0:T(8,128)S(1)}, u32[]{:S(2)}, u32[]{:S(2)}) collective-permute-start(f32[128,1024]{1,0:T(8,128)S(1)} %collective-permute-done.26.own5), channel_id=1, source_target_pairs={{0,1},{1,0},{2,3},{3,2},{4,5},{5,4},{6,7},{7,6},{8,9},{9,8},{10,11... | collective-permute-start | bytes 1572872 | tf_op jit(solution)/shard_map/ppermute | solution.py:263
  71.7 39.6 %collective-permute-start.25 = (f32[128,1024]{1,0:T(8,128)S(1)}, f32[128,1024]{1,0:T(8,128)S(1)}, u32[]{:S(2)}, u32[]{:S(2)}) collective-permute-start(f32[128,1024]{1,0:T(8,128)S(1)} %collective-permute-done.24.own4), channel_id=1, source_target_pairs={{0,1},{1,0},{2,3},{3,2},{4,5},{5,4},{6,7},{7,6},{8,9},{9,8},{10,11... | collective-permute-start | bytes 1572872 | tf_op jit(solution)/shard_map/ppermute | solution.py:263
  73.1 23.5 %collective-permute-start.15 = (f32[256,128]{1,0:T(8,128)S(1)}, f32[256,128]{1,0:T(8,128)S(1)}, u32[]{:S(2)}, u32[]{:S(2)}) collective-permute-start(f32[256,128]{1,0:T(8,128)S(1)} %get-tuple-element.38.low_in.low), channel_id=1, source_target_pairs={{0,8},{1,9},{2,10},{3,11},{16,24},{17,25},{18,26},{19,27}} | collective-permute-start | bytes 393224 | tf_op jit(solution)/shard_map/ppermute | solution.py:260
  97.3 13.9 %collective-permute-start.22 = (f32[256,128]{1,0:T(8,128)S(1)}, f32[256,128]{1,0:T(8,128)S(1)}, u32[]{:S(2)}, u32[]{:S(2)}) collective-permute-start(f32[256,128]{1,0:T(8,128)S(1)} %get-tuple-element.39.top_in.top), channel_id=1, source_target_pairs={{0,8},{1,9},{2,10},{3,11},{16,24},{17,25},{18,26},{19,27}} | collective-permute-start | bytes 393224 | tf_op jit(solution)/shard_map/ppermute | solution.py:260
  111.3 15.9 %collective-permute-start.28 = (f32[512,128]{1,0:T(8,128)S(1)}, f32[512,128]{1,0:T(8,128)S(1)}, u32[]{:S(2)}, u32[]{:S(2)}) collective-permute-start(f32[512,128]{1,0:T(8,128)S(1)} %get-tuple-element.52), channel_id=1, source_target_pairs={{8,12},{9,13},{10,14},{11,15},{24,28},{25,29},{26,30},{27,31}} | collective-permute-start | bytes 786440 | tf_op jit(solution)/shard_map/ppermute | solution.py:260
  112.0 15.2 %collective-permute-start.29 = (f32[256,128]{1,0:T(8,128)S(1)}, f32[256,128]{1,0:T(8,128)S(1)}, u32[]{:S(2)}, u32[]{:S(2)}) collective-permute-start(f32[256,128]{1,0:T(8,128)S(1)} %get-tuple-element.53), channel_id=1, source_target_pairs={{8,0},{9,1},{10,2},{11,3},{24,16},{25,17},{26,18},{27,19}} | collective-permute-start | bytes 393224 | tf_op jit(solution)/shard_map/ppermute | solution.py:260
  113.3 13.9 %collective-permute-start.30 = (f32[256,128]{1,0:T(8,128)S(1)}, f32[256,128]{1,0:T(8,128)}, u32[]{:S(2)}, u32[]{:S(2)}) collective-permute-start(f32[256,128]{1,0:T(8,128)S(1)} %get-tuple-element.54), channel_id=1, source_target_pairs={{8,4},{9,5},{10,6},{11,7},{24,20},{25,21},{26,22},{27,23}} | collective-permute-start | bytes 393224 | tf_op jit(solution)/shard_map/ppermute | solution.py:260
  (10 other events, 70.0 us)

commit v3 on v1

v3 whole, which is shorter than its diff:
```python
import jax
import jax.numpy as jnp
from jax import lax
from jax.experimental import pallas as pl
from jax.experimental.pallas import tpu as pltpu
from jax.sharding import PartitionSpec as P

NRHS = 512
STEPS = 6
HIGH = lax.Precision.HIGH


def mul(a, b):
    return jnp.dot(a, b, precision=HIGH, preferred_element_type=jnp.float32)


def general(right_side, prev_factor, prev_solution, window_factor):
    row_count = lax.axis_size("row")
    row_index = lax.axis_index("row")
    col_count = lax.axis_size("col")
    col_index = lax.axis_index("col")
    blocks = window_factor.shape[1] // STEPS
    slots = right_side.shape[0] // blocks
    width = NRHS // col_count
    partial_value = mul(prev_factor, lax.all_gather(prev_solution, "row", axis=1, tiled=True))
    prior = lax.psum_scatter(partial_value, "col", scatter_dimension=1, tiled=True)
    mine = lax.dynamic_slice_in_dim(right_side, col_index * width, width, 1)
    resid = (mine - prior).reshape(slots, blocks, width)
    tiles = window_factor.reshape(slots, blocks, STEPS, blocks)
    order = jnp.arange(slots, dtype=jnp.int32) * row_count + row_index
    for step in range(STEPS):
        root = step % row_count
        solved = mul(tiles[step // row_count, :, step, :], resid[step // row_count])
        solved = lax.psum(jnp.where(row_index == root, solved, jnp.zeros_like(solved)), "row")
        update = jnp.einsum("sij,jn->sin", tiles[:, :, step, :], solved, precision=HIGH)
        resid = jnp.where((order > step)[:, None, None], resid - update, resid)
        resid = jnp.where((order == step)[:, None, None], solved[None], resid)
    return resid.reshape(slots * blocks, width)


def gather_row(piece, chunks, inject, load):
    rows = piece.shape[0] // chunks
    up = down = [piece[i * rows : (i + 1) * rows] for i in range(chunks)]
    ups, downs = [], []
    for hop in range(3):
        if hop == 1:
            up, down = inject(up, down)
            ups[0], downs[0] = up, down
        if hop == 2:
            loaded = load(ups[0][1], downs[0][1])
            up, down = [after(up[0], loaded[0]), up[1]], [after(down[0], loaded[0]), down[1]]
        first = (0, 0, 1)[hop]
        up = [lax.ppermute(c, "row", [(i, i + 1) for i in range(first, 3)]) for c in up]
        last = (3, 3, 1)[hop]
        down = [lax.ppermute(c, "row", [(i + 1, i) for i in range(0, last)]) for c in down]
        ups.append(up)
        downs.append(down)
    return ups, downs, loaded


BLOCK = 256
HALF = BLOCK // 2
WIDTH = 128
VMEM_SPEC = pl.BlockSpec(memory_space=pltpu.VMEM)


def after(x, *earlier):
    return lax.optimization_barrier((x, *earlier))[0]


def split(x):
    high = x.astype(jnp.bfloat16)
    return high, (x - high.astype(jnp.float32)).astype(jnp.bfloat16)


def wide(x):
    return jnp.concatenate(split(x), 1)


def product(tile, pair):
    high, low = split(tile)
    both = jnp.dot(high, pair, preferred_element_type=jnp.float32)
    both = both + jnp.dot(low, pair, preferred_element_type=jnp.float32)
    return both[:, :WIDTH] + both[:, WIDTH:]


def columns(k):
    return slice(k * BLOCK, (k + 1) * BLOCK)


LOW, TOP = slice(0, BLOCK), slice(BLOCK, 2 * BLOCK)


def call(kernel, shapes, scratch=(), space=pltpu.VMEM, inside=True, aliases={}):
    def run(*args):
        return pl.pallas_call(
            kernel,
            out_shape=[(pltpu.VMEM if inside else jax.ShapeDtypeStruct)(s, jnp.float32) for s in shapes],
            in_specs=[pl.BlockSpec(memory_space=space)] * len(args),
            out_specs=[VMEM_SPEC] * len(shapes),
            scratch_shapes=list(scratch),
            input_output_aliases=aliases,
            compiler_params=pltpu.CompilerParams(vmem_limit_bytes=32 * 1024 * 1024),
        )(*[pltpu.with_memory_space_constraint(a, space) for a in args])

    return run


def sent_rows():
    core = lax.axis_index("col") % 2
    low = pl.ds(pl.multiple_of(core * HALF, HALF), HALF)
    return low, pl.ds(pl.multiple_of(BLOCK + core * HALF, HALF), HALF)


def copy_all(pairs, sem):
    copies = [pltpu.make_async_copy(s, d, sem.at[i]) for i, (s, d) in enumerate(pairs)]
    for copy in copies:
        copy.start()
    for copy in copies:
        copy.wait()


def tile_kernel(factor, three_a, three_b, four_a, four_b, sem):
    low, top = sent_rows()
    pairs = []
    for j in range(8):
        out = slice((j % 4) * HALF, (j % 4 + 1) * HALF)
        pairs.append((factor.at[low, pl.ds(j * HALF, HALF)], (three_a, three_b)[j // 4].at[out, :]))
        pairs.append((factor.at[top, pl.ds(BLOCK + j * HALF, HALF)], (four_a, four_b)[j // 4].at[out, :]))
    copy_all(pairs, sem)


def inject_kernel(up_in, down_in, four, three, up, down):
    @pl.when(lax.axis_index("row") == 0)
    def _():
        up[...] = four[...]

    @pl.when(lax.axis_index("row") == 3)
    def _():
        down[...] = three[...]


def load_kernel(past, factor, side, past_out, factor_out, side_out, five, seven, sem):
    _, top = sent_rows()
    mine = pl.ds(pl.multiple_of(lax.axis_index("col") * WIDTH, WIDTH), WIDTH)
    copy_all(
        [
            (past, past_out),
            (factor, factor_out),
            (side.at[:, mine], side_out),
            (factor.at[top, pl.ds(2 * BLOCK, 4 * BLOCK)], five),
            (factor.at[top, pl.ds(0, 6 * BLOCK)], seven),
        ],
        sem,
    )


def pieces(flag, one, two):
    return jnp.concatenate([wide(jnp.where(flag, one, two)), wide(jnp.where(flag, two, one))], 1)


def spread(factor, pair):
    high, low = split(factor)
    both = jnp.dot(high, pair, preferred_element_type=jnp.float32)
    both = both + jnp.dot(low, pair, preferred_element_type=jnp.float32)
    return [both[:, 2 * i * WIDTH : (2 * i + 1) * WIDTH] + both[:, (2 * i + 1) * WIDTH : (2 * i + 2) * WIDTH] for i in range(2)]


def flags():
    row_index = lax.axis_index("row")
    side = lax.axis_index("col") // 2
    return row_index, lax.div(row_index, 2) == side, lax.div(lax.rem(row_index + 3, 4), 2) == side


def late_pair(up1, down3, up3, down1):
    row_index, _, mine_late = flags()
    front = jnp.where(row_index >= 1, up1[...], down3[...])
    back = jnp.where(row_index >= 3, up3[...], down1[...])
    return pieces(mine_late, front, back)


def early_kernel(past, whole, up2a, up2b, down2a, down2b, up1, down3, up3, down1, early, late):
    row_index, mine_first, _ = flags()
    depth = up1.shape[0]
    for at, (u, d) in enumerate(((up2a, down2a), (up2b, down2b))):
        rows = slice(at * depth, (at + 1) * depth)
        pair = pieces(mine_first, whole[rows, :], jnp.where(row_index >= 2, u[...], d[...]))
        got = spread(past[:, rows], pair)
        for i in range(2):
            early[i] = got[i] if at == 0 else early[i] + got[i]
    got = spread(past[:, :depth], late_pair(up1, down3, up3, down1))
    for i in range(2):
        late[i] = got[i]


def late_kernel(past, early, late, up1, down3, up3, down1, away, keep):
    row_index = lax.axis_index("row")
    keeps_early = lax.rem(lax.axis_index("col"), 2) == lax.rem(row_index, 2)
    got = spread(past[:, up1.shape[0] :], late_pair(up1, down3, up3, down1))
    for i in range(2):
        total = late[i] + got[i]
        away[i] = jnp.where(keeps_early, total, early[i])
        keep[i] = jnp.where(keeps_early, early[i], total)


def sum_kernel(keep, came, own, other_low, other_top):
    own[...] = keep[0] + came[0]
    other_low[...] = keep[1, LOW] + came[1, LOW]
    other_top[...] = keep[1, TOP] + came[1, TOP]


def first_kernel(side, one, two, factor, low):
    low[...] = side[LOW, :] - (one[LOW, :] + two[...])

    @pl.when(lax.axis_index("row") == 0)
    def _():
        low[...] = product(factor[LOW, columns(0)], wide(low[...]))


def top_kernel(side, one, two, factor, low, top):
    top[...] = side[TOP, :] - (one[TOP, :] + two[...])

    @pl.when(lax.axis_index("row") == 0)
    def _():
        top[...] = top[...] - product(factor[TOP, columns(0)], wide(low[...]))


def last_kernel(low, low1, kept, last, block4, block5, out):
    row_index = lax.axis_index("row")

    @pl.when(row_index == 0)
    def _():
        out[LOW, :] = low[...]
        out[TOP, :] = block4[...]

    @pl.when(row_index == 1)
    def _():
        out[LOW, :] = low1[...]
        out[TOP, :] = block5[...]

    @pl.when(row_index == 2)
    def _():
        out[...] = kept[...]

    @pl.when(row_index == 3)
    def _():
        out[...] = last[...]


def second_kernel(solved, low_in, top_in, factor, low, top):
    @pl.when(lax.axis_index("row") == 1)
    def _():
        pair = wide(solved[...])
        value = low_in[...] - product(factor[LOW, columns(0)], pair)
        low[...] = product(factor[LOW, columns(1)], wide(value))
        value = top_in[...] - product(factor[TOP, columns(0)], pair)
        top[...] = value - product(factor[TOP, columns(1)], wide(low[...]))


def halves():
    core = lax.axis_index("col") % 2
    own = pl.ds(pl.multiple_of(core * HALF, HALF), HALF)
    other = pl.ds(pl.multiple_of((1 - core) * HALF, HALF), HALF)
    return own, other


def stacked(one, two):
    def tile(j):
        ref, at = (one, two)[j // 2], (j % 2) * BLOCK
        return jnp.concatenate([ref[at : at + HALF, :], ref[at + HALF : at + BLOCK, :]], 1)

    return tile


def third_kernel(
    first, low2, top2, low3, top3, value4, value5, second, factor,
    a3, b3, c3, d3, a4, b4, c4, d4, own5, other5, own7, other7,
    kept, block4, block5, sent, value,
):
    @pl.when(lax.axis_index("row") == 2)
    def _():
        own, other = halves()
        outs = {2: kept.at[LOW, :], 3: sent.at[LOW, :], 4: block4, 5: block5}
        tiles = {
            3: (0, stacked(a3, b3), stacked(c3, d3)),
            4: (1, stacked(a4, b4), stacked(c4, d4)),
            5: (2, lambda j: own5[:, columns(j)], lambda j: other5[:, columns(j)]),
            7: (0, lambda j: own7[:, columns(j)], lambda j: other7[:, columns(j)]),
        }
        for block, ref in {2: low2, 3: low3, 4: value4, 5: value5, 6: top2, 7: top3}.items():
            value[block - 2] = ref[...]

        def apply(block, k, pair, put):
            if block in (2, 6):
                put(slice(None), product(factor[LOW if block == 2 else TOP, columns(k)], pair))
                return
            skip, mine, theirs = tiles[block]
            put(own, product(mine(k - skip), pair))
            put(other, product(theirs(k - skip), pair))

        def update(block, k, pair):
            at = block - 2

            def put(rows, change):
                value[at, rows, :] = value[at, rows, :] - change

            apply(block, k, pair, put)

        def solve(k):
            def put(rows, solved):
                outs[k][rows, :] = solved

            apply(k, k, wide(value[k - 2]), put)
            return wide(outs[k][...])

        blocks = {0: (2, 3, 6, 7), 1: (2, 3, 4, 6, 7), 2: (3, 4, 5, 6, 7), 3: (4, 5, 6, 7), 4: (5, 6, 7), 5: (6, 7)}
        for k in range(6):
            pair = wide(first[...]) if k == 0 else wide(second[...]) if k == 1 else solve(k)
            for block in blocks[k]:
                update(block, k, pair)
        kept[TOP, :] = value[4]
        sent[TOP, :] = value[5]


def line4(right_side, prev_factor, prev_solution, window_factor):
    def move(x, *pairs):
        return lax.ppermute(x, "row", list(pairs))

    def swap(x):
        return lax.ppermute(x, "col", [(0, 1), (1, 0), (2, 3), (3, 2)])

    def cross(x):
        return lax.ppermute(x, "col", [(0, 2), (2, 0), (1, 3), (3, 1)])

    half, size, six = (HALF, 4 * BLOCK), (BLOCK, WIDTH), (HALF, 6 * BLOCK)
    rows = (2 * BLOCK, WIDTH)
    pair = (2, *rows)

    def inject(up, down):
        tiles = call(tile_kernel, [rows] * 4, [pltpu.SemaphoreType.DMA((16,))], pltpu.HBM)(window_factor)
        done = [
            call(inject_kernel, [rows, rows], aliases={0: 0, 1: 1})(up[i], down[i], tiles[2 + i], tiles[i])
            for i in range(2)
        ]
        return [d[0] for d in done], [d[1] for d in done]

    def load(*earlier):
        return call(
            load_kernel,
            [prev_factor.shape, window_factor.shape, rows, half, six],
            [pltpu.SemaphoreType.DMA((5,))],
            pltpu.HBM,
        )(after(prev_factor, *earlier), window_factor, right_side)

    ups, downs, loaded = gather_row(prev_solution, 2, inject, load)
    past, factor, side, send5, send7 = loaded
    own3, own4 = downs[1], ups[2]
    own5 = move(send5, (1, 2))
    own7 = move(send7, (3, 2))
    early, late = call(early_kernel, [pair, pair])(
        past, prev_solution, *ups[1], *downs[1], ups[0][0], downs[2][0], ups[2][0], downs[0][0]
    )
    away, keep = call(late_kernel, [pair, pair])(
        past, early, late, ups[0][1], downs[2][1], ups[2][1], downs[0][1]
    )
    one, other_low, other_top = call(sum_kernel, [rows, size, size])(keep, swap(away))
    two_low, two_top = cross(other_low), cross(other_top)

    (low,) = call(first_kernel, [size])(side, one, two_low, factor)
    first = move(low, (0, 1), (3, 2))
    (top,) = call(top_kernel, [size])(side, one, two_top, factor, low)
    zero = move(low, (0, 2))
    value4 = move(top, (0, 2))
    top3 = move(top, (3, 2))
    tiles = [*own3, *own4, own5, own7]
    others = [swap(after(x, top)) for x in tiles]
    low1, top1 = call(second_kernel, [size, size])(first, low, top, factor)
    second = move(low1, (1, 2))
    value5 = move(top1, (1, 2))
    kept, block4, block5, sent = call(
        third_kernel, [rows, size, size, rows], [pltpu.VMEM((6, *size), jnp.float32)]
    )(
        zero, low, top, first, top3, value4, value5, second, factor,
        *tiles[:2], *others[:2], *tiles[2:4], *others[2:4], own5, others[4], own7, others[5],
    )
    last = move(sent, (2, 3))
    block5 = move(block5, (2, 1))
    block4 = move(block4, (2, 0))
    return call(last_kernel, [rows], inside=False)(low, low1, kept, last, block4, block5)[0]


def body(right_side, prev_factor, prev_solution, window_factor):
    blocks = window_factor.shape[1] // STEPS
    slots = right_side.shape[0] // blocks
    if lax.axis_size("row") == 4 and lax.axis_size("col") == 4 and slots == 2:
        return line4(right_side, prev_factor, prev_solution, window_factor)
    return general(right_side, prev_factor, prev_solution, window_factor)


def solution(mesh):
    in_specs = (
        P(("groups", "row"), None),
        P(("groups", "row"), "col"),
        P(("groups", "col"), "row"),
        P(("groups", "row"), None),
    )
    out_specs = P(("groups", "row"), "col")
    return jax.shard_map(body, mesh=mesh, in_specs=in_specs, out_specs=out_specs, check_vma=False)
```

time: 114 us -> 95.9 us (0.84)
  the two profiles are of different devices: /device:TPU:16 before, /device:TPU:0 now
where the time goes in v3:
time: 95.9 us; the launch traced here: 95.3 us
  starting transfers between devices  43.8 us (46%)
  waiting for transfers between devices  41.7 us (43%)
  Pallas kernels  8.3 us (9%)
  local copies, waits for them, and re-layouts  1.07 us (1%)
    ppermute x11, waiting for transfers between devices, move(): return lax.ppermute(x, 'row', list(pairs))  22.8 us
    ppermute x6, starting transfers between devices, gather_row(): lax.ppermute(c, 'row', [(i, i + 1) for i in range(first, 3)])  19.1 us
    ppermute x11, starting transfers between devices, move(): return lax.ppermute(x, 'row', list(pairs))  13.6 us
    ppermute x6, waiting for transfers between devices, gather_row(): lax.ppermute(c, 'row', [(i + 1, i) for i in range(0, last)])  11.3 us
    pallas_call x12, Pallas kernels, run(): pl.pallas_call(kernel, out_shape=[(pltpu.VMEM if inside else jax.ShapeDty...  8.3 us
    ppermute x6, starting transfers between devices, gather_row(): lax.ppermute(c, 'row', [(i + 1, i) for i in range(0, last)])  7.74 us
    ppermute x2, waiting for transfers between devices, cross(): return lax.ppermute(x, 'col', [(0, 2), (2, 0), (1, 3), (3, 1)])  6.06 us
    ppermute x2, starting transfers between devices, cross(): return lax.ppermute(x, 'col', [(0, 2), (2, 0), (1, 3), (3, 1)])  2.09 us
  transfers between devices with their start and end apart: 32, of which 12 were waited for; matrix products, arithmetic and copies ran while one was open for 0% of the time, Pallas kernels for 8%

profile of v3, /device:TPU:0, one launch (start us, length us, event | category | flops | bytes accessed | tf_op | source)
XLA Modules:
  0.0 95.3 jit_solution(15655188202442495508)
XLA Ops:
  1.1 4.9 %collective-permute-start.2 = (f32[512,128]{1,0:T(8,128)S(1)}, f32[512,128]{1,0:T(8,128)S(1)}, u32[]{:S(2)}, u32[]{:S(2)}) collective-permute-start(f32[512,128]{1,0:T(8,128)S(1)} %get-tuple-element.75), channel_id=1, source_target_pairs={{0,4},{4,8},{8,12},{1,5},{5,9},{9,13},{2,6},{6,10},{10,14},{3,7},{... | collective-permute-start | bytes 786440 | tf_op jit(solution)/shard_map/ppermute | solution.py:53
  6.0 1.3 %collective-permute-start.3 = (f32[512,128]{1,0:T(8,128)S(1)}, f32[512,128]{1,0:T(8,128)S(1)}, u32[]{:S(2)}, u32[]{:S(2)}) collective-permute-start(f32[512,128]{1,0:T(8,128)S(1)} %get-tuple-element.75), channel_id=1, source_target_pairs={{4,0},{8,4},{12,8},{5,1},{9,5},{13,9},{6,2},{10,6},{14,10},{7,3},{... | collective-permute-start | bytes 786440 | tf_op jit(solution)/shard_map/ppermute | solution.py:55
  7.3 4.6 %collective-permute-start = (f32[512,128]{1,0:T(8,128)S(1)}, f32[512,128]{1,0:T(8,128)S(1)}, u32[]{:S(2)}, u32[]{:S(2)}) collective-permute-start(f32[512,128]{1,0:T(8,128)S(1)} %get-tuple-element.76), channel_id=1, source_target_pairs={{0,4},{4,8},{8,12},{1,5},{5,9},{9,13},{2,6},{6,10},{10,14},{3,7},{... | collective-permute-start | bytes 786440 | tf_op jit(solution)/shard_map/ppermute | solution.py:53
  11.9 1.3 %collective-permute-start.1 = (f32[512,128]{1,0:T(8,128)S(1)}, f32[512,128]{1,0:T(8,128)S(1)}, u32[]{:S(2)}, u32[]{:S(2)}) collective-permute-start(f32[512,128]{1,0:T(8,128)S(1)} %get-tuple-element.76), channel_id=1, source_target_pairs={{4,0},{8,4},{12,8},{5,1},{9,5},{13,9},{6,2},{10,6},{14,10},{7,3},{... | collective-permute-start | bytes 786440 | tf_op jit(solution)/shard_map/ppermute | solution.py:55
  13.2 1.4 %shard_map.46 = (f32[512,128]{1,0:T(8,128)S(1)}, f32[512,128]{1,0:T(8,128)S(1)}, f32[512,128]{1,0:T(8,128)S(1)}, f32[512,128]{1,0:T(8,128)S(1)}) custom-call(f32[512,1536]{1,0:T(8,128)} %factor.3), custom_call_target="tpu_custom_call" | custom-call | tf_op jit(solution)/shard_map/pallas_call | solution.py:96
  14.6 1.3 %collective-permute-done.3.down_in = f32[512,128]{1,0:T(8,128)S(1)} collective-permute-done((f32[512,128]{1,0:T(8,128)S(1)}, f32[512,128]{1,0:T(8,128)S(1)}, u32[]{:S(2)}, u32[]{:S(2)}) %collective-permute-start.3) | collective-permute-done | bytes 262176 | tf_op jit(solution)/shard_map/ppermute | solution.py:55
  15.9 3.5 %collective-permute-start.4 = (f32[512,128]{1,0:T(8,128)S(1)}, f32[512,128]{1,0:T(8,128)S(1)}, u32[]{:S(2)}, u32[]{:S(2)}) collective-permute-start(f32[512,128]{1,0:T(8,128)S(1)} %get-tuple-element.49.up1), channel_id=1, source_target_pairs={{0,4},{4,8},{8,12},{1,5},{5,9},{9,13},{2,6},{6,10},{10,14},{3,7},{... | collective-permute-start | bytes 786440 | tf_op jit(solution)/shard_map/ppermute | solution.py:53
  19.4 1.3 %collective-permute-start.6 = (f32[512,128]{1,0:T(8,128)S(1)}, f32[512,128]{1,0:T(8,128)S(1)}, u32[]{:S(2)}, u32[]{:S(2)}) collective-permute-start(f32[512,128]{1,0:T(8,128)S(1)} %get-tuple-element.50.down1), channel_id=1, source_target_pairs={{4,0},{8,4},{12,8},{5,1},{9,5},{13,9},{6,2},{10,6},{14,10},{7,3},{... | collective-permute-start | bytes 786440 | tf_op jit(solution)/shard_map/ppermute | solution.py:55
  21.3 1.3 %collective-permute-start.7 = (f32[512,128]{1,0:T(8,128)S(1)}, f32[512,128]{1,0:T(8,128)S(1)}, u32[]{:S(2)}, u32[]{:S(2)}) collective-permute-start(f32[512,128]{1,0:T(8,128)S(1)} %get-tuple-element.43.down1), channel_id=1, source_target_pairs={{4,0},{8,4},{12,8},{5,1},{9,5},{13,9},{6,2},{10,6},{14,10},{7,3},{... | collective-permute-start | bytes 786440 | tf_op jit(solution)/shard_map/ppermute | solution.py:55
  22.6 4.8 %collective-permute-start.5 = (f32[512,128]{1,0:T(8,128)S(1)}, f32[512,128]{1,0:T(8,128)S(1)}, u32[]{:S(2)}, u32[]{:S(2)}) collective-permute-start(f32[512,128]{1,0:T(8,128)S(1)} %get-tuple-element.42.up1), channel_id=1, source_target_pairs={{0,4},{4,8},{8,12},{1,5},{5,9},{9,13},{2,6},{6,10},{10,14},{3,7},{... | collective-permute-start | bytes 786440 | tf_op jit(solution)/shard_map/ppermute | solution.py:53
  27.4 3.0 %shard_map.48 = (f32[512,1024]{1,0:T(8,128)S(1)}, f32[512,1536]{1,0:T(8,128)S(1)}, f32[512,128]{1,0:T(8,128)S(1)}, f32[128,1024]{1,0:T(8,128)S(1)}, f32[128,1536]{1,0:T(8,128)S(1)}) custom-call(f32[512,1024]{1,0:T(8,128)} %past, f32[512,1536]{1,0:T(8,128)} %factor.3, f32[512,512]{1,0:T(8,128)} %side.1), custom_call_target="tpu_custom_call" | custom-call | tf_op jit(solution)/shard_map/pallas_call | solution.py:96
  31.1 1.3 %collective-permute-start.8 = (f32[512,128]{1,0:T(8,128)S(1)}, f32[512,128]{1,0:T(8,128)S(1)}, u32[]{:S(2)}, u32[]{:S(2)}) collective-permute-start(f32[512,128]{1,0:T(8,128)S(1)} %collective-permute-done.6.down2a.a3), channel_id=1, source_target_pairs={{4,0},{5,1},{6,2},{7,3},{20,16},{21,17},{22,18},{23,19}} | collective-permute-start | bytes 786440 | tf_op jit(solution)/shard_map/ppermute | solution.py:55
  33.4 1.3 %collective-permute-start.10 = (f32[512,128]{1,0:T(8,128)S(1)}, f32[512,128]{1,0:T(8,128)S(1)}, u32[]{:S(2)}, u32[]{:S(2)}) collective-permute-start(f32[512,128]{1,0:T(8,128)S(1)} %collective-permute-done.7.down2b.b3), channel_id=1, source_target_pairs={{4,0},{5,1},{6,2},{7,3},{20,16},{21,17},{22,18},{23,19}} | collective-permute-start | bytes 786440 | tf_op jit(solution)/shard_map/ppermute | solution.py:55
  36.1 7.5 %collective-permute-done.8.down3 = f32[512,128]{1,0:T(8,128)S(1)} collective-permute-done((f32[512,128]{1,0:T(8,128)S(1)}, f32[512,128]{1,0:T(8,128)S(1)}, u32[]{:S(2)}, u32[]{:S(2)}) %collective-permute-start.8) | collective-permute-done | bytes 262176 | tf_op jit(solution)/shard_map/ppermute | solution.py:55
  43.6 1.8 %shard_map.50 = (f32[2,512,128]{2,1,0:T(8,128)S(1)}, f32[2,512,128]{2,1,0:T(8,128)S(1)}) custom-call(f32[512,1024]{1,0:T(8,128)S(1)} %get-tuple-element.46.past, f32[1024,128]{1,0:T(8,128)S(1)} %copy-done, f32[512,128]{1,0:T(8,128)S(1)} %collective-permute-done.4.up2a, f32[512,128]{1,0:T(8,128)S(1)} %collective-permute-done.5.up2b, ...), custom_call_target="tpu_custom_call" | custom-call | tf_op jit(solution)/shard_map/pallas_call | solution.py:96
  49.2 1.6 %collective-permute-start.13 = (f32[256,128]{1,0:T(8,128)S(1)}, f32[256,128]{1,0:T(8,128)S(1)}, u32[]{:S(2)}, u32[]{:S(2)}) collective-permute-start(f32[256,128]{1,0:T(8,128)S(1)} %get-tuple-element.58), channel_id=1, source_target_pairs={{0,2},{2,0},{1,3},{3,1},{4,6},{6,4},{5,7},{7,5},{8,10},{10,8},{9,1... | collective-permute-start | bytes 393224 | tf_op jit(solution)/shard_map/ppermute | solution.py:333
  51.3 4.3 %collective-permute-done.13.two = f32[256,128]{1,0:T(8,128)S(1)} collective-permute-done((f32[256,128]{1,0:T(8,128)S(1)}, f32[256,128]{1,0:T(8,128)S(1)}, u32[]{:S(2)}, u32[]{:S(2)}) %collective-permute-start.13) | collective-permute-done | bytes 131104 | tf_op jit(solution)/shard_map/ppermute | solution.py:333
  55.8 1.7 %collective-permute-done.15.two = f32[256,128]{1,0:T(8,128)S(1)} collective-permute-done((f32[256,128]{1,0:T(8,128)S(1)}, f32[256,128]{1,0:T(8,128)S(1)}, u32[]{:S(2)}, u32[]{:S(2)}) %collective-permute-start.15) | collective-permute-done | bytes 131104 | tf_op jit(solution)/shard_map/ppermute | solution.py:333
  57.9 3.3 %collective-permute-start.14 = (f32[256,128]{1,0:T(8,128)S(1)}, f32[256,128]{1,0:T(8,128)S(1)}, u32[]{:S(2)}, u32[]{:S(2)}) collective-permute-start(f32[256,128]{1,0:T(8,128)S(1)} %shard_map.53.low.low_in.low2), channel_id=1, source_target_pairs={{0,4},{12,8},{1,5},{13,9},{2,6},{14,10},{3,7},{15,11},{16,20},{28,... | collective-permute-start | bytes 393224 | tf_op jit(solution)/shard_map/ppermute | solution.py:327
  61.9 1.3 %collective-permute-start.18 = (f32[256,128]{1,0:T(8,128)S(1)}, f32[256,128]{1,0:T(8,128)S(1)}, u32[]{:S(2)}, u32[]{:S(2)}) collective-permute-start(f32[256,128]{1,0:T(8,128)S(1)} %shard_map.54.top_in.top2), channel_id=1, source_target_pairs={{0,8},{1,9},{2,10},{3,11},{16,24},{17,25},{18,26},{19,27}} | collective-permute-start | bytes 393224 | tf_op jit(solution)/shard_map/ppermute | solution.py:327
  63.2 3.0 %collective-permute-start.16 = (f32[256,128]{1,0:T(8,128)S(1)}, f32[256,128]{1,0:T(8,128)S(1)}, u32[]{:S(2)}, u32[]{:S(2)}) collective-permute-start(f32[256,128]{1,0:T(8,128)S(1)} %shard_map.53.low.low_in.low2), channel_id=1, source_target_pairs={{0,8},{1,9},{2,10},{3,11},{16,24},{17,25},{18,26},{19,27}} | collective-permute-start | bytes 393224 | tf_op jit(solution)/shard_map/ppermute | solution.py:327
  67.8 2.4 %collective-permute-done.16.first = f32[256,128]{1,0:T(8,128)S(1)} collective-permute-done((f32[256,128]{1,0:T(8,128)S(1)}, f32[256,128]{1,0:T(8,128)S(1)}, u32[]{:S(2)}, u32[]{:S(2)}) %collective-permute-start.16) | collective-permute-done | bytes 131104 | tf_op jit(solution)/shard_map/ppermute | solution.py:327
  73.2 1.3 %collective-permute-start.30 = (f32[256,128]{1,0:T(8,128)S(1)}, f32[256,128]{1,0:T(8,128)S(1)}, u32[]{:S(2)}, u32[]{:S(2)}) collective-permute-start(f32[256,128]{1,0:T(8,128)S(1)} %get-tuple-element.73), channel_id=1, source_target_pairs={{8,0},{9,1},{10,2},{11,3},{24,16},{25,17},{26,18},{27,19}} | collective-permute-start | bytes 393224 | tf_op jit(solution)/shard_map/ppermute | solution.py:327
  75.2 19.4 %collective-permute-done.30.block4 = f32[256,128]{1,0:T(8,128)S(1)} collective-permute-done((f32[256,128]{1,0:T(8,128)S(1)}, f32[256,128]{1,0:T(8,128)S(1)}, u32[]{:S(2)}, u32[]{:S(2)}) %collective-permute-start.30) | collective-permute-done | bytes 131104 | tf_op jit(solution)/shard_map/ppermute | solution.py:327
  (55 shorter events, 16.1 us)
Async XLA Ops:
  1.1 13.5 %collective-permute-start.2 = (f32[512,128]{1,0:T(8,128)S(1)}, f32[512,128]{1,0:T(8,128)S(1)}, u32[]{:S(2)}, u32[]{:S(2)}) collective-permute-start(f32[512,128]{1,0:T(8,128)S(1)} %get-tuple-element.75), channel_id=1, source_target_pairs={{0,4},{4,8},{8,12},{1,5},{5,9},{9,13},{2,6},{6,10},{10,14},{3,7},{... | collective-permute-start | bytes 786440 | tf_op jit(solution)/shard_map/ppermute | solution.py:53
  6.0 9.9 %collective-permute-start.3 = (f32[512,128]{1,0:T(8,128)S(1)}, f32[512,128]{1,0:T(8,128)S(1)}, u32[]{:S(2)}, u32[]{:S(2)}) collective-permute-start(f32[512,128]{1,0:T(8,128)S(1)} %get-tuple-element.75), channel_id=1, source_target_pairs={{4,0},{8,4},{12,8},{5,1},{9,5},{13,9},{6,2},{10,6},{14,10},{7,3},{... | collective-permute-start | bytes 786440 | tf_op jit(solution)/shard_map/ppermute | solution.py:55
  7.3 13.4 %collective-permute-start = (f32[512,128]{1,0:T(8,128)S(1)}, f32[512,128]{1,0:T(8,128)S(1)}, u32[]{:S(2)}, u32[]{:S(2)}) collective-permute-start(f32[512,128]{1,0:T(8,128)S(1)} %get-tuple-element.76), channel_id=1, source_target_pairs={{0,4},{4,8},{8,12},{1,5},{5,9},{9,13},{2,6},{6,10},{10,14},{3,7},{... | collective-permute-start | bytes 786440 | tf_op jit(solution)/shard_map/ppermute | solution.py:53
  11.9 9.4 %collective-permute-start.1 = (f32[512,128]{1,0:T(8,128)S(1)}, f32[512,128]{1,0:T(8,128)S(1)}, u32[]{:S(2)}, u32[]{:S(2)}) collective-permute-start(f32[512,128]{1,0:T(8,128)S(1)} %get-tuple-element.76), channel_id=1, source_target_pairs={{4,0},{8,4},{12,8},{5,1},{9,5},{13,9},{6,2},{10,6},{14,10},{7,3},{... | collective-permute-start | bytes 786440 | tf_op jit(solution)/shard_map/ppermute | solution.py:55
  15.9 14.4 %collective-permute-start.4 = (f32[512,128]{1,0:T(8,128)S(1)}, f32[512,128]{1,0:T(8,128)S(1)}, u32[]{:S(2)}, u32[]{:S(2)}) collective-permute-start(f32[512,128]{1,0:T(8,128)S(1)} %get-tuple-element.49.up1), channel_id=1, source_target_pairs={{0,4},{4,8},{8,12},{1,5},{5,9},{9,13},{2,6},{6,10},{10,14},{3,7},{... | collective-permute-start | bytes 786440 | tf_op jit(solution)/shard_map/ppermute | solution.py:53
  19.4 11.7 %collective-permute-start.6 = (f32[512,128]{1,0:T(8,128)S(1)}, f32[512,128]{1,0:T(8,128)S(1)}, u32[]{:S(2)}, u32[]{:S(2)}) collective-permute-start(f32[512,128]{1,0:T(8,128)S(1)} %get-tuple-element.50.down1), channel_id=1, source_target_pairs={{4,0},{8,4},{12,8},{5,1},{9,5},{13,9},{6,2},{10,6},{14,10},{7,3},{... | collective-permute-start | bytes 786440 | tf_op jit(solution)/shard_map/ppermute | solution.py:55
  21.3 12.1 %collective-permute-start.7 = (f32[512,128]{1,0:T(8,128)S(1)}, f32[512,128]{1,0:T(8,128)S(1)}, u32[]{:S(2)}, u32[]{:S(2)}) collective-permute-start(f32[512,128]{1,0:T(8,128)S(1)} %get-tuple-element.43.down1), channel_id=1, source_target_pairs={{4,0},{8,4},{12,8},{5,1},{9,5},{13,9},{6,2},{10,6},{14,10},{7,3},{... | collective-permute-start | bytes 786440 | tf_op jit(solution)/shard_map/ppermute | solution.py:55
  22.6 12.0 %collective-permute-start.5 = (f32[512,128]{1,0:T(8,128)S(1)}, f32[512,128]{1,0:T(8,128)S(1)}, u32[]{:S(2)}, u32[]{:S(2)}) collective-permute-start(f32[512,128]{1,0:T(8,128)S(1)} %get-tuple-element.42.up1), channel_id=1, source_target_pairs={{0,4},{4,8},{8,12},{1,5},{5,9},{9,13},{2,6},{6,10},{10,14},{3,7},{... | collective-permute-start | bytes 786440 | tf_op jit(solution)/shard_map/ppermute | solution.py:53
  30.4 5.7 %collective-permute-start.9 = (f32[512,128]{1,0:T(8,128)S(1)}, f32[512,128]{1,0:T(8,128)S(1)}, u32[]{:S(2)}, u32[]{:S(2)}) collective-permute-start(f32[512,128]{1,0:T(8,128)S(1)} %collective-permute-done.4.up2a), channel_id=1, source_target_pairs={{4,8},{8,12},{5,9},{9,13},{6,10},{10,14},{7,11},{11,15},{20,24},{2... | collective-permute-start | bytes 786440 | tf_op jit(solution)/shard_map/ppermute | solution.py:53
  31.1 12.5 %collective-permute-start.8 = (f32[512,128]{1,0:T(8,128)S(1)}, f32[512,128]{1,0:T(8,128)S(1)}, u32[]{:S(2)}, u32[]{:S(2)}) collective-permute-start(f32[512,128]{1,0:T(8,128)S(1)} %collective-permute-done.6.down2a.a3), channel_id=1, source_target_pairs={{4,0},{5,1},{6,2},{7,3},{20,16},{21,17},{22,18},{23,19}} | collective-permute-start | bytes 786440 | tf_op jit(solution)/shard_map/ppermute | solution.py:55
  33.4 13.0 %collective-permute-start.10 = (f32[512,128]{1,0:T(8,128)S(1)}, f32[512,128]{1,0:T(8,128)S(1)}, u32[]{:S(2)}, u32[]{:S(2)}) collective-permute-start(f32[512,128]{1,0:T(8,128)S(1)} %collective-permute-done.7.down2b.b3), channel_id=1, source_target_pairs={{4,0},{5,1},{6,2},{7,3},{20,16},{21,17},{22,18},{23,19}} | collective-permute-start | bytes 786440 | tf_op jit(solution)/shard_map/ppermute | solution.py:55
  34.7 11.7 %collective-permute-start.11 = (f32[512,128]{1,0:T(8,128)S(1)}, f32[512,128]{1,0:T(8,128)S(1)}, u32[]{:S(2)}, u32[]{:S(2)}) collective-permute-start(f32[512,128]{1,0:T(8,128)S(1)} %collective-permute-done.5.up2b), channel_id=1, source_target_pairs={{4,8},{8,12},{5,9},{9,13},{6,10},{10,14},{7,11},{11,15},{20,24},{2... | collective-permute-start | bytes 786440 | tf_op jit(solution)/shard_map/ppermute | solution.py:53
  35.4 22.5 %collective-permute-start.27 = (f32[128,1536]{1,0:T(8,128)S(1)}, f32[128,1536]{1,0:T(8,128)S(1)}, u32[]{:S(2)}, u32[]{:S(2)}) collective-permute-start(f32[128,1536]{1,0:T(8,128)S(1)} %get-tuple-element.69), channel_id=1, source_target_pairs={{12,8},{13,9},{14,10},{15,11},{28,24},{29,25},{30,26},{31,27}} | collective-permute-start | bytes 2359304 | tf_op jit(solution)/shard_map/ppermute | solution.py:327
  47.2 16.0 %collective-permute-start.25 = (f32[128,1024]{1,0:T(8,128)S(1)}, f32[128,1024]{1,0:T(8,128)S(1)}, u32[]{:S(2)}, u32[]{:S(2)}) collective-permute-start(f32[128,1024]{1,0:T(8,128)S(1)} %get-tuple-element.67), channel_id=1, source_target_pairs={{4,8},{5,9},{6,10},{7,11},{20,24},{21,25},{22,26},{23,27}} | collective-permute-start | bytes 1572872 | tf_op jit(solution)/shard_map/ppermute | solution.py:327
  49.2 6.4 %collective-permute-start.13 = (f32[256,128]{1,0:T(8,128)S(1)}, f32[256,128]{1,0:T(8,128)S(1)}, u32[]{:S(2)}, u32[]{:S(2)}) collective-permute-start(f32[256,128]{1,0:T(8,128)S(1)} %get-tuple-element.58), channel_id=1, source_target_pairs={{0,2},{2,0},{1,3},{3,1},{4,6},{6,4},{5,7},{7,5},{8,10},{10,8},{9,1... | collective-permute-start | bytes 393224 | tf_op jit(solution)/shard_map/ppermute | solution.py:333
  50.8 6.8 %collective-permute-start.15 = (f32[256,128]{1,0:T(8,128)S(1)}, f32[256,128]{1,0:T(8,128)S(1)}, u32[]{:S(2)}, u32[]{:S(2)}) collective-permute-start(f32[256,128]{1,0:T(8,128)S(1)} %get-tuple-element.60), channel_id=1, source_target_pairs={{0,2},{2,0},{1,3},{3,1},{4,6},{6,4},{5,7},{7,5},{8,10},{10,8},{9,1... | collective-permute-start | bytes 393224 | tf_op jit(solution)/shard_map/ppermute | solution.py:333
  57.9 14.6 %collective-permute-start.28 = (f32[128,1536]{1,0:T(8,128)S(1)}, f32[128,1536]{1,0:T(8,128)S(1)}, u32[]{:S(2)}, u32[]{:S(2)}) collective-permute-start(f32[128,1536]{1,0:T(8,128)S(1)} %collective-permute-done.27.own7), channel_id=1, source_target_pairs={{0,1},{1,0},{2,3},{3,2},{4,5},{5,4},{6,7},{7,6},{8,9},{9,8},{10,11... | collective-permute-start | bytes 2359304 | tf_op jit(solution)/shard_map/ppermute | solution.py:330
  57.9 8.3 %collective-permute-start.14 = (f32[256,128]{1,0:T(8,128)S(1)}, f32[256,128]{1,0:T(8,128)S(1)}, u32[]{:S(2)}, u32[]{:S(2)}) collective-permute-start(f32[256,128]{1,0:T(8,128)S(1)} %shard_map.53.low.low_in.low2), channel_id=1, source_target_pairs={{0,4},{12,8},{1,5},{13,9},{2,6},{14,10},{3,7},{15,11},{16,20},{28,... | collective-permute-start | bytes 393224 | tf_op jit(solution)/shard_map/ppermute | solution.py:327
  61.9 5.9 %collective-permute-start.18 = (f32[256,128]{1,0:T(8,128)S(1)}, f32[256,128]{1,0:T(8,128)S(1)}, u32[]{:S(2)}, u32[]{:S(2)}) collective-permute-start(f32[256,128]{1,0:T(8,128)S(1)} %shard_map.54.top_in.top2), channel_id=1, source_target_pairs={{0,8},{1,9},{2,10},{3,11},{16,24},{17,25},{18,26},{19,27}} | collective-permute-start | bytes 393224 | tf_op jit(solution)/shard_map/ppermute | solution.py:327
  63.2 7.0 %collective-permute-start.16 = (f32[256,128]{1,0:T(8,128)S(1)}, f32[256,128]{1,0:T(8,128)S(1)}, u32[]{:S(2)}, u32[]{:S(2)}) collective-permute-start(f32[256,128]{1,0:T(8,128)S(1)} %shard_map.53.low.low_in.low2), channel_id=1, source_target_pairs={{0,8},{1,9},{2,10},{3,11},{16,24},{17,25},{18,26},{19,27}} | collective-permute-start | bytes 393224 | tf_op jit(solution)/shard_map/ppermute | solution.py:327
  66.3 6.1 %collective-permute-start.26 = (f32[128,1024]{1,0:T(8,128)S(1)}, f32[128,1024]{1,0:T(8,128)S(1)}, u32[]{:S(2)}, u32[]{:S(2)}) collective-permute-start(f32[128,1024]{1,0:T(8,128)S(1)} %collective-permute-done.25.own5), channel_id=1, source_target_pairs={{0,1},{1,0},{2,3},{3,2},{4,5},{5,4},{6,7},{7,6},{8,9},{9,8},{10,11... | collective-permute-start | bytes 1572872 | tf_op jit(solution)/shard_map/ppermute | solution.py:330
  72.5 22.0 %collective-permute-start.29 = (f32[512,128]{1,0:T(8,128)S(1)}, f32[512,128]{1,0:T(8,128)S(1)}, u32[]{:S(2)}, u32[]{:S(2)}) collective-permute-start(f32[512,128]{1,0:T(8,128)S(1)} %get-tuple-element.72), channel_id=1, source_target_pairs={{8,12},{9,13},{10,14},{11,15},{24,28},{25,29},{26,30},{27,31}} | collective-permute-start | bytes 786440 | tf_op jit(solution)/shard_map/ppermute | solution.py:327
  73.2 21.3 %collective-permute-start.30 = (f32[256,128]{1,0:T(8,128)S(1)}, f32[256,128]{1,0:T(8,128)S(1)}, u32[]{:S(2)}, u32[]{:S(2)}) collective-permute-start(f32[256,128]{1,0:T(8,128)S(1)} %get-tuple-element.73), channel_id=1, source_target_pairs={{8,0},{9,1},{10,2},{11,3},{24,16},{25,17},{26,18},{27,19}} | collective-permute-start | bytes 393224 | tf_op jit(solution)/shard_map/ppermute | solution.py:327
  74.5 20.0 %collective-permute-start.31 = (f32[256,128]{1,0:T(8,128)S(1)}, f32[256,128]{1,0:T(8,128)S(1)}, u32[]{:S(2)}, u32[]{:S(2)}) collective-permute-start(f32[256,128]{1,0:T(8,128)S(1)} %get-tuple-element.74), channel_id=1, source_target_pairs={{8,4},{9,5},{10,6},{11,7},{24,20},{25,21},{26,22},{27,23}} | collective-permute-start | bytes 393224 | tf_op jit(solution)/shard_map/ppermute | solution.py:327
  (9 other events, 41.1 us)

commit v4 on v3

v4 whole, which is shorter than its diff:
```python
import jax
import jax.numpy as jnp
from jax import lax
from jax.experimental import pallas as pl
from jax.experimental.pallas import tpu as pltpu
from jax.sharding import PartitionSpec as P

NRHS = 512
STEPS = 6
HIGH = lax.Precision.HIGH


def mul(a, b):
    return jnp.dot(a, b, precision=HIGH, preferred_element_type=jnp.float32)


def general(right_side, prev_factor, prev_solution, window_factor):
    row_count = lax.axis_size("row")
    row_index = lax.axis_index("row")
    col_count = lax.axis_size("col")
    col_index = lax.axis_index("col")
    blocks = window_factor.shape[1] // STEPS
    slots = right_side.shape[0] // blocks
    width = NRHS // col_count
    partial_value = mul(prev_factor, lax.all_gather(prev_solution, "row", axis=1, tiled=True))
    prior = lax.psum_scatter(partial_value, "col", scatter_dimension=1, tiled=True)
    mine = lax.dynamic_slice_in_dim(right_side, col_index * width, width, 1)
    resid = (mine - prior).reshape(slots, blocks, width)
    tiles = window_factor.reshape(slots, blocks, STEPS, blocks)
    order = jnp.arange(slots, dtype=jnp.int32) * row_count + row_index
    for step in range(STEPS):
        root = step % row_count
        solved = mul(tiles[step // row_count, :, step, :], resid[step // row_count])
        solved = lax.psum(jnp.where(row_index == root, solved, jnp.zeros_like(solved)), "row")
        update = jnp.einsum("sij,jn->sin", tiles[:, :, step, :], solved, precision=HIGH)
        resid = jnp.where((order > step)[:, None, None], resid - update, resid)
        resid = jnp.where((order == step)[:, None, None], solved[None], resid)
    return resid.reshape(slots * blocks, width)


BLOCK = 256
HALF = BLOCK // 2
WIDTH = 128
VMEM_SPEC = pl.BlockSpec(memory_space=pltpu.VMEM)


def after(x, *earlier):
    return lax.optimization_barrier((x, *earlier))[0]


def split(x):
    high = x.astype(jnp.bfloat16)
    return high, (x - high.astype(jnp.float32)).astype(jnp.bfloat16)


def wide(x):
    return jnp.concatenate(split(x), 1)


def product(tile, pair):
    high, low = split(tile)
    both = jnp.dot(high, pair, preferred_element_type=jnp.float32)
    both = both + jnp.dot(low, pair, preferred_element_type=jnp.float32)
    return both[:, :WIDTH] + both[:, WIDTH:]


def columns(k):
    return slice(k * BLOCK, (k + 1) * BLOCK)


LOW, TOP = slice(0, BLOCK), slice(BLOCK, 2 * BLOCK)


def call(kernel, shapes, scratch=(), space=pltpu.VMEM, inside=True, aliases={}):
    def run(*args):
        return pl.pallas_call(
            kernel,
            out_shape=[(pltpu.VMEM if inside else jax.ShapeDtypeStruct)(s, jnp.float32) for s in shapes],
            in_specs=[pl.BlockSpec(memory_space=space)] * len(args),
            out_specs=[VMEM_SPEC] * len(shapes),
            scratch_shapes=list(scratch),
            input_output_aliases=aliases,
            compiler_params=pltpu.CompilerParams(vmem_limit_bytes=32 * 1024 * 1024),
        )(*[pltpu.with_memory_space_constraint(a, space) for a in args])

    return run


def sent_rows():
    core = lax.axis_index("col") % 2
    low = pl.ds(pl.multiple_of(core * HALF, HALF), HALF)
    return low, pl.ds(pl.multiple_of(BLOCK + core * HALF, HALF), HALF)


def copy_all(pairs, sem):
    copies = [pltpu.make_async_copy(s, d, sem.at[i]) for i, (s, d) in enumerate(pairs)]
    for copy in copies:
        copy.start()
    for copy in copies:
        copy.wait()


def stack_copies(source, rows, start, out, count=8):
    return [
        (source.at[rows, pl.ds(start + j * HALF, HALF)], out.at[slice(j * HALF, (j + 1) * HALF), :])
        for j in range(count)
    ]


def tile_kernel(factor, three, four, sem):
    low, top = sent_rows()
    copy_all(stack_copies(factor, low, 0, three) + stack_copies(factor, top, BLOCK, four), sem)


def inject_kernel(x_in, three, four, x):
    @pl.when(lax.axis_index("row") == 0)
    def _():
        x[...] = four[...]

    @pl.when(lax.axis_index("row") == 3)
    def _():
        x[...] = three[...]


def inject_seven_kernel(x_in, seven, x):
    @pl.when(lax.axis_index("row") == 3)
    def _():
        x[...] = seven[...]


def load_kernel(past, factor, side, past_out, factor_out, side_out, five, seven, eight, sem):
    _, top = sent_rows()
    mine = pl.ds(pl.multiple_of(lax.axis_index("col") * WIDTH, WIDTH), WIDTH)
    copy_all(
        stack_copies(factor, top, 0, seven)
        + [
            (past, past_out),
            (factor, factor_out),
            (side.at[:, mine], side_out),
        ]
        + stack_copies(factor, top, 2 * BLOCK, five)
        + stack_copies(factor, top, 4 * BLOCK, eight, 4),
        sem,
    )


def spread(factor, *parts):
    high, low = split(factor)
    pair = jnp.concatenate([wide(x) for x in parts], 1)
    both = jnp.dot(high, pair, preferred_element_type=jnp.float32)
    both = both + jnp.dot(low, pair, preferred_element_type=jnp.float32)
    lanes = [both[:, i * WIDTH : (i + 1) * WIDTH] for i in range(2 * len(parts))]
    return [lanes[2 * i] + lanes[2 * i + 1] for i in range(len(parts))]


def at_end():
    row_index = lax.axis_index("row")
    return jnp.logical_or(row_index == 0, row_index == 3)


def early_kernel(past, own, edge1, edge2, middle2, early):
    got = spread(past[...], own[...], jnp.where(at_end(), edge2[...], middle2[...]), edge1[...])
    for i in range(3):
        early[i] = got[i]


def late_kernel(past, early, edge3, middle3, away, keep):
    row_index, col_index = lax.axis_index("row"), lax.axis_index("col")
    keeps_even = lax.rem(col_index, 2) == lax.rem(row_index, 2)
    (three,) = spread(past[...], jnp.where(at_end(), edge3[...], middle3[...]))
    near = lax.div(row_index, 2) == lax.div(col_index, 2)
    even = [jnp.where(near, early[0], early[1]), jnp.where(near, early[1], early[0])]
    odd = [jnp.where(near, early[2], three), jnp.where(near, three, early[2])]
    for i in range(2):
        away[i] = jnp.where(keeps_even, odd[i], even[i])
        keep[i] = jnp.where(keeps_even, even[i], odd[i])


def sum_kernel(keep, came, own, other_low, other_top):
    own[...] = keep[0] + came[0]
    other_low[...] = keep[1, LOW] + came[1, LOW]
    other_top[...] = keep[1, TOP] + came[1, TOP]


def first_kernel(side, one, two, factor, low):
    low[...] = side[LOW, :] - (one[LOW, :] + two[...])

    @pl.when(lax.axis_index("row") == 0)
    def _():
        low[...] = product(factor[LOW, columns(0)], wide(low[...]))


def top_kernel(side, one, two, factor, low, top):
    top[...] = side[TOP, :] - (one[TOP, :] + two[...])

    @pl.when(lax.axis_index("row") == 0)
    def _():
        top[...] = top[...] - product(factor[TOP, columns(0)], wide(low[...]))


def second_kernel(solved, low_in, factor, low):
    @pl.when(lax.axis_index("row") == 1)
    def _():
        value = low_in[...] - product(factor[LOW, columns(0)], wide(solved[...]))
        low[LOW, :] = solved[...]
        low[TOP, :] = product(factor[LOW, columns(1)], wide(value))


def five_kernel(solved, top_in, factor, top):
    @pl.when(lax.axis_index("row") == 1)
    def _():
        value = top_in[...] - product(factor[TOP, columns(0)], wide(solved[LOW, :]))
        top[...] = value - product(factor[TOP, columns(1)], wide(solved[TOP, :]))


def last_kernel(low, low1, low2, top2, last, block4, block5, out):
    row_index = lax.axis_index("row")

    @pl.when(row_index == 0)
    def _():
        out[LOW, :] = low[...]
        out[TOP, :] = block4[...]

    @pl.when(row_index == 1)
    def _():
        out[LOW, :] = low1[TOP, :]
        out[TOP, :] = block5[...]

    @pl.when(row_index == 2)
    def _():
        out[LOW, :] = low2[...]
        out[TOP, :] = top2[...]

    @pl.when(row_index == 3)
    def _():
        out[...] = last[...]


def halves():
    core = lax.axis_index("col") % 2
    own = pl.ds(pl.multiple_of(core * HALF, HALF), HALF)
    other = pl.ds(pl.multiple_of((1 - core) * HALF, HALF), HALF)
    return own, other


def stacked(ref, j):
    return jnp.concatenate([ref[j * BLOCK : j * BLOCK + HALF, :], ref[j * BLOCK + HALF : (j + 1) * BLOCK, :]], 1)


def join_kernel(*refs):
    out, at = refs[-1], 0
    for ref in refs[:-1]:
        out[at : at + ref.shape[0], :] = ref[...]
        at += ref.shape[0]


def third_kernel(first, second, low2, factor, mine3, theirs3, block2, block3, value):
    @pl.when(lax.axis_index("row") == 2)
    def _():
        own, other = halves()
        pairs = [wide(second[LOW, :]), wide(second[TOP, :])]
        start = low2[...]
        for k in range(2):
            start = start - product(factor[LOW, columns(k)], pairs[k])
        block2[...] = product(factor[LOW, columns(2)], wide(start))
        pairs.append(wide(block2[...]))
        for rows, ref in ((own, mine3), (other, theirs3)):
            start = first[rows, :]
            for k in range(3):
                start = start - product(stacked(ref, k), pairs[k])
            value[rows, :] = start
        pair = wide(value[...])
        block3[own, :] = product(stacked(mine3, 3), pair)
        block3[other, :] = product(stacked(theirs3, 3), pair)


def fourth_kernel(
    second, block2, block3, top2, value4, value5, top3, factor,
    mine37, theirs37, mine458, theirs458,
    kept, block4, block5, sent, value,
):
    @pl.when(lax.axis_index("row") == 2)
    def _():
        own, other = halves()
        sides = ((own, mine37, mine458), (other, theirs37, theirs458))
        pairs = [wide(x) for x in (second[LOW, :], second[TOP, :], block2[...], block3[...])]
        for rows, _, tiles in sides:
            start = value4[rows, :]
            for k in range(1, 4):
                start = start - product(stacked(tiles, k - 1), pairs[k])
            value[rows, :] = start
        pair = wide(value[...])
        for rows, _, tiles in sides:
            block4[rows, :] = product(stacked(tiles, 3), pair)
        pairs.append(wide(block4[...]))
        for rows, _, tiles in sides:
            start = value5[rows, :]
            for k in range(2, 5):
                start = start - product(stacked(tiles, 4 + k - 2), pairs[k])
            value[rows, :] = start
        pair = wide(value[...])
        for rows, _, tiles in sides:
            block5[rows, :] = product(stacked(tiles, 7), pair)
        pairs.append(wide(block5[...]))
        start = top2[...]
        for k in range(6):
            start = start - product(factor[TOP, columns(k)], pairs[k])
        kept[...] = start
        sent[LOW, :] = block3[...]
        for rows, sevens, tiles in sides:
            start = top3[rows, :]
            for k in range(6):
                tile = stacked(sevens, 4 + k) if k < 4 else stacked(tiles, 8 + k - 4)
                start = start - product(tile, pairs[k])
            value[rows, :] = start
        sent[TOP, :] = value[...]


def line4(right_side, prev_factor, prev_solution, window_factor):
    def move(x, *pairs):
        return lax.ppermute(x, "row", list(pairs))

    def swap(x):
        return lax.ppermute(x, "col", [(0, 1), (1, 0), (2, 3), (3, 2)])

    def cross(x):
        return lax.ppermute(x, "col", [(0, 2), (2, 0), (1, 3), (3, 1)])

    def edges(x):
        return move(x, (0, 1), (1, 0), (2, 3), (3, 2))

    def middle(x):
        return move(x, (1, 2), (2, 1))

    size, rows, tall = (BLOCK, WIDTH), (2 * BLOCK, WIDTH), prev_solution.shape
    dma = pltpu.SemaphoreType.DMA

    edge1 = edges(prev_solution)
    send3, send4 = call(tile_kernel, [tall, tall], [dma((16,))], pltpu.HBM)(window_factor)
    middle3 = middle(after(prev_solution, send3))
    (carried,) = call(inject_kernel, [tall], aliases={0: 0})(middle3, send3, send4)
    edge2 = edges(carried)
    middle2 = middle(edge1)
    past, factor, side, send5, send7, send8 = call(
        load_kernel,
        [prev_factor.shape, window_factor.shape, rows, tall, tall, rows],
        [dma((23,))],
        pltpu.HBM,
    )(after(prev_factor, carried, edge1), window_factor, right_side)
    (carried,) = call(inject_seven_kernel, [tall], aliases={0: 0})(middle2, send7)
    middle2 = carried
    edge3 = edges(carried)
    (mine37,) = call(join_kernel, [(2 * tall[0], WIDTH)])(edge2, edge3)
    own4 = move(edge2, (1, 2))
    own5 = move(send5, (1, 2))
    own8 = move(send8, (3, 2))

    (early,) = call(early_kernel, [(3, *rows)])(past, prev_solution, edge1, edge2, middle2)
    away, keep = call(late_kernel, [(2, *rows)] * 2)(past, early, edge3, middle3)
    one, other_low, other_top = call(sum_kernel, [rows, size, size])(after(keep, own5), swap(away))
    two_low, two_top = cross(other_low), cross(other_top)
    (low,) = call(first_kernel, [size])(side, one, two_low, factor)
    first = move(low, (0, 1), (3, 2))
    (top,) = call(top_kernel, [size])(side, one, two_top, factor, low)
    value4 = move(top, (0, 2))
    top3 = move(top, (3, 2))
    (low1,) = call(second_kernel, [rows])(first, after(low, own4, own8), factor)
    second = move(low1, (1, 2))
    (top1,) = call(five_kernel, [size])(low1, top, factor)
    value5 = move(top1, (1, 2))
    theirs37 = swap(after(mine37, one))
    (mine458,) = call(join_kernel, [(2 * tall[0] + rows[0], WIDTH)])(own4, own5, own8)
    theirs458 = swap(after(mine458, low1))
    block2, block3 = call(third_kernel, [size, size], [pltpu.VMEM(size, jnp.float32)])(
        first, second, low, factor, mine37, theirs37
    )
    kept, block4, block5, sent = call(
        fourth_kernel, [size, size, size, rows], [pltpu.VMEM(size, jnp.float32)]
    )(
        second, block2, block3, top, value4, value5, top3, factor,
        mine37, theirs37, mine458, theirs458,
    )
    last = move(sent, (2, 3))
    block5 = move(block5, (2, 1))
    block4 = move(block4, (2, 0))
    return call(last_kernel, [rows], inside=False)(low, low1, block2, kept, last, block4, block5)[0]


def body(right_side, prev_factor, prev_solution, window_factor):
    blocks = window_factor.shape[1] // STEPS
    slots = right_side.shape[0] // blocks
    if lax.axis_size("row") == 4 and lax.axis_size("col") == 4 and slots == 2:
        return line4(right_side, prev_factor, prev_solution, window_factor)
    return general(right_side, prev_factor, prev_solution, window_factor)


def solution(mesh):
    in_specs = (
        P(("groups", "row"), None),
        P(("groups", "row"), "col"),
        P(("groups", "col"), "row"),
        P(("groups", "row"), None),
    )
    out_specs = P(("groups", "row"), "col")
    return jax.shard_map(body, mesh=mesh, in_specs=in_specs, out_specs=out_specs, check_vma=False)
```

time: 95.9 us -> 91.5 us (0.954)
  starting transfers between devices: 43.8 us -> 39.2 us
  waiting for transfers between devices: 41.7 us -> 43 us
  local copies, waits for them, and re-layouts: 1.07 us -> 0.04 us
    ppermute x12 -> x0, starting transfers between devices: 26.8 us -> none  [the longest x6 19.1 us: gather_row(): lax.ppermute(c, 'row', [(i, i + 1) for i in range(first, 3)])]
    ppermute x11 -> x16, starting transfers between devices: 13.6 us -> 35.4 us  [move(): return lax.ppermute(x, 'row', list(pairs))]
    ppermute x11 -> x16, waiting for transfers between devices: 22.8 us -> 34.5 us  [move(): return lax.ppermute(x, 'row', list(pairs))]
    ppermute x12 -> x0, waiting for transfers between devices: 11.3 us -> none  [the longest x6 11.3 us: gather_row(): lax.ppermute(c, 'row', [(i + 1, i) for i in range(0, last)])]
    ppermute x2, waiting for transfers between devices: 6.06 us -> 7.98 us  [cross(): return lax.ppermute(x, 'col', [(0, 2), (2, 0), (1, 3), (3, 1)])]
    slice x1 -> x0, local copies, waits for them, and re-layouts: 1.06 us -> none  [gather_row(): up = down = [piece[i * rows:(i + 1) * rows] for i in range(chunks)]]
    ppermute x7 -> x3, waiting for transfers between devices: 1.56 us -> 0.5 us  [swap(): return lax.ppermute(x, 'col', [(0, 1), (1, 0), (2, 3), (3, 2)])]
    ppermute x2, starting transfers between devices: 2.09 us -> 3.11 us  [cross(): return lax.ppermute(x, 'col', [(0, 2), (2, 0), (1, 3), (3, 1)])]
  transfers between devices with their start and end apart: 32 -> 21, of which waited for: 12 -> 8; matrix products, arithmetic and copies ran while one was open for 0% -> 0% of each run, Pallas kernels for 8% -> 9%
where the time goes in v4:
time: 91.5 us; the launch traced here: 91.1 us
  waiting for transfers between devices  43 us (47%)
  starting transfers between devices  39.2 us (43%)
  Pallas kernels  8.65 us (9%)
    ppermute x16, starting transfers between devices, move(): return lax.ppermute(x, 'row', list(pairs))  35.4 us
    ppermute x16, waiting for transfers between devices, move(): return lax.ppermute(x, 'row', list(pairs))  34.5 us
    pallas_call x16, Pallas kernels, run(): pl.pallas_call(kernel, out_shape=[(pltpu.VMEM if inside else jax.ShapeDty...  8.65 us
    ppermute x2, waiting for transfers between devices, cross(): return lax.ppermute(x, 'col', [(0, 2), (2, 0), (1, 3), (3, 1)])  7.98 us
    ppermute x2, starting transfers between devices, cross(): return lax.ppermute(x, 'col', [(0, 2), (2, 0), (1, 3), (3, 1)])  3.11 us
  transfers between devices with their start and end apart: 21, of which 8 were waited for; matrix products, arithmetic and copies ran while one was open for 0% of the time, Pallas kernels for 9%

profile of v4, /device:TPU:0, one launch (start us, length us, event | category | flops | bytes accessed | tf_op | source)
XLA Modules:
  0.0 91.1 jit_solution(17028038081335723779)
XLA Ops:
  0.0 3.0 %collective-permute-start.1 = (f32[1024,128]{1,0:T(8,128)}, f32[1024,128]{1,0:T(8,128)S(1)}, u32[]{:S(2)}, u32[]{:S(2)}) collective-permute-start(f32[1024,128]{1,0:T(8,128)} %own.1), channel_id=1, source_target_pairs={{0,4},{4,0},{8,12},{12,8},{1,5},{5,1},{9,13},{13,9},{2,6},{6,2},{1... | collective-permute-start | bytes 1572872 | tf_op jit(solution)/shard_map/ppermute | solution.py:321
  3.0 1.4 %shard_map.46 = (f32[1024,128]{1,0:T(8,128)S(1)}, f32[1024,128]{1,0:T(8,128)S(1)}) custom-call(f32[512,1536]{1,0:T(8,128)} %factor.3), custom_call_target="tpu_custom_call" | custom-call | tf_op jit(solution)/shard_map/pallas_call | solution.py:76
  4.4 0.7 collective-permute-start
  5.1 10.1 %collective-permute-done.1.edge1 = f32[1024,128]{1,0:T(8,128)S(1)} collective-permute-done((f32[1024,128]{1,0:T(8,128)}, f32[1024,128]{1,0:T(8,128)S(1)}, u32[]{:S(2)}, u32[]{:S(2)}) %collective-permute-start.1) | collective-permute-done | bytes 524320 | tf_op jit(solution)/shard_map/ppermute | solution.py:321
  15.2 0.7 collective-permute-start.3
  16.0 5.9 %collective-permute-start.2 = (f32[1024,128]{1,0:T(8,128)S(1)}, f32[1024,128]{1,0:T(8,128)S(1)}, u32[]{:S(2)}, u32[]{:S(2)}) collective-permute-start(f32[1024,128]{1,0:T(8,128)S(1)} %shard_map.47), channel_id=1, source_target_pairs={{0,4},{4,0},{8,12},{12,8},{1,5},{5,1},{9,13},{13,9},{2,6},{6,2},{1... | collective-permute-start | bytes 1572872 | tf_op jit(solution)/shard_map/ppermute | solution.py:321
  22.0 3.2 %shard_map.48 = (f32[512,1024]{1,0:T(8,128)S(1)}, f32[512,1536]{1,0:T(8,128)S(1)}, f32[512,128]{1,0:T(8,128)S(1)}, f32[1024,128]{1,0:T(8,128)S(1)}, f32[1024,128]{1,0:T(8,128)S(1)}, /*index=5*/f32[512,128]{1,0:T(8,128)S(1)}) custom-call(f32[512,1024]{1,0:T(8,128)} %past, f32[512,1536]{1,0:T(8,128)} %factor.3, f32[512,512]{1,0:T(8,128)} %side.1), custom_call_target="tpu_custom_call" | custom-call | tf_op jit(solution)/shard_map/pallas_call | solution.py:76
  25.2 7.2 %collective-permute-start.4 = (f32[1024,128]{1,0:T(8,128)S(1)}, f32[1024,128]{1,0:T(8,128)S(1)}, u32[]{:S(2)}, u32[]{:S(2)}) collective-permute-start(f32[1024,128]{1,0:T(8,128)S(1)} %shard_map.49.middle2), channel_id=1, source_target_pairs={{0,4},{4,0},{8,12},{12,8},{1,5},{5,1},{9,13},{13,9},{2,6},{6,2},{1... | collective-permute-start | bytes 1572872 | tf_op jit(solution)/shard_map/ppermute | solution.py:321
  32.4 0.7 collective-permute-start.5
  33.1 1.8 %shard_map.50.early = f32[3,512,128]{2,1,0:T(8,128)S(1)} custom-call(f32[512,1024]{1,0:T(8,128)S(1)} %get-tuple-element.35.past, f32[1024,128]{1,0:T(8,128)S(1)} %copy-done, f32[1024,128]{1,0:T(8,128)S(1)} %collective-permute-done.1.edge1, f32[1024,128]{1,0:T(8,128)S(1)} %collective-permute-done.2.edge2.refs_0_, f32[1024,128]{1,0:T(8,128)S(1)} %shard_map.49.middle2), custom_call_target="tpu_custom_call" | custom-call | tf_op jit(solution)/shard_map/pallas_call | solution.py:76
  34.9 8.7 %collective-permute-done.4.edge3.refs_1_ = f32[1024,128]{1,0:T(8,128)S(1)} collective-permute-done((f32[1024,128]{1,0:T(8,128)S(1)}, f32[1024,128]{1,0:T(8,128)S(1)}, u32[]{:S(2)}, u32[]{:S(2)}) %collective-permute-start.4) | collective-permute-done | bytes 524320 | tf_op jit(solution)/shard_map/ppermute | solution.py:321
  43.5 0.7 shard_map.51
  44.4 0.7 collective-permute-start.9
  46.3 1.6 %collective-permute-start.7 = (f32[256,128]{1,0:T(8,128)S(1)}, f32[256,128]{1,0:T(8,128)S(1)}, u32[]{:S(2)}, u32[]{:S(2)}) collective-permute-start(f32[256,128]{1,0:T(8,128)S(1)} %get-tuple-element.42), channel_id=1, source_target_pairs={{0,2},{2,0},{1,3},{3,1},{4,6},{6,4},{5,7},{7,5},{8,10},{10,8},{9,1... | collective-permute-start | bytes 393224 | tf_op jit(solution)/shard_map/ppermute | solution.py:327
  47.9 4.0 %collective-permute-done.7.two = f32[256,128]{1,0:T(8,128)S(1)} collective-permute-done((f32[256,128]{1,0:T(8,128)S(1)}, f32[256,128]{1,0:T(8,128)S(1)}, u32[]{:S(2)}, u32[]{:S(2)}) %collective-permute-start.7) | collective-permute-done | bytes 131104 | tf_op jit(solution)/shard_map/ppermute | solution.py:327
  52.2 5.9 %collective-permute-start.8 = (f32[256,128]{1,0:T(8,128)S(1)}, f32[256,128]{1,0:T(8,128)S(1)}, u32[]{:S(2)}, u32[]{:S(2)}) collective-permute-start(f32[256,128]{1,0:T(8,128)S(1)} %shard_map.53.low_in.low2.low), channel_id=1, source_target_pairs={{0,4},{12,8},{1,5},{13,9},{2,6},{14,10},{3,7},{15,11},{16,20},{28,... | collective-permute-start | bytes 393224 | tf_op jit(solution)/shard_map/ppermute | solution.py:321
  58.2 2.4 %collective-permute-done.8.solved.first = f32[256,128]{1,0:T(8,128)S(1)} collective-permute-done((f32[256,128]{1,0:T(8,128)S(1)}, f32[256,128]{1,0:T(8,128)S(1)}, u32[]{:S(2)}, u32[]{:S(2)}) %collective-permute-start.8) | collective-permute-done | bytes 131104 | tf_op jit(solution)/shard_map/ppermute | solution.py:321
  61.9 1.6 %collective-permute-start.13 = (f32[256,128]{1,0:T(8,128)S(1)}, f32[256,128]{1,0:T(8,128)S(1)}, u32[]{:S(2)}, u32[]{:S(2)}) collective-permute-start(f32[256,128]{1,0:T(8,128)S(1)} %get-tuple-element.49), channel_id=1, source_target_pairs={{0,2},{2,0},{1,3},{3,1},{4,6},{6,4},{5,7},{7,5},{8,10},{10,8},{9,1... | collective-permute-start | bytes 393224 | tf_op jit(solution)/shard_map/ppermute | solution.py:327
  63.4 3.9 %collective-permute-done.13.two = f32[256,128]{1,0:T(8,128)S(1)} collective-permute-done((f32[256,128]{1,0:T(8,128)S(1)}, f32[256,128]{1,0:T(8,128)S(1)}, u32[]{:S(2)}, u32[]{:S(2)}) %collective-permute-start.13) | collective-permute-done | bytes 131104 | tf_op jit(solution)/shard_map/ppermute | solution.py:327
  67.6 5.3 %collective-permute-start.14 = (f32[256,128]{1,0:T(8,128)S(1)}, f32[256,128]{1,0:T(8,128)S(1)}, u32[]{:S(2)}, u32[]{:S(2)}) collective-permute-start(f32[256,128]{1,0:T(8,128)S(1)} %shard_map.57.top_in.top2), channel_id=1, source_target_pairs={{0,8},{1,9},{2,10},{3,11},{16,24},{17,25},{18,26},{19,27}} | collective-permute-start | bytes 393224 | tf_op jit(solution)/shard_map/ppermute | solution.py:321
  74.4 1.1 %collective-permute-done.14.value4 = f32[256,128]{1,0:T(8,128)S(1)} collective-permute-done((f32[256,128]{1,0:T(8,128)S(1)}, f32[256,128]{1,0:T(8,128)S(1)}, u32[]{:S(2)}, u32[]{:S(2)}) %collective-permute-start.14) | collective-permute-done | bytes 131104 | tf_op jit(solution)/shard_map/ppermute | solution.py:321
  76.2 1.3 %collective-permute-start.19 = (f32[256,128]{1,0:T(8,128)S(1)}, f32[256,128]{1,0:T(8,128)S(1)}, u32[]{:S(2)}, u32[]{:S(2)}) collective-permute-start(f32[256,128]{1,0:T(8,128)S(1)} %get-tuple-element.53), channel_id=1, source_target_pairs={{8,0},{9,1},{10,2},{11,3},{24,16},{25,17},{26,18},{27,19}} | collective-permute-start | bytes 393224 | tf_op jit(solution)/shard_map/ppermute | solution.py:321
  78.1 12.2 %collective-permute-done.19.block4 = f32[256,128]{1,0:T(8,128)S(1)} collective-permute-done((f32[256,128]{1,0:T(8,128)S(1)}, f32[256,128]{1,0:T(8,128)S(1)}, u32[]{:S(2)}, u32[]{:S(2)}) %collective-permute-start.19) | collective-permute-done | bytes 131104 | tf_op jit(solution)/shard_map/ppermute | solution.py:321
  90.4 0.7 shard_map.61
  (37 shorter events, 6.1 us)
Async XLA Ops:
  0.0 4.4 %copy-start = (f32[1024,128]{1,0:T(8,128)S(1)}, f32[1024,128]{1,0:T(8,128)}, u32[]{:S(2)}) copy-start(f32[1024,128]{1,0:T(8,128)} %own.1) | copy-start | bytes 1572868
  0.0 15.2 %collective-permute-start.1 = (f32[1024,128]{1,0:T(8,128)}, f32[1024,128]{1,0:T(8,128)S(1)}, u32[]{:S(2)}, u32[]{:S(2)}) collective-permute-start(f32[1024,128]{1,0:T(8,128)} %own.1), channel_id=1, source_target_pairs={{0,4},{4,0},{8,12},{12,8},{1,5},{5,1},{9,13},{13,9},{2,6},{6,2},{1... | collective-permute-start | bytes 1572872 | tf_op jit(solution)/shard_map/ppermute | solution.py:321
  4.4 11.5 %collective-permute-start = (f32[1024,128]{1,0:T(8,128)S(1)}, f32[1024,128]{1,0:T(8,128)S(1)}, u32[]{:S(2)}, u32[]{:S(2)}) collective-permute-start(f32[1024,128]{1,0:T(8,128)S(1)} %copy-done), channel_id=1, source_target_pairs={{4,8},{8,4},{5,9},{9,5},{6,10},{10,6},{7,11},{11,7},{20,24},{24,20... | collective-permute-start | bytes 1572872 | tf_op jit(solution)/shard_map/ppermute | solution.py:321
  15.2 9.9 %collective-permute-start.3 = (f32[1024,128]{1,0:T(8,128)S(1)}, f32[1024,128]{1,0:T(8,128)S(1)}, u32[]{:S(2)}, u32[]{:S(2)}) collective-permute-start(f32[1024,128]{1,0:T(8,128)S(1)} %collective-permute-done.1.edge1), channel_id=1, source_target_pairs={{4,8},{8,4},{5,9},{9,5},{6,10},{10,6},{7,11},{11,7},{20,24},{24,20... | collective-permute-start | bytes 1572872 | tf_op jit(solution)/shard_map/ppermute | solution.py:321
  16.0 17.0 %collective-permute-start.2 = (f32[1024,128]{1,0:T(8,128)S(1)}, f32[1024,128]{1,0:T(8,128)S(1)}, u32[]{:S(2)}, u32[]{:S(2)}) collective-permute-start(f32[1024,128]{1,0:T(8,128)S(1)} %shard_map.47), channel_id=1, source_target_pairs={{0,4},{4,0},{8,12},{12,8},{1,5},{5,1},{9,13},{13,9},{2,6},{6,2},{1... | collective-permute-start | bytes 1572872 | tf_op jit(solution)/shard_map/ppermute | solution.py:321
  25.2 18.4 %collective-permute-start.4 = (f32[1024,128]{1,0:T(8,128)S(1)}, f32[1024,128]{1,0:T(8,128)S(1)}, u32[]{:S(2)}, u32[]{:S(2)}) collective-permute-start(f32[1024,128]{1,0:T(8,128)S(1)} %shard_map.49.middle2), channel_id=1, source_target_pairs={{0,4},{4,0},{8,12},{12,8},{1,5},{5,1},{9,13},{13,9},{2,6},{6,2},{1... | collective-permute-start | bytes 1572872 | tf_op jit(solution)/shard_map/ppermute | solution.py:321
  32.4 13.4 %collective-permute-start.5 = (f32[1024,128]{1,0:T(8,128)S(1)}, f32[1024,128]{1,0:T(8,128)S(1)}, u32[]{:S(2)}, u32[]{:S(2)}) collective-permute-start(f32[1024,128]{1,0:T(8,128)S(1)} %get-tuple-element.38), channel_id=1, source_target_pairs={{4,8},{5,9},{6,10},{7,11},{20,24},{21,25},{22,26},{23,27}} | collective-permute-start | bytes 1572872 | tf_op jit(solution)/shard_map/ppermute | solution.py:321
  44.3 2.0 %collective-permute-start.6 = (f32[2,512,128]{2,1,0:T(8,128)S(1)}, f32[2,512,128]{2,1,0:T(8,128)S(1)}, u32[]{:S(2)}, u32[]{:S(2)}) collective-permute-start(f32[2,512,128]{2,1,0:T(8,128)S(1)} %get-tuple-element.40), channel_id=1, source_target_pairs={{0,1},{1,0},{2,3},{3,2},{4,5},{5,4},{6,7},{7,6},{8,9},{9,8},{10,11... | collective-permute-start | bytes 1572872 | tf_op jit(solution)/shard_map/ppermute | solution.py:324
  44.4 13.7 %collective-permute-start.9 = (f32[1024,128]{1,0:T(8,128)S(1)}, f32[1024,128]{1,0:T(8,128)S(1)}, u32[]{:S(2)}, u32[]{:S(2)}) collective-permute-start(f32[1024,128]{1,0:T(8,128)S(1)} %collective-permute-done.2.edge2.refs_0_), channel_id=1, source_target_pairs={{4,8},{5,9},{6,10},{7,11},{20,24},{21,25},{22,26},{23,27}} | collective-permute-start | bytes 1572872 | tf_op jit(solution)/shard_map/ppermute | solution.py:321
  45.1 13.0 %collective-permute-start.10 = (f32[512,128]{1,0:T(8,128)S(1)}, f32[512,128]{1,0:T(8,128)S(1)}, u32[]{:S(2)}, u32[]{:S(2)}) collective-permute-start(f32[512,128]{1,0:T(8,128)S(1)} %get-tuple-element.44), channel_id=1, source_target_pairs={{12,8},{13,9},{14,10},{15,11},{28,24},{29,25},{30,26},{31,27}} | collective-permute-start | bytes 786440 | tf_op jit(solution)/shard_map/ppermute | solution.py:321
  46.3 5.6 %collective-permute-start.7 = (f32[256,128]{1,0:T(8,128)S(1)}, f32[256,128]{1,0:T(8,128)S(1)}, u32[]{:S(2)}, u32[]{:S(2)}) collective-permute-start(f32[256,128]{1,0:T(8,128)S(1)} %get-tuple-element.42), channel_id=1, source_target_pairs={{0,2},{2,0},{1,3},{3,1},{4,6},{6,4},{5,7},{7,5},{8,10},{10,8},{9,1... | collective-permute-start | bytes 393224 | tf_op jit(solution)/shard_map/ppermute | solution.py:327
  52.2 8.4 %collective-permute-start.8 = (f32[256,128]{1,0:T(8,128)S(1)}, f32[256,128]{1,0:T(8,128)S(1)}, u32[]{:S(2)}, u32[]{:S(2)}) collective-permute-start(f32[256,128]{1,0:T(8,128)S(1)} %shard_map.53.low_in.low2.low), channel_id=1, source_target_pairs={{0,4},{12,8},{1,5},{13,9},{2,6},{14,10},{3,7},{15,11},{16,20},{28,... | collective-permute-start | bytes 393224 | tf_op jit(solution)/shard_map/ppermute | solution.py:321
  60.6 14.9 %collective-permute-start.17 = (f32[2560,128]{1,0:T(8,128)S(1)}, f32[2560,128]{1,0:T(8,128)S(1)}, u32[]{:S(2)}, u32[]{:S(2)}) collective-permute-start(f32[2560,128]{1,0:T(8,128)S(1)} %shard_map.59.mine458), channel_id=1, source_target_pairs={{0,1},{1,0},{2,3},{3,2},{4,5},{5,4},{6,7},{7,6},{8,9},{9,8},{10,11... | collective-permute-start | bytes 3932168 | tf_op jit(solution)/shard_map/ppermute | solution.py:324
  60.6 13.7 %collective-permute-start.12 = (f32[2048,128]{1,0:T(8,128)S(1)}, f32[2048,128]{1,0:T(8,128)S(1)}, u32[]{:S(2)}, u32[]{:S(2)}) collective-permute-start(f32[2048,128]{1,0:T(8,128)S(1)} %shard_map.55.mine3.mine37), channel_id=1, source_target_pairs={{0,1},{1,0},{2,3},{3,2},{4,5},{5,4},{6,7},{7,6},{8,9},{9,8},{10,11... | collective-permute-start | bytes 3145736 | tf_op jit(solution)/shard_map/ppermute | solution.py:324
  61.2 12.4 %collective-permute-start.11 = (f32[512,128]{1,0:T(8,128)S(1)}, f32[512,128]{1,0:T(8,128)S(1)}, u32[]{:S(2)}, u32[]{:S(2)}) collective-permute-start(f32[512,128]{1,0:T(8,128)S(1)} %shard_map.54.solved.low1), channel_id=1, source_target_pairs={{4,8},{5,9},{6,10},{7,11},{20,24},{21,25},{22,26},{23,27}} | collective-permute-start | bytes 786440 | tf_op jit(solution)/shard_map/ppermute | solution.py:321
  61.9 5.5 %collective-permute-start.13 = (f32[256,128]{1,0:T(8,128)S(1)}, f32[256,128]{1,0:T(8,128)S(1)}, u32[]{:S(2)}, u32[]{:S(2)}) collective-permute-start(f32[256,128]{1,0:T(8,128)S(1)} %get-tuple-element.49), channel_id=1, source_target_pairs={{0,2},{2,0},{1,3},{3,1},{4,6},{6,4},{5,7},{7,5},{8,10},{10,8},{9,1... | collective-permute-start | bytes 393224 | tf_op jit(solution)/shard_map/ppermute | solution.py:327
  67.6 7.8 %collective-permute-start.14 = (f32[256,128]{1,0:T(8,128)S(1)}, f32[256,128]{1,0:T(8,128)S(1)}, u32[]{:S(2)}, u32[]{:S(2)}) collective-permute-start(f32[256,128]{1,0:T(8,128)S(1)} %shard_map.57.top_in.top2), channel_id=1, source_target_pairs={{0,8},{1,9},{2,10},{3,11},{16,24},{17,25},{18,26},{19,27}} | collective-permute-start | bytes 393224 | tf_op jit(solution)/shard_map/ppermute | solution.py:321
  72.9 2.5 %collective-permute-start.16 = (f32[256,128]{1,0:T(8,128)S(1)}, f32[256,128]{1,0:T(8,128)S(1)}, u32[]{:S(2)}, u32[]{:S(2)}) collective-permute-start(f32[256,128]{1,0:T(8,128)S(1)} %shard_map.57.top_in.top2), channel_id=1, source_target_pairs={{12,8},{13,9},{14,10},{15,11},{28,24},{29,25},{30,26},{31,27}} | collective-permute-start | bytes 393224 | tf_op jit(solution)/shard_map/ppermute | solution.py:321
  73.6 1.8 %collective-permute-start.15 = (f32[256,128]{1,0:T(8,128)S(1)}, f32[256,128]{1,0:T(8,128)S(1)}, u32[]{:S(2)}, u32[]{:S(2)}) collective-permute-start(f32[256,128]{1,0:T(8,128)S(1)} %shard_map.58), channel_id=1, source_target_pairs={{4,8},{5,9},{6,10},{7,11},{20,24},{21,25},{22,26},{23,27}} | collective-permute-start | bytes 393224 | tf_op jit(solution)/shard_map/ppermute | solution.py:321
  75.5 14.9 %collective-permute-start.18 = (f32[512,128]{1,0:T(8,128)S(1)}, f32[512,128]{1,0:T(8,128)S(1)}, u32[]{:S(2)}, u32[]{:S(2)}) collective-permute-start(f32[512,128]{1,0:T(8,128)S(1)} %get-tuple-element.52), channel_id=1, source_target_pairs={{8,12},{9,13},{10,14},{11,15},{24,28},{25,29},{26,30},{27,31}} | collective-permute-start | bytes 786440 | tf_op jit(solution)/shard_map/ppermute | solution.py:321
  76.2 14.2 %collective-permute-start.19 = (f32[256,128]{1,0:T(8,128)S(1)}, f32[256,128]{1,0:T(8,128)S(1)}, u32[]{:S(2)}, u32[]{:S(2)}) collective-permute-start(f32[256,128]{1,0:T(8,128)S(1)} %get-tuple-element.53), channel_id=1, source_target_pairs={{8,0},{9,1},{10,2},{11,3},{24,16},{25,17},{26,18},{27,19}} | collective-permute-start | bytes 393224 | tf_op jit(solution)/shard_map/ppermute | solution.py:321
  77.5 12.9 %collective-permute-start.20 = (f32[256,128]{1,0:T(8,128)S(1)}, f32[256,128]{1,0:T(8,128)S(1)}, u32[]{:S(2)}, u32[]{:S(2)}) collective-permute-start(f32[256,128]{1,0:T(8,128)S(1)} %get-tuple-element.54), channel_id=1, source_target_pairs={{8,4},{9,5},{10,6},{11,7},{24,20},{25,21},{26,22},{27,23}} | collective-permute-start | bytes 393224 | tf_op jit(solution)/shard_map/ppermute | solution.py:321

commit v5 on v4

--- a/solution.py
+++ b/solution.py
@@ -73,15 +73,16 @@
 
 def call(kernel, shapes, scratch=(), space=pltpu.VMEM, inside=True, aliases={}):
     def run(*args):
+        spaces = space if isinstance(space, list) else [space] * len(args)
         return pl.pallas_call(
             kernel,
             out_shape=[(pltpu.VMEM if inside else jax.ShapeDtypeStruct)(s, jnp.float32) for s in shapes],
-            in_specs=[pl.BlockSpec(memory_space=space)] * len(args),
+            in_specs=[pl.BlockSpec(memory_space=m) for m in spaces],
             out_specs=[VMEM_SPEC] * len(shapes),
             scratch_shapes=list(scratch),
             input_output_aliases=aliases,
             compiler_params=pltpu.CompilerParams(vmem_limit_bytes=32 * 1024 * 1024),
-        )(*[pltpu.with_memory_space_constraint(a, space) for a in args])
+        )(*[pltpu.with_memory_space_constraint(a, m) for a, m in zip(args, spaces)])
 
     return run
 
@@ -107,19 +108,16 @@
     ]
 
 
-def tile_kernel(factor, three, four, sem):
+def inject_kernel(x_in, factor, x, sem):
     low, top = sent_rows()
-    copy_all(stack_copies(factor, low, 0, three) + stack_copies(factor, top, BLOCK, four), sem)
-
-
-def inject_kernel(x_in, three, four, x):
+
     @pl.when(lax.axis_index("row") == 0)
     def _():
-        x[...] = four[...]
+        copy_all(stack_copies(factor, top, BLOCK, x), sem)
 
     @pl.when(lax.axis_index("row") == 3)
     def _():
-        x[...] = three[...]
+        copy_all(stack_copies(factor, low, 0, x), sem)
 
 
 def inject_seven_kernel(x_in, seven, x):
@@ -213,7 +211,7 @@
         top[...] = value - product(factor[TOP, columns(1)], wide(solved[TOP, :]))
 
 
-def last_kernel(low, low1, low2, top2, last, block4, block5, out):
+def last_kernel(low, low1, low2, top2, last3, last7, block4, block5, out):
     row_index = lax.axis_index("row")
 
     @pl.when(row_index == 0)
@@ -233,7 +231,8 @@
 
     @pl.when(row_index == 3)
     def _():
-        out[...] = last[...]
+        out[LOW, :] = last3[...]
+        out[TOP, :] = last7[...]
 
 
 def halves():
@@ -254,7 +253,7 @@
         at += ref.shape[0]
 
 
-def third_kernel(first, second, low2, factor, mine3, theirs3, block2, block3, value):
+def third_kernel(first, second, low2, factor, mine, theirs, block2, block3, value):
     @pl.when(lax.axis_index("row") == 2)
     def _():
         own, other = halves()
@@ -264,56 +263,53 @@
             start = start - product(factor[LOW, columns(k)], pairs[k])
         block2[...] = product(factor[LOW, columns(2)], wide(start))
         pairs.append(wide(block2[...]))
-        for rows, ref in ((own, mine3), (other, theirs3)):
+        for rows, ref in ((own, mine), (other, theirs)):
             start = first[rows, :]
             for k in range(3):
                 start = start - product(stacked(ref, k), pairs[k])
             value[rows, :] = start
         pair = wide(value[...])
-        block3[own, :] = product(stacked(mine3, 3), pair)
-        block3[other, :] = product(stacked(theirs3, 3), pair)
+        block3[own, :] = product(stacked(mine, 3), pair)
+        block3[other, :] = product(stacked(theirs, 3), pair)
 
 
 def fourth_kernel(
     second, block2, block3, top2, value4, value5, top3, factor,
-    mine37, theirs37, mine458, theirs458,
+    mine, theirs,
     kept, block4, block5, sent, value,
 ):
     @pl.when(lax.axis_index("row") == 2)
     def _():
         own, other = halves()
-        sides = ((own, mine37, mine458), (other, theirs37, theirs458))
+        sides = ((own, mine), (other, theirs))
         pairs = [wide(x) for x in (second[LOW, :], second[TOP, :], block2[...], block3[...])]
-        for rows, _, tiles in sides:
+        for rows, tiles in sides:
             start = value4[rows, :]
             for k in range(1, 4):
-                start = start - product(stacked(tiles, k - 1), pairs[k])
+                start = start - product(stacked(tiles, 10 + k - 1), pairs[k])
             value[rows, :] = start
         pair = wide(value[...])
-        for rows, _, tiles in sides:
-            block4[rows, :] = product(stacked(tiles, 3), pair)
+        for rows, tiles in sides:
+            block4[rows, :] = product(stacked(tiles, 13), pair)
         pairs.append(wide(block4[...]))
-        for rows, _, tiles in sides:
+        for rows, tiles in sides:
             start = value5[rows, :]
             for k in range(2, 5):
-                start = start - product(stacked(tiles, 4 + k - 2), pairs[k])
+                start = start - product(stacked(tiles, 14 + k - 2), pairs[k])
             value[rows, :] = start
         pair = wide(value[...])
-        for rows, _, tiles in sides:
-            block5[rows, :] = product(stacked(tiles, 7), pair)
+        for rows, tiles in sides:
+            block5[rows, :] = product(stacked(tiles, 17), pair)
         pairs.append(wide(block5[...]))
         start = top2[...]
         for k in range(6):
             start = start - product(factor[TOP, columns(k)], pairs[k])
         kept[...] = start
-        sent[LOW, :] = block3[...]
-        for rows, sevens, tiles in sides:
+        for rows, tiles in sides:
             start = top3[rows, :]
             for k in range(6):
-                tile = stacked(sevens, 4 + k) if k < 4 else stacked(tiles, 8 + k - 4)
-                start = start - product(tile, pairs[k])
-            value[rows, :] = start
-        sent[TOP, :] = value[...]
+                start = start - product(stacked(tiles, 4 + k), pairs[k])
+            sent[rows, :] = start
 
 
 def line4(right_side, prev_factor, prev_solution, window_factor):
@@ -336,9 +332,10 @@
     dma = pltpu.SemaphoreType.DMA
 
     edge1 = edges(prev_solution)
-    send3, send4 = call(tile_kernel, [tall, tall], [dma((16,))], pltpu.HBM)(window_factor)
-    middle3 = middle(after(prev_solution, send3))
-    (carried,) = call(inject_kernel, [tall], aliases={0: 0})(middle3, send3, send4)
+    middle3 = middle(prev_solution)
+    (carried,) = call(inject_kernel, [tall], [dma((8,))], [pltpu.VMEM, pltpu.HBM], aliases={0: 0})(
+        middle3, window_factor
+    )
     edge2 = edges(carried)
     middle2 = middle(edge1)
     past, factor, side, send5, send7, send8 = call(
@@ -350,40 +347,40 @@
     (carried,) = call(inject_seven_kernel, [tall], aliases={0: 0})(middle2, send7)
     middle2 = carried
     edge3 = edges(carried)
-    (mine37,) = call(join_kernel, [(2 * tall[0], WIDTH)])(edge2, edge3)
-    own4 = move(edge2, (1, 2))
-    own5 = move(send5, (1, 2))
-    own8 = move(send8, (3, 2))
 
     (early,) = call(early_kernel, [(3, *rows)])(past, prev_solution, edge1, edge2, middle2)
+    (send45,) = call(join_kernel, [(2 * tall[0], WIDTH)])(after(edge2, early), send5)
+    mine45 = move(send45, (1, 2))
     away, keep = call(late_kernel, [(2, *rows)] * 2)(past, early, edge3, middle3)
-    one, other_low, other_top = call(sum_kernel, [rows, size, size])(after(keep, own5), swap(away))
+    one, other_low, other_top = call(sum_kernel, [rows, size, size])(keep, swap(away))
     two_low, two_top = cross(other_low), cross(other_top)
+    own8 = move(after(send8, one), (3, 2))
     (low,) = call(first_kernel, [size])(side, one, two_low, factor)
     first = move(low, (0, 1), (3, 2))
     (top,) = call(top_kernel, [size])(side, one, two_top, factor, low)
     value4 = move(top, (0, 2))
     top3 = move(top, (3, 2))
-    (low1,) = call(second_kernel, [rows])(first, after(low, own4, own8), factor)
+    (mine,) = call(join_kernel, [(4 * tall[0] + rows[0], WIDTH)])(edge2, edge3, own8, after(mine45, first, top))
+    theirs = swap(mine)
+    (low1,) = call(second_kernel, [rows])(first, after(low, top), factor)
     second = move(low1, (1, 2))
     (top1,) = call(five_kernel, [size])(low1, top, factor)
     value5 = move(top1, (1, 2))
-    theirs37 = swap(after(mine37, one))
-    (mine458,) = call(join_kernel, [(2 * tall[0] + rows[0], WIDTH)])(own4, own5, own8)
-    theirs458 = swap(after(mine458, low1))
     block2, block3 = call(third_kernel, [size, size], [pltpu.VMEM(size, jnp.float32)])(
-        first, second, low, factor, mine37, theirs37
+        first, second, low, factor, mine, theirs
     )
+    last3 = move(block3, (2, 3))
     kept, block4, block5, sent = call(
-        fourth_kernel, [size, size, size, rows], [pltpu.VMEM(size, jnp.float32)]
+        fourth_kernel, [size] * 4, [pltpu.VMEM(size, jnp.float32)]
     )(
-        second, block2, block3, top, value4, value5, top3, factor,
-        mine37, theirs37, mine458, theirs458,
+        second, block2, block3, top, value4, value5, top3, factor, mine, theirs
     )
-    last = move(sent, (2, 3))
+    last7 = move(sent, (2, 3))
     block5 = move(block5, (2, 1))
     block4 = move(block4, (2, 0))
-    return call(last_kernel, [rows], inside=False)(low, low1, block2, kept, last, block4, block5)[0]
+    return call(last_kernel, [rows], inside=False)(
+        low, low1, block2, kept, last3, last7, block4, block5
+    )[0]
 
 
 def body(right_side, prev_factor, prev_solution, window_factor):

time: 91.5 us -> 88.6 us (0.968)
  starting transfers between devices: 39.2 us -> 34.8 us
  waiting for transfers between devices: 43 us -> 44.7 us
    ppermute x16, waiting for transfers between devices: 34.5 us -> 39.3 us  [move(): return lax.ppermute(x, 'row', list(pairs))]
    ppermute x2, waiting for transfers between devices: 7.98 us -> 3.58 us  [cross(): return lax.ppermute(x, 'col', [(0, 2), (2, 0), (1, 3), (3, 1)])]
    ppermute x16, starting transfers between devices: 35.4 us -> 32.5 us  [move(): return lax.ppermute(x, 'row', list(pairs))]
    ppermute x3 -> x2, waiting for transfers between devices: 0.5 us -> 1.9 us  [swap(): return lax.ppermute(x, 'col', [(0, 1), (1, 0), (2, 3), (3, 2)])]
    ppermute x2, starting transfers between devices: 3.11 us -> 2.16 us  [cross(): return lax.ppermute(x, 'col', [(0, 2), (2, 0), (1, 3), (3, 1)])]
    pallas_call x16 -> x15, Pallas kernels: 8.65 us -> 8.42 us  [run(): pl.pallas_call(kernel, out_shape=[(pltpu.VMEM if inside else jax.ShapeDty...]
  transfers between devices with their start and end apart: 21 -> 20, of which waited for: 8 -> 8; matrix products, arithmetic and copies ran while one was open for 0% -> 0% of each run, Pallas kernels for 9% -> 9%
where the time goes in v5:
time: 88.6 us; the launch traced here: 88.3 us
  waiting for transfers between devices  44.7 us (50%)
  starting transfers between devices  34.8 us (39%)
  Pallas kernels  8.42 us (10%)
    ppermute x16, waiting for transfers between devices, move(): return lax.ppermute(x, 'row', list(pairs))  39.3 us
    ppermute x16, starting transfers between devices, move(): return lax.ppermute(x, 'row', list(pairs))  32.5 us
    pallas_call x15, Pallas kernels, run(): pl.pallas_call(kernel, out_shape=[(pltpu.VMEM if inside else jax.ShapeDty...  8.42 us
    ppermute x2, waiting for transfers between devices, cross(): return lax.ppermute(x, 'col', [(0, 2), (2, 0), (1, 3), (3, 1)])  3.58 us
    ppermute x2, starting transfers between devices, cross(): return lax.ppermute(x, 'col', [(0, 2), (2, 0), (1, 3), (3, 1)])  2.16 us
    ppermute x2, waiting for transfers between devices, swap(): return lax.ppermute(x, 'col', [(0, 1), (1, 0), (2, 3), (3, 2)])  1.9 us
  transfers between devices with their start and end apart: 20, of which 8 were waited for; matrix products, arithmetic and copies ran while one was open for 0% of the time, Pallas kernels for 9%

profile of v5, /device:TPU:0, one launch (start us, length us, event | category | flops | bytes accessed | tf_op | source)
XLA Modules:
  0.0 88.3 jit_solution(4688926935866333253)
XLA Ops:
  0.0 3.0 %collective-permute-start.1 = (f32[1024,128]{1,0:T(8,128)}, f32[1024,128]{1,0:T(8,128)S(1)}, u32[]{:S(2)}, u32[]{:S(2)}) collective-permute-start(f32[1024,128]{1,0:T(8,128)} %own.1), channel_id=1, source_target_pairs={{0,4},{4,0},{8,12},{12,8},{1,5},{5,1},{9,13},{13,9},{2,6},{6,2},{1... | collective-permute-start | bytes 1572872 | tf_op jit(solution)/shard_map/ppermute | solution.py:317
  3.0 0.7 collective-permute-start
  3.7 11.4 %collective-permute-done.1.edge1 = f32[1024,128]{1,0:T(8,128)S(1)} collective-permute-done((f32[1024,128]{1,0:T(8,128)}, f32[1024,128]{1,0:T(8,128)S(1)}, u32[]{:S(2)}, u32[]{:S(2)}) %collective-permute-start.1) | collective-permute-done | bytes 524320 | tf_op jit(solution)/shard_map/ppermute | solution.py:317
  15.2 0.7 collective-permute-start.3
  15.9 1.2 %shard_map.46 = f32[1024,128]{1,0:T(8,128)S(1)} custom-call(f32[1024,128]{1,0:T(8,128)S(1)} %copy.7.x_in, f32[512,1536]{1,0:T(8,128)} %factor.3), custom_call_target="tpu_custom_call", output_to_operand_aliasing={{}: (0, {})} | custom-call | tf_op jit(solution)/shard_map/pallas_call | solution.py:77
  17.1 3.6 %collective-permute-start.2 = (f32[1024,128]{1,0:T(8,128)S(1)}, f32[1024,128]{1,0:T(8,128)S(1)}, u32[]{:S(2)}, u32[]{:S(2)}) collective-permute-start(f32[1024,128]{1,0:T(8,128)S(1)} %shard_map.46), channel_id=1, source_target_pairs={{0,4},{4,0},{8,12},{12,8},{1,5},{5,1},{9,13},{13,9},{2,6},{6,2},{1... | collective-permute-start | bytes 1572872 | tf_op jit(solution)/shard_map/ppermute | solution.py:317
  20.6 3.2 %shard_map.47 = (f32[512,1024]{1,0:T(8,128)S(1)}, f32[512,1536]{1,0:T(8,128)S(1)}, f32[512,128]{1,0:T(8,128)S(1)}, f32[1024,128]{1,0:T(8,128)S(1)}, f32[1024,128]{1,0:T(8,128)S(1)}, /*index=5*/f32[512,128]{1,0:T(8,128)S(1)}) custom-call(f32[512,1024]{1,0:T(8,128)} %past, f32[512,1536]{1,0:T(8,128)} %factor.3, f32[512,512]{1,0:T(8,128)} %side.1), custom_call_target="tpu_custom_call" | custom-call | tf_op jit(solution)/shard_map/pallas_call | solution.py:77
  23.8 7.7 %collective-permute-start.4 = (f32[1024,128]{1,0:T(8,128)S(1)}, f32[1024,128]{1,0:T(8,128)S(1)}, u32[]{:S(2)}, u32[]{:S(2)}) collective-permute-start(f32[1024,128]{1,0:T(8,128)S(1)} %shard_map.48.middle2), channel_id=1, source_target_pairs={{0,4},{4,0},{8,12},{12,8},{1,5},{5,1},{9,13},{13,9},{2,6},{6,2},{1... | collective-permute-start | bytes 1572872 | tf_op jit(solution)/shard_map/ppermute | solution.py:317
  31.6 0.7 collective-permute-done.2.edge2.refs_0_
  32.3 1.8 %shard_map.49.early = f32[3,512,128]{2,1,0:T(8,128)S(1)} custom-call(f32[512,1024]{1,0:T(8,128)S(1)} %get-tuple-element.29.past, f32[1024,128]{1,0:T(8,128)S(1)} %copy-done, f32[1024,128]{1,0:T(8,128)S(1)} %collective-permute-done.1.edge1, f32[1024,128]{1,0:T(8,128)S(1)} %collective-permute-done.2.edge2.refs_0_, f32[1024,128]{1,0:T(8,128)S(1)} %shard_map.48.middle2), custom_call_target="tpu_custom_call" | custom-call | tf_op jit(solution)/shard_map/pallas_call | solution.py:77
  34.2 0.7 collective-permute-start.11
  34.9 7.7 %collective-permute-done.4.edge3.refs_1_ = f32[1024,128]{1,0:T(8,128)S(1)} collective-permute-done((f32[1024,128]{1,0:T(8,128)S(1)}, f32[1024,128]{1,0:T(8,128)S(1)}, u32[]{:S(2)}, u32[]{:S(2)}) %collective-permute-start.4) | collective-permute-done | bytes 524320 | tf_op jit(solution)/shard_map/ppermute | solution.py:317
  42.6 0.7 shard_map.50
  43.5 1.9 %collective-permute-done.5.came = f32[2,512,128]{2,1,0:T(8,128)S(1)} collective-permute-done((f32[2,512,128]{2,1,0:T(8,128)S(1)}, f32[2,512,128]{2,1,0:T(8,128)S(1)}, u32[]{:S(2)}, u32[]{:S(2)}) %collective-permute-start.5) | collective-permute-done | bytes 524320 | tf_op jit(solution)/shard_map/ppermute | solution.py:320
  45.4 1.6 %collective-permute-start.6 = (f32[256,128]{1,0:T(8,128)S(1)}, f32[256,128]{1,0:T(8,128)S(1)}, u32[]{:S(2)}, u32[]{:S(2)}) collective-permute-start(f32[256,128]{1,0:T(8,128)S(1)} %get-tuple-element.34), channel_id=1, source_target_pairs={{0,2},{2,0},{1,3},{3,1},{4,6},{6,4},{5,7},{7,5},{8,10},{10,8},{9,1... | collective-permute-start | bytes 393224 | tf_op jit(solution)/shard_map/ppermute | solution.py:323
  48.3 3.6 %collective-permute-done.6.two = f32[256,128]{1,0:T(8,128)S(1)} collective-permute-done((f32[256,128]{1,0:T(8,128)S(1)}, f32[256,128]{1,0:T(8,128)S(1)}, u32[]{:S(2)}, u32[]{:S(2)}) %collective-permute-start.6) | collective-permute-done | bytes 131104 | tf_op jit(solution)/shard_map/ppermute | solution.py:323
  52.1 3.4 %collective-permute-start.7 = (f32[256,128]{1,0:T(8,128)S(1)}, f32[256,128]{1,0:T(8,128)S(1)}, u32[]{:S(2)}, u32[]{:S(2)}) collective-permute-start(f32[256,128]{1,0:T(8,128)S(1)} %shard_map.52.low.low_in.low2), channel_id=1, source_target_pairs={{0,4},{12,8},{1,5},{13,9},{2,6},{14,10},{3,7},{15,11},{16,20},{28,... | collective-permute-start | bytes 393224 | tf_op jit(solution)/shard_map/ppermute | solution.py:317
  55.8 2.2 %collective-permute-done.7.solved.first = f32[256,128]{1,0:T(8,128)S(1)} collective-permute-done((f32[256,128]{1,0:T(8,128)S(1)}, f32[256,128]{1,0:T(8,128)S(1)}, u32[]{:S(2)}, u32[]{:S(2)}) %collective-permute-start.7) | collective-permute-done | bytes 131104 | tf_op jit(solution)/shard_map/ppermute | solution.py:317
  58.3 0.7 collective-permute-start.9
  59.0 6.7 %collective-permute-start.13 = (f32[256,128]{1,0:T(8,128)S(1)}, f32[256,128]{1,0:T(8,128)S(1)}, u32[]{:S(2)}, u32[]{:S(2)}) collective-permute-start(f32[256,128]{1,0:T(8,128)S(1)} %shard_map.53.top_in.top2), channel_id=1, source_target_pairs={{0,8},{1,9},{2,10},{3,11},{16,24},{17,25},{18,26},{19,27}} | collective-permute-start | bytes 393224 | tf_op jit(solution)/shard_map/ppermute | solution.py:317
  67.0 2.0 %collective-permute-done.13.value4 = f32[256,128]{1,0:T(8,128)S(1)} collective-permute-done((f32[256,128]{1,0:T(8,128)S(1)}, f32[256,128]{1,0:T(8,128)S(1)}, u32[]{:S(2)}, u32[]{:S(2)}) %collective-permute-start.13) | collective-permute-done | bytes 131104 | tf_op jit(solution)/shard_map/ppermute | solution.py:317
  69.7 1.3 %collective-permute-start.18 = (f32[256,128]{1,0:T(8,128)S(1)}, f32[256,128]{1,0:T(8,128)S(1)}, u32[]{:S(2)}, u32[]{:S(2)}) collective-permute-start(f32[256,128]{1,0:T(8,128)S(1)} %get-tuple-element.47), channel_id=1, source_target_pairs={{8,0},{9,1},{10,2},{11,3},{24,16},{25,17},{26,18},{27,19}} | collective-permute-start | bytes 393224 | tf_op jit(solution)/shard_map/ppermute | solution.py:317
  72.4 15.2 %collective-permute-done.18.block4 = f32[256,128]{1,0:T(8,128)S(1)} collective-permute-done((f32[256,128]{1,0:T(8,128)S(1)}, f32[256,128]{1,0:T(8,128)S(1)}, u32[]{:S(2)}, u32[]{:S(2)}) %collective-permute-start.18) | collective-permute-done | bytes 131104 | tf_op jit(solution)/shard_map/ppermute | solution.py:317
  87.5 0.7 shard_map.60
  (34 shorter events, 5.7 us)
Async XLA Ops:
  0.0 15.2 %collective-permute-start.1 = (f32[1024,128]{1,0:T(8,128)}, f32[1024,128]{1,0:T(8,128)S(1)}, u32[]{:S(2)}, u32[]{:S(2)}) collective-permute-start(f32[1024,128]{1,0:T(8,128)} %own.1), channel_id=1, source_target_pairs={{0,4},{4,0},{8,12},{12,8},{1,5},{5,1},{9,13},{13,9},{2,6},{6,2},{1... | collective-permute-start | bytes 1572872 | tf_op jit(solution)/shard_map/ppermute | solution.py:317
  3.0 12.8 %collective-permute-start = (f32[1024,128]{1,0:T(8,128)}, f32[1024,128]{1,0:T(8,128)S(1)}, u32[]{:S(2)}, u32[]{:S(2)}) collective-permute-start(f32[1024,128]{1,0:T(8,128)} %own.1), channel_id=1, source_target_pairs={{4,8},{8,4},{5,9},{9,5},{6,10},{10,6},{7,11},{11,7},{20,24},{24,20... | collective-permute-start | bytes 1572872 | tf_op jit(solution)/shard_map/ppermute | solution.py:317
  15.2 8.6 %collective-permute-start.3 = (f32[1024,128]{1,0:T(8,128)S(1)}, f32[1024,128]{1,0:T(8,128)S(1)}, u32[]{:S(2)}, u32[]{:S(2)}) collective-permute-start(f32[1024,128]{1,0:T(8,128)S(1)} %collective-permute-done.1.edge1), channel_id=1, source_target_pairs={{4,8},{8,4},{5,9},{9,5},{6,10},{10,6},{7,11},{11,7},{20,24},{24,20... | collective-permute-start | bytes 1572872 | tf_op jit(solution)/shard_map/ppermute | solution.py:317
  17.1 15.2 %copy-start = (f32[1024,128]{1,0:T(8,128)S(1)}, f32[1024,128]{1,0:T(8,128)}, u32[]{:S(2)}) copy-start(f32[1024,128]{1,0:T(8,128)} %own.1) | copy-start | bytes 1572868
  17.1 15.2 %collective-permute-start.2 = (f32[1024,128]{1,0:T(8,128)S(1)}, f32[1024,128]{1,0:T(8,128)S(1)}, u32[]{:S(2)}, u32[]{:S(2)}) collective-permute-start(f32[1024,128]{1,0:T(8,128)S(1)} %shard_map.46), channel_id=1, source_target_pairs={{0,4},{4,0},{8,12},{12,8},{1,5},{5,1},{9,13},{13,9},{2,6},{6,2},{1... | collective-permute-start | bytes 1572872 | tf_op jit(solution)/shard_map/ppermute | solution.py:317
  23.8 18.8 %collective-permute-start.4 = (f32[1024,128]{1,0:T(8,128)S(1)}, f32[1024,128]{1,0:T(8,128)S(1)}, u32[]{:S(2)}, u32[]{:S(2)}) collective-permute-start(f32[1024,128]{1,0:T(8,128)S(1)} %shard_map.48.middle2), channel_id=1, source_target_pairs={{0,4},{4,0},{8,12},{12,8},{1,5},{5,1},{9,13},{13,9},{2,6},{6,2},{1... | collective-permute-start | bytes 1572872 | tf_op jit(solution)/shard_map/ppermute | solution.py:317
  34.2 21.6 %collective-permute-start.11 = (f32[2048,128]{1,0:T(8,128)S(1)}, f32[2048,128]{1,0:T(8,128)S(1)}, u32[]{:S(2)}, u32[]{:S(2)}) collective-permute-start(f32[2048,128]{1,0:T(8,128)S(1)} %shard_map.55), channel_id=1, source_target_pairs={{4,8},{5,9},{6,10},{7,11},{20,24},{21,25},{22,26},{23,27}} | collective-permute-start | bytes 3145736 | tf_op jit(solution)/shard_map/ppermute | solution.py:317
  43.4 2.0 %collective-permute-start.5 = (f32[2,512,128]{2,1,0:T(8,128)S(1)}, f32[2,512,128]{2,1,0:T(8,128)S(1)}, u32[]{:S(2)}, u32[]{:S(2)}) collective-permute-start(f32[2,512,128]{2,1,0:T(8,128)S(1)} %get-tuple-element.32), channel_id=1, source_target_pairs={{0,1},{1,0},{2,3},{3,2},{4,5},{5,4},{6,7},{7,6},{8,9},{9,8},{10,11... | collective-permute-start | bytes 1572872 | tf_op jit(solution)/shard_map/ppermute | solution.py:320
  45.4 6.4 %collective-permute-start.6 = (f32[256,128]{1,0:T(8,128)S(1)}, f32[256,128]{1,0:T(8,128)S(1)}, u32[]{:S(2)}, u32[]{:S(2)}) collective-permute-start(f32[256,128]{1,0:T(8,128)S(1)} %get-tuple-element.34), channel_id=1, source_target_pairs={{0,2},{2,0},{1,3},{3,1},{4,6},{6,4},{5,7},{7,5},{8,10},{10,8},{9,1... | collective-permute-start | bytes 393224 | tf_op jit(solution)/shard_map/ppermute | solution.py:323
  47.0 11.0 %collective-permute-start.10 = (f32[512,128]{1,0:T(8,128)S(1)}, f32[512,128]{1,0:T(8,128)S(1)}, u32[]{:S(2)}, u32[]{:S(2)}) collective-permute-start(f32[512,128]{1,0:T(8,128)S(1)} %get-tuple-element.39), channel_id=1, source_target_pairs={{12,8},{13,9},{14,10},{15,11},{28,24},{29,25},{30,26},{31,27}} | collective-permute-start | bytes 786440 | tf_op jit(solution)/shard_map/ppermute | solution.py:317
  47.6 7.9 %collective-permute-start.8 = (f32[256,128]{1,0:T(8,128)S(1)}, f32[256,128]{1,0:T(8,128)S(1)}, u32[]{:S(2)}, u32[]{:S(2)}) collective-permute-start(f32[256,128]{1,0:T(8,128)S(1)} %get-tuple-element.36), channel_id=1, source_target_pairs={{0,2},{2,0},{1,3},{3,1},{4,6},{6,4},{5,7},{7,5},{8,10},{10,8},{9,1... | collective-permute-start | bytes 393224 | tf_op jit(solution)/shard_map/ppermute | solution.py:323
  52.1 5.9 %collective-permute-start.7 = (f32[256,128]{1,0:T(8,128)S(1)}, f32[256,128]{1,0:T(8,128)S(1)}, u32[]{:S(2)}, u32[]{:S(2)}) collective-permute-start(f32[256,128]{1,0:T(8,128)S(1)} %shard_map.52.low.low_in.low2), channel_id=1, source_target_pairs={{0,4},{12,8},{1,5},{13,9},{2,6},{14,10},{3,7},{15,11},{16,20},{28,... | collective-permute-start | bytes 393224 | tf_op jit(solution)/shard_map/ppermute | solution.py:317
  58.2 8.8 %collective-permute-start.12 = (f32[4608,128]{1,0:T(8,128)S(1)}, f32[4608,128]{1,0:T(8,128)S(1)}, u32[]{:S(2)}, u32[]{:S(2)}) collective-permute-start(f32[4608,128]{1,0:T(8,128)S(1)} %shard_map.56.mine), channel_id=1, source_target_pairs={{0,1},{1,0},{2,3},{3,2},{4,5},{5,4},{6,7},{7,6},{8,9},{9,8},{10,11... | collective-permute-start | bytes 7077896 | tf_op jit(solution)/shard_map/ppermute | solution.py:320
  58.3 8.7 %collective-permute-start.9 = (f32[512,128]{1,0:T(8,128)S(1)}, f32[512,128]{1,0:T(8,128)S(1)}, u32[]{:S(2)}, u32[]{:S(2)}) collective-permute-start(f32[512,128]{1,0:T(8,128)S(1)} %shard_map.54.solved.low1), channel_id=1, source_target_pairs={{4,8},{5,9},{6,10},{7,11},{20,24},{21,25},{22,26},{23,27}} | collective-permute-start | bytes 786440 | tf_op jit(solution)/shard_map/ppermute | solution.py:317
  59.0 10.1 %collective-permute-start.13 = (f32[256,128]{1,0:T(8,128)S(1)}, f32[256,128]{1,0:T(8,128)S(1)}, u32[]{:S(2)}, u32[]{:S(2)}) collective-permute-start(f32[256,128]{1,0:T(8,128)S(1)} %shard_map.53.top_in.top2), channel_id=1, source_target_pairs={{0,8},{1,9},{2,10},{3,11},{16,24},{17,25},{18,26},{19,27}} | collective-permute-start | bytes 393224 | tf_op jit(solution)/shard_map/ppermute | solution.py:317
  65.6 3.4 %collective-permute-start.15 = (f32[256,128]{1,0:T(8,128)S(1)}, f32[256,128]{1,0:T(8,128)S(1)}, u32[]{:S(2)}, u32[]{:S(2)}) collective-permute-start(f32[256,128]{1,0:T(8,128)S(1)} %shard_map.53.top_in.top2), channel_id=1, source_target_pairs={{12,8},{13,9},{14,10},{15,11},{28,24},{29,25},{30,26},{31,27}} | collective-permute-start | bytes 393224 | tf_op jit(solution)/shard_map/ppermute | solution.py:317
  66.3 2.7 %collective-permute-start.14 = (f32[256,128]{1,0:T(8,128)S(1)}, f32[256,128]{1,0:T(8,128)S(1)}, u32[]{:S(2)}, u32[]{:S(2)}) collective-permute-start(f32[256,128]{1,0:T(8,128)S(1)} %shard_map.58), channel_id=1, source_target_pairs={{4,8},{5,9},{6,10},{7,11},{20,24},{21,25},{22,26},{23,27}} | collective-permute-start | bytes 393224 | tf_op jit(solution)/shard_map/ppermute | solution.py:317
  69.0 3.3 %collective-permute-start.17 = (f32[256,128]{1,0:T(8,128)S(1)}, f32[256,128]{1,0:T(8,128)S(1)}, u32[]{:S(2)}, u32[]{:S(2)}) collective-permute-start(f32[256,128]{1,0:T(8,128)S(1)} %get-tuple-element.46), channel_id=1, source_target_pairs={{8,12},{9,13},{10,14},{11,15},{24,28},{25,29},{26,30},{27,31}} | collective-permute-start | bytes 393224 | tf_op jit(solution)/shard_map/ppermute | solution.py:317
  69.7 17.8 %collective-permute-start.18 = (f32[256,128]{1,0:T(8,128)S(1)}, f32[256,128]{1,0:T(8,128)S(1)}, u32[]{:S(2)}, u32[]{:S(2)}) collective-permute-start(f32[256,128]{1,0:T(8,128)S(1)} %get-tuple-element.47), channel_id=1, source_target_pairs={{8,0},{9,1},{10,2},{11,3},{24,16},{25,17},{26,18},{27,19}} | collective-permute-start | bytes 393224 | tf_op jit(solution)/shard_map/ppermute | solution.py:317
  71.0 16.5 %collective-permute-start.19 = (f32[256,128]{1,0:T(8,128)S(1)}, f32[256,128]{1,0:T(8,128)S(1)}, u32[]{:S(2)}, u32[]{:S(2)}) collective-permute-start(f32[256,128]{1,0:T(8,128)S(1)} %get-tuple-element.48), channel_id=1, source_target_pairs={{8,4},{9,5},{10,6},{11,7},{24,20},{25,21},{26,22},{27,23}} | collective-permute-start | bytes 393224 | tf_op jit(solution)/shard_map/ppermute | solution.py:317
  71.7 15.8 %collective-permute-start.16 = (f32[256,128]{1,0:T(8,128)S(1)}, f32[256,128]{1,0:T(8,128)S(1)}, u32[]{:S(2)}, u32[]{:S(2)}) collective-permute-start(f32[256,128]{1,0:T(8,128)S(1)} %get-tuple-element.44.block3), channel_id=1, source_target_pairs={{8,12},{9,13},{10,14},{11,15},{24,28},{25,29},{26,30},{27,31}} | collective-permute-start | bytes 393224 | tf_op jit(solution)/shard_map/ppermute | solution.py:317

commit v6 on v5

--- a/solution.py
+++ b/solution.py
@@ -253,63 +253,54 @@
         at += ref.shape[0]
 
 
-def third_kernel(first, second, low2, factor, mine, theirs, block2, block3, value):
+def third_kernel(first, second, low2, top2, factor, mine, theirs, block2, block3, change4, change5, change6, change7, value):
     @pl.when(lax.axis_index("row") == 2)
     def _():
         own, other = halves()
+        sides = ((own, mine), (other, theirs))
         pairs = [wide(second[LOW, :]), wide(second[TOP, :])]
         start = low2[...]
         for k in range(2):
             start = start - product(factor[LOW, columns(k)], pairs[k])
         block2[...] = product(factor[LOW, columns(2)], wide(start))
         pairs.append(wide(block2[...]))
-        for rows, ref in ((own, mine), (other, theirs)):
+        for rows, tiles in sides:
             start = first[rows, :]
             for k in range(3):
-                start = start - product(stacked(ref, k), pairs[k])
+                start = start - product(stacked(tiles, k), pairs[k])
             value[rows, :] = start
         pair = wide(value[...])
-        block3[own, :] = product(stacked(mine, 3), pair)
-        block3[other, :] = product(stacked(theirs, 3), pair)
+        for rows, tiles in sides:
+            block3[rows, :] = product(stacked(tiles, 3), pair)
+        pairs.append(wide(block3[...]))
+        for rows, tiles in sides:
+            change4[rows, :] = sum(product(stacked(tiles, 10 + k - 1), pairs[k]) for k in range(1, 4))
+            change5[rows, :] = sum(product(stacked(tiles, 14 + k - 2), pairs[k]) for k in range(2, 4))
+            change7[rows, :] = sum(product(stacked(tiles, 4 + k), pairs[k]) for k in range(4))
+        change6[...] = top2[...] - sum(product(factor[TOP, columns(k)], pairs[k]) for k in range(4))
 
 
 def fourth_kernel(
-    second, block2, block3, top2, value4, value5, top3, factor,
-    mine, theirs,
-    kept, block4, block5, sent, value,
+    value4, value5, top3, change4, change5, value6, change7, factor, mine, theirs, kept, block4, block5, sent
 ):
     @pl.when(lax.axis_index("row") == 2)
     def _():
         own, other = halves()
         sides = ((own, mine), (other, theirs))
-        pairs = [wide(x) for x in (second[LOW, :], second[TOP, :], block2[...], block3[...])]
-        for rows, tiles in sides:
-            start = value4[rows, :]
-            for k in range(1, 4):
-                start = start - product(stacked(tiles, 10 + k - 1), pairs[k])
-            value[rows, :] = start
-        pair = wide(value[...])
+        pair = wide(value4[...] - change4[...])
         for rows, tiles in sides:
             block4[rows, :] = product(stacked(tiles, 13), pair)
-        pairs.append(wide(block4[...]))
-        for rows, tiles in sides:
-            start = value5[rows, :]
-            for k in range(2, 5):
-                start = start - product(stacked(tiles, 14 + k - 2), pairs[k])
-            value[rows, :] = start
-        pair = wide(value[...])
+        four = wide(block4[...])
+        for rows, tiles in sides:
+            sent[rows, :] = value5[rows, :] - change5[rows, :] - product(stacked(tiles, 16), four)
+        pair = wide(sent[...])
         for rows, tiles in sides:
             block5[rows, :] = product(stacked(tiles, 17), pair)
-        pairs.append(wide(block5[...]))
-        start = top2[...]
-        for k in range(6):
-            start = start - product(factor[TOP, columns(k)], pairs[k])
-        kept[...] = start
-        for rows, tiles in sides:
-            start = top3[rows, :]
-            for k in range(6):
-                start = start - product(stacked(tiles, 4 + k), pairs[k])
-            sent[rows, :] = start
+        five = wide(block5[...])
+        kept[...] = value6[...] - product(factor[TOP, columns(4)], four) - product(factor[TOP, columns(5)], five)
+        for rows, tiles in sides:
+            start = top3[rows, :] - change7[rows, :] - product(stacked(tiles, 8), four)
+            sent[rows, :] = start - product(stacked(tiles, 9), five)
 
 
 def line4(right_side, prev_factor, prev_solution, window_factor):
@@ -366,14 +357,12 @@
     second = move(low1, (1, 2))
     (top1,) = call(five_kernel, [size])(low1, top, factor)
     value5 = move(top1, (1, 2))
-    block2, block3 = call(third_kernel, [size, size], [pltpu.VMEM(size, jnp.float32)])(
-        first, second, low, factor, mine, theirs
+    block2, block3, change4, change5, value6, change7 = call(third_kernel, [size] * 6, [pltpu.VMEM(size, jnp.float32)])(
+        first, second, low, top, factor, mine, theirs
     )
     last3 = move(block3, (2, 3))
-    kept, block4, block5, sent = call(
-        fourth_kernel, [size] * 4, [pltpu.VMEM(size, jnp.float32)]
-    )(
-        second, block2, block3, top, value4, value5, top3, factor, mine, theirs
+    kept, block4, block5, sent = call(fourth_kernel, [size] * 4)(
+        value4, value5, top3, change4, change5, value6, change7, factor, mine, theirs
     )
     last7 = move(sent, (2, 3))
     block5 = move(block5, (2, 1))

time: 88.6 us -> 87.7 us (0.990)
  no operation moved by 1% of the time
where the time goes in v6:
time: 87.7 us; the launch traced here: 87.4 us
  waiting for transfers between devices  43.9 us (50%)
  starting transfers between devices  34.8 us (40%)
  Pallas kernels  8.42 us (10%)
    ppermute x16, waiting for transfers between devices, move(): return lax.ppermute(x, 'row', list(pairs))  38.4 us
    ppermute x16, starting transfers between devices, move(): return lax.ppermute(x, 'row', list(pairs))  32.5 us
    pallas_call x15, Pallas kernels, run(): pl.pallas_call(kernel, out_shape=[(pltpu.VMEM if inside else jax.ShapeDty...  8.42 us
    ppermute x2, waiting for transfers between devices, cross(): return lax.ppermute(x, 'col', [(0, 2), (2, 0), (1, 3), (3, 1)])  3.58 us
    ppermute x2, starting transfers between devices, cross(): return lax.ppermute(x, 'col', [(0, 2), (2, 0), (1, 3), (3, 1)])  2.16 us
    ppermute x2, waiting for transfers between devices, swap(): return lax.ppermute(x, 'col', [(0, 1), (1, 0), (2, 3), (3, 2)])  1.9 us
  transfers between devices with their start and end apart: 20, of which 8 were waited for; matrix products, arithmetic and copies ran while one was open for 0% of the time, Pallas kernels for 9%

profile of v6, /device:TPU:0, one launch (start us, length us, event | category | flops | bytes accessed | tf_op | source)
XLA Modules:
  0.0 87.4 jit_solution(3751616991959491403)
XLA Ops:
  0.0 3.0 %collective-permute-start.1 = (f32[1024,128]{1,0:T(8,128)}, f32[1024,128]{1,0:T(8,128)S(1)}, u32[]{:S(2)}, u32[]{:S(2)}) collective-permute-start(f32[1024,128]{1,0:T(8,128)} %own.1), channel_id=1, source_target_pairs={{0,4},{4,0},{8,12},{12,8},{1,5},{5,1},{9,13},{13,9},{2,6},{6,2},{1... | collective-permute-start | bytes 1572872 | tf_op jit(solution)/shard_map/ppermute | solution.py:308
  3.0 0.7 collective-permute-start
  3.7 11.4 %collective-permute-done.1.edge1 = f32[1024,128]{1,0:T(8,128)S(1)} collective-permute-done((f32[1024,128]{1,0:T(8,128)}, f32[1024,128]{1,0:T(8,128)S(1)}, u32[]{:S(2)}, u32[]{:S(2)}) %collective-permute-start.1) | collective-permute-done | bytes 524320 | tf_op jit(solution)/shard_map/ppermute | solution.py:308
  15.2 0.7 collective-permute-start.3
  15.9 1.2 %shard_map.46 = f32[1024,128]{1,0:T(8,128)S(1)} custom-call(f32[1024,128]{1,0:T(8,128)S(1)} %copy.7.x_in, f32[512,1536]{1,0:T(8,128)} %factor.3), custom_call_target="tpu_custom_call", output_to_operand_aliasing={{}: (0, {})} | custom-call | tf_op jit(solution)/shard_map/pallas_call | solution.py:77
  17.1 3.6 %collective-permute-start.2 = (f32[1024,128]{1,0:T(8,128)S(1)}, f32[1024,128]{1,0:T(8,128)S(1)}, u32[]{:S(2)}, u32[]{:S(2)}) collective-permute-start(f32[1024,128]{1,0:T(8,128)S(1)} %shard_map.46), channel_id=1, source_target_pairs={{0,4},{4,0},{8,12},{12,8},{1,5},{5,1},{9,13},{13,9},{2,6},{6,2},{1... | collective-permute-start | bytes 1572872 | tf_op jit(solution)/shard_map/ppermute | solution.py:308
  20.6 3.2 %shard_map.47 = (f32[512,1024]{1,0:T(8,128)S(1)}, f32[512,1536]{1,0:T(8,128)S(1)}, f32[512,128]{1,0:T(8,128)S(1)}, f32[1024,128]{1,0:T(8,128)S(1)}, f32[1024,128]{1,0:T(8,128)S(1)}, /*index=5*/f32[512,128]{1,0:T(8,128)S(1)}) custom-call(f32[512,1024]{1,0:T(8,128)} %past, f32[512,1536]{1,0:T(8,128)} %factor.3, f32[512,512]{1,0:T(8,128)} %side.1), custom_call_target="tpu_custom_call" | custom-call | tf_op jit(solution)/shard_map/pallas_call | solution.py:77
  23.8 7.7 %collective-permute-start.4 = (f32[1024,128]{1,0:T(8,128)S(1)}, f32[1024,128]{1,0:T(8,128)S(1)}, u32[]{:S(2)}, u32[]{:S(2)}) collective-permute-start(f32[1024,128]{1,0:T(8,128)S(1)} %shard_map.48.middle2), channel_id=1, source_target_pairs={{0,4},{4,0},{8,12},{12,8},{1,5},{5,1},{9,13},{13,9},{2,6},{6,2},{1... | collective-permute-start | bytes 1572872 | tf_op jit(solution)/shard_map/ppermute | solution.py:308
  31.6 0.7 collective-permute-done.2.edge2.refs_0_
  32.3 1.8 %shard_map.49.early = f32[3,512,128]{2,1,0:T(8,128)S(1)} custom-call(f32[512,1024]{1,0:T(8,128)S(1)} %get-tuple-element.33.past, f32[1024,128]{1,0:T(8,128)S(1)} %copy-done, f32[1024,128]{1,0:T(8,128)S(1)} %collective-permute-done.1.edge1, f32[1024,128]{1,0:T(8,128)S(1)} %collective-permute-done.2.edge2.refs_0_, f32[1024,128]{1,0:T(8,128)S(1)} %shard_map.48.middle2), custom_call_target="tpu_custom_call" | custom-call | tf_op jit(solution)/shard_map/pallas_call | solution.py:77
  34.2 0.7 collective-permute-start.11
  34.9 7.7 %collective-permute-done.4.edge3.refs_1_ = f32[1024,128]{1,0:T(8,128)S(1)} collective-permute-done((f32[1024,128]{1,0:T(8,128)S(1)}, f32[1024,128]{1,0:T(8,128)S(1)}, u32[]{:S(2)}, u32[]{:S(2)}) %collective-permute-start.4) | collective-permute-done | bytes 524320 | tf_op jit(solution)/shard_map/ppermute | solution.py:308
  42.6 0.7 shard_map.50
  43.5 1.9 %collective-permute-done.5.came = f32[2,512,128]{2,1,0:T(8,128)S(1)} collective-permute-done((f32[2,512,128]{2,1,0:T(8,128)S(1)}, f32[2,512,128]{2,1,0:T(8,128)S(1)}, u32[]{:S(2)}, u32[]{:S(2)}) %collective-permute-start.5) | collective-permute-done | bytes 524320 | tf_op jit(solution)/shard_map/ppermute | solution.py:311
  45.4 1.6 %collective-permute-start.6 = (f32[256,128]{1,0:T(8,128)S(1)}, f32[256,128]{1,0:T(8,128)S(1)}, u32[]{:S(2)}, u32[]{:S(2)}) collective-permute-start(f32[256,128]{1,0:T(8,128)S(1)} %get-tuple-element.38), channel_id=1, source_target_pairs={{0,2},{2,0},{1,3},{3,1},{4,6},{6,4},{5,7},{7,5},{8,10},{10,8},{9,1... | collective-permute-start | bytes 393224 | tf_op jit(solution)/shard_map/ppermute | solution.py:314
  48.3 3.6 %collective-permute-done.6.two = f32[256,128]{1,0:T(8,128)S(1)} collective-permute-done((f32[256,128]{1,0:T(8,128)S(1)}, f32[256,128]{1,0:T(8,128)S(1)}, u32[]{:S(2)}, u32[]{:S(2)}) %collective-permute-start.6) | collective-permute-done | bytes 131104 | tf_op jit(solution)/shard_map/ppermute | solution.py:314
  52.1 3.4 %collective-permute-start.7 = (f32[256,128]{1,0:T(8,128)S(1)}, f32[256,128]{1,0:T(8,128)S(1)}, u32[]{:S(2)}, u32[]{:S(2)}) collective-permute-start(f32[256,128]{1,0:T(8,128)S(1)} %shard_map.52.low.low_in.low2), channel_id=1, source_target_pairs={{0,4},{12,8},{1,5},{13,9},{2,6},{14,10},{3,7},{15,11},{16,20},{28,... | collective-permute-start | bytes 393224 | tf_op jit(solution)/shard_map/ppermute | solution.py:308
  55.8 2.2 %collective-permute-done.7.solved.first = f32[256,128]{1,0:T(8,128)S(1)} collective-permute-done((f32[256,128]{1,0:T(8,128)S(1)}, f32[256,128]{1,0:T(8,128)S(1)}, u32[]{:S(2)}, u32[]{:S(2)}) %collective-permute-start.7) | collective-permute-done | bytes 131104 | tf_op jit(solution)/shard_map/ppermute | solution.py:308
  58.3 0.7 collective-permute-start.9
  59.0 6.7 %collective-permute-start.13 = (f32[256,128]{1,0:T(8,128)S(1)}, f32[256,128]{1,0:T(8,128)S(1)}, u32[]{:S(2)}, u32[]{:S(2)}) collective-permute-start(f32[256,128]{1,0:T(8,128)S(1)} %shard_map.53.top2.top_in), channel_id=1, source_target_pairs={{0,8},{1,9},{2,10},{3,11},{16,24},{17,25},{18,26},{19,27}} | collective-permute-start | bytes 393224 | tf_op jit(solution)/shard_map/ppermute | solution.py:308
  67.0 2.0 %collective-permute-done.13.value4 = f32[256,128]{1,0:T(8,128)S(1)} collective-permute-done((f32[256,128]{1,0:T(8,128)S(1)}, f32[256,128]{1,0:T(8,128)S(1)}, u32[]{:S(2)}, u32[]{:S(2)}) %collective-permute-start.13) | collective-permute-done | bytes 131104 | tf_op jit(solution)/shard_map/ppermute | solution.py:308
  69.7 1.3 %collective-permute-start.18 = (f32[256,128]{1,0:T(8,128)S(1)}, f32[256,128]{1,0:T(8,128)S(1)}, u32[]{:S(2)}, u32[]{:S(2)}) collective-permute-start(f32[256,128]{1,0:T(8,128)S(1)} %get-tuple-element.55), channel_id=1, source_target_pairs={{8,0},{9,1},{10,2},{11,3},{24,16},{25,17},{26,18},{27,19}} | collective-permute-start | bytes 393224 | tf_op jit(solution)/shard_map/ppermute | solution.py:308
  72.4 14.3 %collective-permute-done.18.block4 = f32[256,128]{1,0:T(8,128)S(1)} collective-permute-done((f32[256,128]{1,0:T(8,128)S(1)}, f32[256,128]{1,0:T(8,128)S(1)}, u32[]{:S(2)}, u32[]{:S(2)}) %collective-permute-start.18) | collective-permute-done | bytes 131104 | tf_op jit(solution)/shard_map/ppermute | solution.py:308
  86.7 0.7 shard_map.60
  (34 shorter events, 5.7 us)
Async XLA Ops:
  0.0 15.2 %collective-permute-start.1 = (f32[1024,128]{1,0:T(8,128)}, f32[1024,128]{1,0:T(8,128)S(1)}, u32[]{:S(2)}, u32[]{:S(2)}) collective-permute-start(f32[1024,128]{1,0:T(8,128)} %own.1), channel_id=1, source_target_pairs={{0,4},{4,0},{8,12},{12,8},{1,5},{5,1},{9,13},{13,9},{2,6},{6,2},{1... | collective-permute-start | bytes 1572872 | tf_op jit(solution)/shard_map/ppermute | solution.py:308
  3.0 12.8 %collective-permute-start = (f32[1024,128]{1,0:T(8,128)}, f32[1024,128]{1,0:T(8,128)S(1)}, u32[]{:S(2)}, u32[]{:S(2)}) collective-permute-start(f32[1024,128]{1,0:T(8,128)} %own.1), channel_id=1, source_target_pairs={{4,8},{8,4},{5,9},{9,5},{6,10},{10,6},{7,11},{11,7},{20,24},{24,20... | collective-permute-start | bytes 1572872 | tf_op jit(solution)/shard_map/ppermute | solution.py:308
  15.2 8.6 %collective-permute-start.3 = (f32[1024,128]{1,0:T(8,128)S(1)}, f32[1024,128]{1,0:T(8,128)S(1)}, u32[]{:S(2)}, u32[]{:S(2)}) collective-permute-start(f32[1024,128]{1,0:T(8,128)S(1)} %collective-permute-done.1.edge1), channel_id=1, source_target_pairs={{4,8},{8,4},{5,9},{9,5},{6,10},{10,6},{7,11},{11,7},{20,24},{24,20... | collective-permute-start | bytes 1572872 | tf_op jit(solution)/shard_map/ppermute | solution.py:308
  17.1 15.2 %copy-start = (f32[1024,128]{1,0:T(8,128)S(1)}, f32[1024,128]{1,0:T(8,128)}, u32[]{:S(2)}) copy-start(f32[1024,128]{1,0:T(8,128)} %own.1) | copy-start | bytes 1572868
  17.1 15.2 %collective-permute-start.2 = (f32[1024,128]{1,0:T(8,128)S(1)}, f32[1024,128]{1,0:T(8,128)S(1)}, u32[]{:S(2)}, u32[]{:S(2)}) collective-permute-start(f32[1024,128]{1,0:T(8,128)S(1)} %shard_map.46), channel_id=1, source_target_pairs={{0,4},{4,0},{8,12},{12,8},{1,5},{5,1},{9,13},{13,9},{2,6},{6,2},{1... | collective-permute-start | bytes 1572872 | tf_op jit(solution)/shard_map/ppermute | solution.py:308
  23.8 18.8 %collective-permute-start.4 = (f32[1024,128]{1,0:T(8,128)S(1)}, f32[1024,128]{1,0:T(8,128)S(1)}, u32[]{:S(2)}, u32[]{:S(2)}) collective-permute-start(f32[1024,128]{1,0:T(8,128)S(1)} %shard_map.48.middle2), channel_id=1, source_target_pairs={{0,4},{4,0},{8,12},{12,8},{1,5},{5,1},{9,13},{13,9},{2,6},{6,2},{1... | collective-permute-start | bytes 1572872 | tf_op jit(solution)/shard_map/ppermute | solution.py:308
  34.2 21.6 %collective-permute-start.11 = (f32[2048,128]{1,0:T(8,128)S(1)}, f32[2048,128]{1,0:T(8,128)S(1)}, u32[]{:S(2)}, u32[]{:S(2)}) collective-permute-start(f32[2048,128]{1,0:T(8,128)S(1)} %shard_map.55), channel_id=1, source_target_pairs={{4,8},{5,9},{6,10},{7,11},{20,24},{21,25},{22,26},{23,27}} | collective-permute-start | bytes 3145736 | tf_op jit(solution)/shard_map/ppermute | solution.py:308
  43.4 2.0 %collective-permute-start.5 = (f32[2,512,128]{2,1,0:T(8,128)S(1)}, f32[2,512,128]{2,1,0:T(8,128)S(1)}, u32[]{:S(2)}, u32[]{:S(2)}) collective-permute-start(f32[2,512,128]{2,1,0:T(8,128)S(1)} %get-tuple-element.36), channel_id=1, source_target_pairs={{0,1},{1,0},{2,3},{3,2},{4,5},{5,4},{6,7},{7,6},{8,9},{9,8},{10,11... | collective-permute-start | bytes 1572872 | tf_op jit(solution)/shard_map/ppermute | solution.py:311
  45.4 6.4 %collective-permute-start.6 = (f32[256,128]{1,0:T(8,128)S(1)}, f32[256,128]{1,0:T(8,128)S(1)}, u32[]{:S(2)}, u32[]{:S(2)}) collective-permute-start(f32[256,128]{1,0:T(8,128)S(1)} %get-tuple-element.38), channel_id=1, source_target_pairs={{0,2},{2,0},{1,3},{3,1},{4,6},{6,4},{5,7},{7,5},{8,10},{10,8},{9,1... | collective-permute-start | bytes 393224 | tf_op jit(solution)/shard_map/ppermute | solution.py:314
  47.0 11.0 %collective-permute-start.10 = (f32[512,128]{1,0:T(8,128)S(1)}, f32[512,128]{1,0:T(8,128)S(1)}, u32[]{:S(2)}, u32[]{:S(2)}) collective-permute-start(f32[512,128]{1,0:T(8,128)S(1)} %get-tuple-element.43), channel_id=1, source_target_pairs={{12,8},{13,9},{14,10},{15,11},{28,24},{29,25},{30,26},{31,27}} | collective-permute-start | bytes 786440 | tf_op jit(solution)/shard_map/ppermute | solution.py:308
  47.6 7.9 %collective-permute-start.8 = (f32[256,128]{1,0:T(8,128)S(1)}, f32[256,128]{1,0:T(8,128)S(1)}, u32[]{:S(2)}, u32[]{:S(2)}) collective-permute-start(f32[256,128]{1,0:T(8,128)S(1)} %get-tuple-element.40), channel_id=1, source_target_pairs={{0,2},{2,0},{1,3},{3,1},{4,6},{6,4},{5,7},{7,5},{8,10},{10,8},{9,1... | collective-permute-start | bytes 393224 | tf_op jit(solution)/shard_map/ppermute | solution.py:314
  52.1 5.9 %collective-permute-start.7 = (f32[256,128]{1,0:T(8,128)S(1)}, f32[256,128]{1,0:T(8,128)S(1)}, u32[]{:S(2)}, u32[]{:S(2)}) collective-permute-start(f32[256,128]{1,0:T(8,128)S(1)} %shard_map.52.low.low_in.low2), channel_id=1, source_target_pairs={{0,4},{12,8},{1,5},{13,9},{2,6},{14,10},{3,7},{15,11},{16,20},{28,... | collective-permute-start | bytes 393224 | tf_op jit(solution)/shard_map/ppermute | solution.py:308
  58.2 8.8 %collective-permute-start.12 = (f32[4608,128]{1,0:T(8,128)S(1)}, f32[4608,128]{1,0:T(8,128)S(1)}, u32[]{:S(2)}, u32[]{:S(2)}) collective-permute-start(f32[4608,128]{1,0:T(8,128)S(1)} %shard_map.56.mine), channel_id=1, source_target_pairs={{0,1},{1,0},{2,3},{3,2},{4,5},{5,4},{6,7},{7,6},{8,9},{9,8},{10,11... | collective-permute-start | bytes 7077896 | tf_op jit(solution)/shard_map/ppermute | solution.py:311
  58.3 8.7 %collective-permute-start.9 = (f32[512,128]{1,0:T(8,128)S(1)}, f32[512,128]{1,0:T(8,128)S(1)}, u32[]{:S(2)}, u32[]{:S(2)}) collective-permute-start(f32[512,128]{1,0:T(8,128)S(1)} %shard_map.54.solved.low1), channel_id=1, source_target_pairs={{4,8},{5,9},{6,10},{7,11},{20,24},{21,25},{22,26},{23,27}} | collective-permute-start | bytes 786440 | tf_op jit(solution)/shard_map/ppermute | solution.py:308
  59.0 10.1 %collective-permute-start.13 = (f32[256,128]{1,0:T(8,128)S(1)}, f32[256,128]{1,0:T(8,128)S(1)}, u32[]{:S(2)}, u32[]{:S(2)}) collective-permute-start(f32[256,128]{1,0:T(8,128)S(1)} %shard_map.53.top2.top_in), channel_id=1, source_target_pairs={{0,8},{1,9},{2,10},{3,11},{16,24},{17,25},{18,26},{19,27}} | collective-permute-start | bytes 393224 | tf_op jit(solution)/shard_map/ppermute | solution.py:308
  65.6 3.4 %collective-permute-start.15 = (f32[256,128]{1,0:T(8,128)S(1)}, f32[256,128]{1,0:T(8,128)S(1)}, u32[]{:S(2)}, u32[]{:S(2)}) collective-permute-start(f32[256,128]{1,0:T(8,128)S(1)} %shard_map.53.top2.top_in), channel_id=1, source_target_pairs={{12,8},{13,9},{14,10},{15,11},{28,24},{29,25},{30,26},{31,27}} | collective-permute-start | bytes 393224 | tf_op jit(solution)/shard_map/ppermute | solution.py:308
  66.3 2.7 %collective-permute-start.14 = (f32[256,128]{1,0:T(8,128)S(1)}, f32[256,128]{1,0:T(8,128)S(1)}, u32[]{:S(2)}, u32[]{:S(2)}) collective-permute-start(f32[256,128]{1,0:T(8,128)S(1)} %shard_map.58), channel_id=1, source_target_pairs={{4,8},{5,9},{6,10},{7,11},{20,24},{21,25},{22,26},{23,27}} | collective-permute-start | bytes 393224 | tf_op jit(solution)/shard_map/ppermute | solution.py:308
  69.0 3.3 %collective-permute-start.17 = (f32[256,128]{1,0:T(8,128)S(1)}, f32[256,128]{1,0:T(8,128)S(1)}, u32[]{:S(2)}, u32[]{:S(2)}) collective-permute-start(f32[256,128]{1,0:T(8,128)S(1)} %get-tuple-element.54), channel_id=1, source_target_pairs={{8,12},{9,13},{10,14},{11,15},{24,28},{25,29},{26,30},{27,31}} | collective-permute-start | bytes 393224 | tf_op jit(solution)/shard_map/ppermute | solution.py:308
  69.7 17.0 %collective-permute-start.18 = (f32[256,128]{1,0:T(8,128)S(1)}, f32[256,128]{1,0:T(8,128)S(1)}, u32[]{:S(2)}, u32[]{:S(2)}) collective-permute-start(f32[256,128]{1,0:T(8,128)S(1)} %get-tuple-element.55), channel_id=1, source_target_pairs={{8,0},{9,1},{10,2},{11,3},{24,16},{25,17},{26,18},{27,19}} | collective-permute-start | bytes 393224 | tf_op jit(solution)/shard_map/ppermute | solution.py:308
  71.0 15.7 %collective-permute-start.19 = (f32[256,128]{1,0:T(8,128)S(1)}, f32[256,128]{1,0:T(8,128)S(1)}, u32[]{:S(2)}, u32[]{:S(2)}) collective-permute-start(f32[256,128]{1,0:T(8,128)S(1)} %get-tuple-element.56), channel_id=1, source_target_pairs={{8,4},{9,5},{10,6},{11,7},{24,20},{25,21},{26,22},{27,23}} | collective-permute-start | bytes 393224 | tf_op jit(solution)/shard_map/ppermute | solution.py:308
  71.7 15.0 %collective-permute-start.16 = (f32[256,128]{1,0:T(8,128)S(1)}, f32[256,128]{1,0:T(8,128)S(1)}, u32[]{:S(2)}, u32[]{:S(2)}) collective-permute-start(f32[256,128]{1,0:T(8,128)S(1)} %get-tuple-element.53), channel_id=1, source_target_pairs={{8,12},{9,13},{10,14},{11,15},{24,28},{25,29},{26,30},{27,31}} | collective-permute-start | bytes 393224 | tf_op jit(solution)/shard_map/ppermute | solution.py:308

commit v7 on v6

--- a/solution.py
+++ b/solution.py
@@ -200,18 +200,17 @@
     @pl.when(lax.axis_index("row") == 1)
     def _():
         value = low_in[...] - product(factor[LOW, columns(0)], wide(solved[...]))
-        low[LOW, :] = solved[...]
-        low[TOP, :] = product(factor[LOW, columns(1)], wide(value))
-
-
-def five_kernel(solved, top_in, factor, top):
+        low[...] = product(factor[LOW, columns(1)], wide(value))
+
+
+def five_kernel(zero, one, top_in, factor, top):
     @pl.when(lax.axis_index("row") == 1)
     def _():
-        value = top_in[...] - product(factor[TOP, columns(0)], wide(solved[LOW, :]))
-        top[...] = value - product(factor[TOP, columns(1)], wide(solved[TOP, :]))
-
-
-def last_kernel(low, low1, low2, top2, last3, last7, block4, block5, out):
+        value = top_in[...] - product(factor[TOP, columns(0)], wide(zero[...]))
+        top[...] = value - product(factor[TOP, columns(1)], wide(one[...]))
+
+
+def last_kernel(block4, block5, last3, last7, low, low1, low2, top2, out):
     row_index = lax.axis_index("row")
 
     @pl.when(row_index == 0)
@@ -221,7 +220,7 @@
 
     @pl.when(row_index == 1)
     def _():
-        out[LOW, :] = low1[TOP, :]
+        out[LOW, :] = low1[...]
         out[TOP, :] = block5[...]
 
     @pl.when(row_index == 2)
@@ -253,12 +252,12 @@
         at += ref.shape[0]
 
 
-def third_kernel(first, second, low2, top2, factor, mine, theirs, block2, block3, change4, change5, change6, change7, value):
+def third_kernel(first, zero, second, low2, top2, factor, mine, theirs, block2, block3, change4, change5, change6, change7, value):
     @pl.when(lax.axis_index("row") == 2)
     def _():
         own, other = halves()
         sides = ((own, mine), (other, theirs))
-        pairs = [wide(second[LOW, :]), wide(second[TOP, :])]
+        pairs = [wide(zero[...]), wide(second[...])]
         start = low2[...]
         for k in range(2):
             start = start - product(factor[LOW, columns(k)], pairs[k])
@@ -281,7 +280,7 @@
 
 
 def fourth_kernel(
-    value4, value5, top3, change4, change5, value6, change7, factor, mine, theirs, kept, block4, block5, sent
+    change4, change5, value6, change7, factor, mine, theirs, value5, value4, top3, kept, block4, block5, sent
 ):
     @pl.when(lax.axis_index("row") == 2)
     def _():
@@ -348,27 +347,28 @@
     own8 = move(after(send8, one), (3, 2))
     (low,) = call(first_kernel, [size])(side, one, two_low, factor)
     first = move(low, (0, 1), (3, 2))
+    zero = move(low, (0, 2))
     (top,) = call(top_kernel, [size])(side, one, two_top, factor, low)
     value4 = move(top, (0, 2))
     top3 = move(top, (3, 2))
-    (mine,) = call(join_kernel, [(4 * tall[0] + rows[0], WIDTH)])(edge2, edge3, own8, after(mine45, first, top))
+    (mine,) = call(join_kernel, [(4 * tall[0] + rows[0], WIDTH)])(edge2, edge3, own8, after(mine45, first, zero, top))
     theirs = swap(mine)
-    (low1,) = call(second_kernel, [rows])(first, after(low, top), factor)
+    (low1,) = call(second_kernel, [size])(first, after(low, top), factor)
     second = move(low1, (1, 2))
-    (top1,) = call(five_kernel, [size])(low1, top, factor)
+    (top1,) = call(five_kernel, [size])(first, low1, top, factor)
     value5 = move(top1, (1, 2))
     block2, block3, change4, change5, value6, change7 = call(third_kernel, [size] * 6, [pltpu.VMEM(size, jnp.float32)])(
-        first, second, low, top, factor, mine, theirs
+        first, zero, second, low, top, factor, mine, theirs
     )
     last3 = move(block3, (2, 3))
     kept, block4, block5, sent = call(fourth_kernel, [size] * 4)(
-        value4, value5, top3, change4, change5, value6, change7, factor, mine, theirs
+        change4, change5, value6, change7, factor, mine, theirs, value5, value4, top3
     )
     last7 = move(sent, (2, 3))
     block5 = move(block5, (2, 1))
     block4 = move(block4, (2, 0))
     return call(last_kernel, [rows], inside=False)(
-        low, low1, block2, kept, last3, last7, block4, block5
+        block4, block5, last3, last7, low, low1, block2, kept
     )[0]
 
 

time: 87.7 us -> 86 us (0.981)
  waiting for transfers between devices: 43.9 us -> 40.7 us
    ppermute x16 -> x17, waiting for transfers between devices: 38.4 us -> 35.2 us  [move(): return lax.ppermute(x, 'row', list(pairs))]
    ppermute x16 -> x17, starting transfers between devices: 32.5 us -> 33 us  [move(): return lax.ppermute(x, 'row', list(pairs))]
  transfers between devices with their start and end apart: 20 -> 21, of which waited for: 8 -> 9; matrix products, arithmetic and copies ran while one was open for 0% -> 0% of each run, Pallas kernels for 9% -> 9%
where the time goes in v7:
time: 86 us; the launch traced here: 84.8 us
  waiting for transfers between devices  40.7 us (47%)
  starting transfers between devices  35.3 us (41%)
  Pallas kernels  8.44 us (10%)
    ppermute x17, waiting for transfers between devices, move(): return lax.ppermute(x, 'row', list(pairs))  35.2 us
    ppermute x17, starting transfers between devices, move(): return lax.ppermute(x, 'row', list(pairs))  33 us
    pallas_call x15, Pallas kernels, run(): pl.pallas_call(kernel, out_shape=[(pltpu.VMEM if inside else jax.ShapeDty...  8.44 us
    ppermute x2, waiting for transfers between devices, cross(): return lax.ppermute(x, 'col', [(0, 2), (2, 0), (1, 3), (3, 1)])  3.58 us
    ppermute x2, starting transfers between devices, cross(): return lax.ppermute(x, 'col', [(0, 2), (2, 0), (1, 3), (3, 1)])  2.16 us
    ppermute x2, waiting for transfers between devices, swap(): return lax.ppermute(x, 'col', [(0, 1), (1, 0), (2, 3), (3, 2)])  1.9 us
  transfers between devices with their start and end apart: 21, of which 9 were waited for; matrix products, arithmetic and copies ran while one was open for 0% of the time, Pallas kernels for 9%

profile of v7, /device:TPU:0, one launch (start us, length us, event | category | flops | bytes accessed | tf_op | source)
XLA Modules:
  0.0 84.8 jit_solution(5702191105228030484)
XLA Ops:
  0.0 3.0 %collective-permute-start.1 = (f32[1024,128]{1,0:T(8,128)}, f32[1024,128]{1,0:T(8,128)S(1)}, u32[]{:S(2)}, u32[]{:S(2)}) collective-permute-start(f32[1024,128]{1,0:T(8,128)} %own.1), channel_id=1, source_target_pairs={{0,4},{4,0},{8,12},{12,8},{1,5},{5,1},{9,13},{13,9},{2,6},{6,2},{1... | collective-permute-start | bytes 1572872 | tf_op jit(solution)/shard_map/ppermute | solution.py:307
  3.7 11.4 %collective-permute-done.1.edge1 = f32[1024,128]{1,0:T(8,128)S(1)} collective-permute-done((f32[1024,128]{1,0:T(8,128)}, f32[1024,128]{1,0:T(8,128)S(1)}, u32[]{:S(2)}, u32[]{:S(2)}) %collective-permute-start.1) | collective-permute-done | bytes 524320 | tf_op jit(solution)/shard_map/ppermute | solution.py:307
  15.2 0.7 collective-permute-start.3
  15.9 1.2 %shard_map.46 = f32[1024,128]{1,0:T(8,128)S(1)} custom-call(f32[1024,128]{1,0:T(8,128)S(1)} %copy.7.x_in, f32[512,1536]{1,0:T(8,128)} %factor.3), custom_call_target="tpu_custom_call", output_to_operand_aliasing={{}: (0, {})} | custom-call | tf_op jit(solution)/shard_map/pallas_call | solution.py:77
  17.1 3.6 %collective-permute-start.2 = (f32[1024,128]{1,0:T(8,128)S(1)}, f32[1024,128]{1,0:T(8,128)S(1)}, u32[]{:S(2)}, u32[]{:S(2)}) collective-permute-start(f32[1024,128]{1,0:T(8,128)S(1)} %shard_map.46), channel_id=1, source_target_pairs={{0,4},{4,0},{8,12},{12,8},{1,5},{5,1},{9,13},{13,9},{2,6},{6,2},{1... | collective-permute-start | bytes 1572872 | tf_op jit(solution)/shard_map/ppermute | solution.py:307
  20.6 3.2 %shard_map.47 = (f32[512,1024]{1,0:T(8,128)S(1)}, f32[512,1536]{1,0:T(8,128)S(1)}, f32[512,128]{1,0:T(8,128)S(1)}, f32[1024,128]{1,0:T(8,128)S(1)}, f32[1024,128]{1,0:T(8,128)S(1)}, /*index=5*/f32[512,128]{1,0:T(8,128)S(1)}) custom-call(f32[512,1024]{1,0:T(8,128)} %past, f32[512,1536]{1,0:T(8,128)} %factor.3, f32[512,512]{1,0:T(8,128)} %side.1), custom_call_target="tpu_custom_call" | custom-call | tf_op jit(solution)/shard_map/pallas_call | solution.py:77
  23.8 7.7 %collective-permute-start.4 = (f32[1024,128]{1,0:T(8,128)S(1)}, f32[1024,128]{1,0:T(8,128)S(1)}, u32[]{:S(2)}, u32[]{:S(2)}) collective-permute-start(f32[1024,128]{1,0:T(8,128)S(1)} %shard_map.48.middle2), channel_id=1, source_target_pairs={{0,4},{4,0},{8,12},{12,8},{1,5},{5,1},{9,13},{13,9},{2,6},{6,2},{1... | collective-permute-start | bytes 1572872 | tf_op jit(solution)/shard_map/ppermute | solution.py:307
  31.6 0.7 collective-permute-done.2.edge2.refs_0_
  32.3 1.8 %shard_map.49.early = f32[3,512,128]{2,1,0:T(8,128)S(1)} custom-call(f32[512,1024]{1,0:T(8,128)S(1)} %get-tuple-element.33.past, f32[1024,128]{1,0:T(8,128)S(1)} %copy-done, f32[1024,128]{1,0:T(8,128)S(1)} %collective-permute-done.1.edge1, f32[1024,128]{1,0:T(8,128)S(1)} %collective-permute-done.2.edge2.refs_0_, f32[1024,128]{1,0:T(8,128)S(1)} %shard_map.48.middle2), custom_call_target="tpu_custom_call" | custom-call | tf_op jit(solution)/shard_map/pallas_call | solution.py:77
  34.2 0.7 collective-permute-start.12
  34.9 7.7 %collective-permute-done.4.edge3.refs_1_ = f32[1024,128]{1,0:T(8,128)S(1)} collective-permute-done((f32[1024,128]{1,0:T(8,128)S(1)}, f32[1024,128]{1,0:T(8,128)S(1)}, u32[]{:S(2)}, u32[]{:S(2)}) %collective-permute-start.4) | collective-permute-done | bytes 524320 | tf_op jit(solution)/shard_map/ppermute | solution.py:307
  42.6 0.7 shard_map.50
  43.5 1.9 %collective-permute-done.5.came = f32[2,512,128]{2,1,0:T(8,128)S(1)} collective-permute-done((f32[2,512,128]{2,1,0:T(8,128)S(1)}, f32[2,512,128]{2,1,0:T(8,128)S(1)}, u32[]{:S(2)}, u32[]{:S(2)}) %collective-permute-start.5) | collective-permute-done | bytes 524320 | tf_op jit(solution)/shard_map/ppermute | solution.py:310
  45.4 1.6 %collective-permute-start.6 = (f32[256,128]{1,0:T(8,128)S(1)}, f32[256,128]{1,0:T(8,128)S(1)}, u32[]{:S(2)}, u32[]{:S(2)}) collective-permute-start(f32[256,128]{1,0:T(8,128)S(1)} %get-tuple-element.38), channel_id=1, source_target_pairs={{0,2},{2,0},{1,3},{3,1},{4,6},{6,4},{5,7},{7,5},{8,10},{10,8},{9,1... | collective-permute-start | bytes 393224 | tf_op jit(solution)/shard_map/ppermute | solution.py:313
  48.3 3.6 %collective-permute-done.6.two = f32[256,128]{1,0:T(8,128)S(1)} collective-permute-done((f32[256,128]{1,0:T(8,128)S(1)}, f32[256,128]{1,0:T(8,128)S(1)}, u32[]{:S(2)}, u32[]{:S(2)}) %collective-permute-start.6) | collective-permute-done | bytes 131104 | tf_op jit(solution)/shard_map/ppermute | solution.py:313
  52.1 3.4 %collective-permute-start.7 = (f32[256,128]{1,0:T(8,128)S(1)}, f32[256,128]{1,0:T(8,128)S(1)}, u32[]{:S(2)}, u32[]{:S(2)}) collective-permute-start(f32[256,128]{1,0:T(8,128)S(1)} %shard_map.52.low.low_in.low2), channel_id=1, source_target_pairs={{0,4},{12,8},{1,5},{13,9},{2,6},{14,10},{3,7},{15,11},{16,20},{28,... | collective-permute-start | bytes 393224 | tf_op jit(solution)/shard_map/ppermute | solution.py:307
  55.5 1.3 %collective-permute-start.8 = (f32[256,128]{1,0:T(8,128)S(1)}, f32[256,128]{1,0:T(8,128)S(1)}, u32[]{:S(2)}, u32[]{:S(2)}) collective-permute-start(f32[256,128]{1,0:T(8,128)S(1)} %shard_map.52.low.low_in.low2), channel_id=1, source_target_pairs={{0,8},{1,9},{2,10},{3,11},{16,24},{17,25},{18,26},{19,27}} | collective-permute-start | bytes 393224 | tf_op jit(solution)/shard_map/ppermute | solution.py:307
  57.1 1.7 %collective-permute-done.7.solved.first.zero = f32[256,128]{1,0:T(8,128)S(1)} collective-permute-done((f32[256,128]{1,0:T(8,128)S(1)}, f32[256,128]{1,0:T(8,128)S(1)}, u32[]{:S(2)}, u32[]{:S(2)}) %collective-permute-start.7) | collective-permute-done | bytes 131104 | tf_op jit(solution)/shard_map/ppermute | solution.py:307
  58.9 1.4 %collective-permute-done.8.zero = f32[256,128]{1,0:T(8,128)S(1)} collective-permute-done((f32[256,128]{1,0:T(8,128)S(1)}, f32[256,128]{1,0:T(8,128)S(1)}, u32[]{:S(2)}, u32[]{:S(2)}) %collective-permute-start.8) | collective-permute-done | bytes 131104 | tf_op jit(solution)/shard_map/ppermute | solution.py:307
  61.2 5.9 %collective-permute-start.15 = (f32[256,128]{1,0:T(8,128)S(1)}, f32[256,128]{1,0:T(8,128)S(1)}, u32[]{:S(2)}, u32[]{:S(2)}) collective-permute-start(f32[256,128]{1,0:T(8,128)S(1)} %shard_map.53.top2.top_in), channel_id=1, source_target_pairs={{0,8},{1,9},{2,10},{3,11},{16,24},{17,25},{18,26},{19,27}} | collective-permute-start | bytes 393224 | tf_op jit(solution)/shard_map/ppermute | solution.py:307
  68.6 2.0 %collective-permute-done.15.value4 = f32[256,128]{1,0:T(8,128)S(1)} collective-permute-done((f32[256,128]{1,0:T(8,128)S(1)}, f32[256,128]{1,0:T(8,128)S(1)}, u32[]{:S(2)}, u32[]{:S(2)}) %collective-permute-start.15) | collective-permute-done | bytes 131104 | tf_op jit(solution)/shard_map/ppermute | solution.py:307
  70.5 1.3 %collective-permute-start.17 = (f32[256,128]{1,0:T(8,128)S(1)}, f32[256,128]{1,0:T(8,128)S(1)}, u32[]{:S(2)}, u32[]{:S(2)}) collective-permute-start(f32[256,128]{1,0:T(8,128)S(1)} %get-tuple-element.51), channel_id=1, source_target_pairs={{8,0},{9,1},{10,2},{11,3},{24,16},{25,17},{26,18},{27,19}} | collective-permute-start | bytes 393224 | tf_op jit(solution)/shard_map/ppermute | solution.py:307
  73.9 10.2 %collective-permute-done.17.block4 = f32[256,128]{1,0:T(8,128)S(1)} collective-permute-done((f32[256,128]{1,0:T(8,128)S(1)}, f32[256,128]{1,0:T(8,128)S(1)}, u32[]{:S(2)}, u32[]{:S(2)}) %collective-permute-start.17) | collective-permute-done | bytes 131104 | tf_op jit(solution)/shard_map/ppermute | solution.py:307
  84.1 0.7 shard_map.60
  (36 shorter events, 7.0 us)
Async XLA Ops:
  0.0 15.2 %collective-permute-start.1 = (f32[1024,128]{1,0:T(8,128)}, f32[1024,128]{1,0:T(8,128)S(1)}, u32[]{:S(2)}, u32[]{:S(2)}) collective-permute-start(f32[1024,128]{1,0:T(8,128)} %own.1), channel_id=1, source_target_pairs={{0,4},{4,0},{8,12},{12,8},{1,5},{5,1},{9,13},{13,9},{2,6},{6,2},{1... | collective-permute-start | bytes 1572872 | tf_op jit(solution)/shard_map/ppermute | solution.py:307
  3.0 12.8 %collective-permute-start = (f32[1024,128]{1,0:T(8,128)}, f32[1024,128]{1,0:T(8,128)S(1)}, u32[]{:S(2)}, u32[]{:S(2)}) collective-permute-start(f32[1024,128]{1,0:T(8,128)} %own.1), channel_id=1, source_target_pairs={{4,8},{8,4},{5,9},{9,5},{6,10},{10,6},{7,11},{11,7},{20,24},{24,20... | collective-permute-start | bytes 1572872 | tf_op jit(solution)/shard_map/ppermute | solution.py:307
  15.2 8.6 %collective-permute-start.3 = (f32[1024,128]{1,0:T(8,128)S(1)}, f32[1024,128]{1,0:T(8,128)S(1)}, u32[]{:S(2)}, u32[]{:S(2)}) collective-permute-start(f32[1024,128]{1,0:T(8,128)S(1)} %collective-permute-done.1.edge1), channel_id=1, source_target_pairs={{4,8},{8,4},{5,9},{9,5},{6,10},{10,6},{7,11},{11,7},{20,24},{24,20... | collective-permute-start | bytes 1572872 | tf_op jit(solution)/shard_map/ppermute | solution.py:307
  17.1 15.2 %copy-start = (f32[1024,128]{1,0:T(8,128)S(1)}, f32[1024,128]{1,0:T(8,128)}, u32[]{:S(2)}) copy-start(f32[1024,128]{1,0:T(8,128)} %own.1) | copy-start | bytes 1572868
  17.1 15.2 %collective-permute-start.2 = (f32[1024,128]{1,0:T(8,128)S(1)}, f32[1024,128]{1,0:T(8,128)S(1)}, u32[]{:S(2)}, u32[]{:S(2)}) collective-permute-start(f32[1024,128]{1,0:T(8,128)S(1)} %shard_map.46), channel_id=1, source_target_pairs={{0,4},{4,0},{8,12},{12,8},{1,5},{5,1},{9,13},{13,9},{2,6},{6,2},{1... | collective-permute-start | bytes 1572872 | tf_op jit(solution)/shard_map/ppermute | solution.py:307
  23.8 18.8 %collective-permute-start.4 = (f32[1024,128]{1,0:T(8,128)S(1)}, f32[1024,128]{1,0:T(8,128)S(1)}, u32[]{:S(2)}, u32[]{:S(2)}) collective-permute-start(f32[1024,128]{1,0:T(8,128)S(1)} %shard_map.48.middle2), channel_id=1, source_target_pairs={{0,4},{4,0},{8,12},{12,8},{1,5},{5,1},{9,13},{13,9},{2,6},{6,2},{1... | collective-permute-start | bytes 1572872 | tf_op jit(solution)/shard_map/ppermute | solution.py:307
  34.2 22.9 %collective-permute-start.12 = (f32[2048,128]{1,0:T(8,128)S(1)}, f32[2048,128]{1,0:T(8,128)S(1)}, u32[]{:S(2)}, u32[]{:S(2)}) collective-permute-start(f32[2048,128]{1,0:T(8,128)S(1)} %shard_map.55), channel_id=1, source_target_pairs={{4,8},{5,9},{6,10},{7,11},{20,24},{21,25},{22,26},{23,27}} | collective-permute-start | bytes 3145736 | tf_op jit(solution)/shard_map/ppermute | solution.py:307
  43.4 2.0 %collective-permute-start.5 = (f32[2,512,128]{2,1,0:T(8,128)S(1)}, f32[2,512,128]{2,1,0:T(8,128)S(1)}, u32[]{:S(2)}, u32[]{:S(2)}) collective-permute-start(f32[2,512,128]{2,1,0:T(8,128)S(1)} %get-tuple-element.36), channel_id=1, source_target_pairs={{0,1},{1,0},{2,3},{3,2},{4,5},{5,4},{6,7},{7,6},{8,9},{9,8},{10,11... | collective-permute-start | bytes 1572872 | tf_op jit(solution)/shard_map/ppermute | solution.py:310
  45.4 6.4 %collective-permute-start.6 = (f32[256,128]{1,0:T(8,128)S(1)}, f32[256,128]{1,0:T(8,128)S(1)}, u32[]{:S(2)}, u32[]{:S(2)}) collective-permute-start(f32[256,128]{1,0:T(8,128)S(1)} %get-tuple-element.38), channel_id=1, source_target_pairs={{0,2},{2,0},{1,3},{3,1},{4,6},{6,4},{5,7},{7,5},{8,10},{10,8},{9,1... | collective-permute-start | bytes 393224 | tf_op jit(solution)/shard_map/ppermute | solution.py:313
  47.0 13.3 %collective-permute-start.11 = (f32[512,128]{1,0:T(8,128)S(1)}, f32[512,128]{1,0:T(8,128)S(1)}, u32[]{:S(2)}, u32[]{:S(2)}) collective-permute-start(f32[512,128]{1,0:T(8,128)S(1)} %get-tuple-element.43), channel_id=1, source_target_pairs={{12,8},{13,9},{14,10},{15,11},{28,24},{29,25},{30,26},{31,27}} | collective-permute-start | bytes 786440 | tf_op jit(solution)/shard_map/ppermute | solution.py:307
  47.6 9.2 %collective-permute-start.9 = (f32[256,128]{1,0:T(8,128)S(1)}, f32[256,128]{1,0:T(8,128)S(1)}, u32[]{:S(2)}, u32[]{:S(2)}) collective-permute-start(f32[256,128]{1,0:T(8,128)S(1)} %get-tuple-element.40), channel_id=1, source_target_pairs={{0,2},{2,0},{1,3},{3,1},{4,6},{6,4},{5,7},{7,5},{8,10},{10,8},{9,1... | collective-permute-start | bytes 393224 | tf_op jit(solution)/shard_map/ppermute | solution.py:313
  52.1 6.8 %collective-permute-start.7 = (f32[256,128]{1,0:T(8,128)S(1)}, f32[256,128]{1,0:T(8,128)S(1)}, u32[]{:S(2)}, u32[]{:S(2)}) collective-permute-start(f32[256,128]{1,0:T(8,128)S(1)} %shard_map.52.low.low_in.low2), channel_id=1, source_target_pairs={{0,4},{12,8},{1,5},{13,9},{2,6},{14,10},{3,7},{15,11},{16,20},{28,... | collective-permute-start | bytes 393224 | tf_op jit(solution)/shard_map/ppermute | solution.py:307
  55.5 4.8 %collective-permute-start.8 = (f32[256,128]{1,0:T(8,128)S(1)}, f32[256,128]{1,0:T(8,128)S(1)}, u32[]{:S(2)}, u32[]{:S(2)}) collective-permute-start(f32[256,128]{1,0:T(8,128)S(1)} %shard_map.52.low.low_in.low2), channel_id=1, source_target_pairs={{0,8},{1,9},{2,10},{3,11},{16,24},{17,25},{18,26},{19,27}} | collective-permute-start | bytes 393224 | tf_op jit(solution)/shard_map/ppermute | solution.py:307
  60.4 8.1 %collective-permute-start.13 = (f32[4608,128]{1,0:T(8,128)S(1)}, f32[4608,128]{1,0:T(8,128)S(1)}, u32[]{:S(2)}, u32[]{:S(2)}) collective-permute-start(f32[4608,128]{1,0:T(8,128)S(1)} %shard_map.56.mine), channel_id=1, source_target_pairs={{0,1},{1,0},{2,3},{3,2},{4,5},{5,4},{6,7},{7,6},{8,9},{9,8},{10,11... | collective-permute-start | bytes 7077896 | tf_op jit(solution)/shard_map/ppermute | solution.py:310
  60.5 8.0 %collective-permute-start.10 = (f32[256,128]{1,0:T(8,128)S(1)}, f32[256,128]{1,0:T(8,128)S(1)}, u32[]{:S(2)}, u32[]{:S(2)}) collective-permute-start(f32[256,128]{1,0:T(8,128)S(1)} %shard_map.54.one.low1), channel_id=1, source_target_pairs={{4,8},{5,9},{6,10},{7,11},{20,24},{21,25},{22,26},{23,27}} | collective-permute-start | bytes 393224 | tf_op jit(solution)/shard_map/ppermute | solution.py:307
  61.2 9.3 %collective-permute-start.15 = (f32[256,128]{1,0:T(8,128)S(1)}, f32[256,128]{1,0:T(8,128)S(1)}, u32[]{:S(2)}, u32[]{:S(2)}) collective-permute-start(f32[256,128]{1,0:T(8,128)S(1)} %shard_map.53.top2.top_in), channel_id=1, source_target_pairs={{0,8},{1,9},{2,10},{3,11},{16,24},{17,25},{18,26},{19,27}} | collective-permute-start | bytes 393224 | tf_op jit(solution)/shard_map/ppermute | solution.py:307
  67.1 3.4 %collective-permute-start.16 = (f32[256,128]{1,0:T(8,128)S(1)}, f32[256,128]{1,0:T(8,128)S(1)}, u32[]{:S(2)}, u32[]{:S(2)}) collective-permute-start(f32[256,128]{1,0:T(8,128)S(1)} %shard_map.53.top2.top_in), channel_id=1, source_target_pairs={{12,8},{13,9},{14,10},{15,11},{28,24},{29,25},{30,26},{31,27}} | collective-permute-start | bytes 393224 | tf_op jit(solution)/shard_map/ppermute | solution.py:307
  67.8 2.7 %collective-permute-start.14 = (f32[256,128]{1,0:T(8,128)S(1)}, f32[256,128]{1,0:T(8,128)S(1)}, u32[]{:S(2)}, u32[]{:S(2)}) collective-permute-start(f32[256,128]{1,0:T(8,128)S(1)} %shard_map.58), channel_id=1, source_target_pairs={{4,8},{5,9},{6,10},{7,11},{20,24},{21,25},{22,26},{23,27}} | collective-permute-start | bytes 393224 | tf_op jit(solution)/shard_map/ppermute | solution.py:307
  70.5 13.5 %collective-permute-start.17 = (f32[256,128]{1,0:T(8,128)S(1)}, f32[256,128]{1,0:T(8,128)S(1)}, u32[]{:S(2)}, u32[]{:S(2)}) collective-permute-start(f32[256,128]{1,0:T(8,128)S(1)} %get-tuple-element.51), channel_id=1, source_target_pairs={{8,0},{9,1},{10,2},{11,3},{24,16},{25,17},{26,18},{27,19}} | collective-permute-start | bytes 393224 | tf_op jit(solution)/shard_map/ppermute | solution.py:307
  71.8 12.2 %collective-permute-start.18 = (f32[256,128]{1,0:T(8,128)S(1)}, f32[256,128]{1,0:T(8,128)S(1)}, u32[]{:S(2)}, u32[]{:S(2)}) collective-permute-start(f32[256,128]{1,0:T(8,128)S(1)} %get-tuple-element.52), channel_id=1, source_target_pairs={{8,4},{9,5},{10,6},{11,7},{24,20},{25,21},{26,22},{27,23}} | collective-permute-start | bytes 393224 | tf_op jit(solution)/shard_map/ppermute | solution.py:307
  72.5 11.6 %collective-permute-start.20 = (f32[256,128]{1,0:T(8,128)S(1)}, f32[256,128]{1,0:T(8,128)S(1)}, u32[]{:S(2)}, u32[]{:S(2)}) collective-permute-start(f32[256,128]{1,0:T(8,128)S(1)} %get-tuple-element.54), channel_id=1, source_target_pairs={{8,12},{9,13},{10,14},{11,15},{24,28},{25,29},{26,30},{27,31}} | collective-permute-start | bytes 393224 | tf_op jit(solution)/shard_map/ppermute | solution.py:307
  73.2 10.9 %collective-permute-start.19 = (f32[256,128]{1,0:T(8,128)S(1)}, f32[256,128]{1,0:T(8,128)S(1)}, u32[]{:S(2)}, u32[]{:S(2)}) collective-permute-start(f32[256,128]{1,0:T(8,128)S(1)} %get-tuple-element.53), channel_id=1, source_target_pairs={{8,12},{9,13},{10,14},{11,15},{24,28},{25,29},{26,30},{27,31}} | collective-permute-start | bytes 393224 | tf_op jit(solution)/shard_map/ppermute | solution.py:307

commit v8 on v7

--- a/solution.py
+++ b/solution.py
@@ -156,28 +156,32 @@
     return jnp.logical_or(row_index == 0, row_index == 3)
 
 
-def early_kernel(past, own, edge1, edge2, middle2, early):
+def keeps_even():
+    return lax.rem(lax.axis_index("col"), 2) == lax.rem(lax.axis_index("row"), 2)
+
+
+def early_kernel(past, own, edge1, edge2, middle2, early, away):
     got = spread(past[...], own[...], jnp.where(at_end(), edge2[...], middle2[...]), edge1[...])
     for i in range(3):
         early[i] = got[i]
-
-
-def late_kernel(past, early, edge3, middle3, away, keep):
-    row_index, col_index = lax.axis_index("row"), lax.axis_index("col")
-    keeps_even = lax.rem(col_index, 2) == lax.rem(row_index, 2)
+    away[...] = jnp.where(keeps_even(), got[2], got[0])
+
+
+def late_kernel(past, early, came, edge3, middle3, away, keep, total):
+    even = keeps_even()
     (three,) = spread(past[...], jnp.where(at_end(), edge3[...], middle3[...]))
-    near = lax.div(row_index, 2) == lax.div(col_index, 2)
-    even = [jnp.where(near, early[0], early[1]), jnp.where(near, early[1], early[0])]
-    odd = [jnp.where(near, early[2], three), jnp.where(near, three, early[2])]
-    for i in range(2):
-        away[i] = jnp.where(keeps_even, odd[i], even[i])
-        keep[i] = jnp.where(keeps_even, even[i], odd[i])
-
-
-def sum_kernel(keep, came, own, other_low, other_top):
-    own[...] = keep[0] + came[0]
-    other_low[...] = keep[1, LOW] + came[1, LOW]
-    other_top[...] = keep[1, TOP] + came[1, TOP]
+    away[...] = jnp.where(even, three, early[1])
+    keep[...] = jnp.where(even, early[1], three)
+    total[...] = jnp.where(even, early[0], early[2]) + came[...]
+
+
+def sum_kernel(keep, came, total, own, other_low, other_top):
+    near = lax.div(lax.axis_index("row"), 2) == lax.div(lax.axis_index("col"), 2)
+    late = keep[...] + came[...]
+    own[...] = jnp.where(near, total[...], late)
+    other = jnp.where(near, late, total[...])
+    other_low[...] = other[LOW, :]
+    other_top[...] = other[TOP, :]
 
 
 def first_kernel(side, one, two, factor, low):
@@ -252,31 +256,43 @@
         at += ref.shape[0]
 
 
-def third_kernel(first, zero, second, low2, top2, factor, mine, theirs, block2, block3, change4, change5, change6, change7, value):
+def zero_kernel(zero, first, low2, top2, factor, mine, theirs, state2, state3, state6, change7):
+    @pl.when(lax.axis_index("row") == 2)
+    def _():
+        own, other = halves()
+        pair = wide(zero[...])
+        state2[...] = low2[...] - product(factor[LOW, columns(0)], pair)
+        state6[...] = top2[...] - product(factor[TOP, columns(0)], pair)
+        for rows, tiles in ((own, mine), (other, theirs)):
+            state3[rows, :] = first[rows, :] - product(stacked(tiles, 0), pair)
+            change7[rows, :] = product(stacked(tiles, 4), pair)
+
+
+def third_kernel(
+    second, state2, state3, state6, state7, factor, mine, theirs,
+    block2, block3, change4, change5, value6, change7, value,
+):
     @pl.when(lax.axis_index("row") == 2)
     def _():
         own, other = halves()
         sides = ((own, mine), (other, theirs))
-        pairs = [wide(zero[...]), wide(second[...])]
-        start = low2[...]
-        for k in range(2):
-            start = start - product(factor[LOW, columns(k)], pairs[k])
-        block2[...] = product(factor[LOW, columns(2)], wide(start))
-        pairs.append(wide(block2[...]))
-        for rows, tiles in sides:
-            start = first[rows, :]
-            for k in range(3):
-                start = start - product(stacked(tiles, k), pairs[k])
-            value[rows, :] = start
+        pairs = {1: wide(second[...])}
+        block2[...] = product(
+            factor[LOW, columns(2)], wide(state2[...] - product(factor[LOW, columns(1)], pairs[1]))
+        )
+        pairs[2] = wide(block2[...])
+        for rows, tiles in sides:
+            start = state3[rows, :] - product(stacked(tiles, 1), pairs[1])
+            value[rows, :] = start - product(stacked(tiles, 2), pairs[2])
         pair = wide(value[...])
         for rows, tiles in sides:
             block3[rows, :] = product(stacked(tiles, 3), pair)
-        pairs.append(wide(block3[...]))
+        pairs[3] = wide(block3[...])
         for rows, tiles in sides:
             change4[rows, :] = sum(product(stacked(tiles, 10 + k - 1), pairs[k]) for k in range(1, 4))
             change5[rows, :] = sum(product(stacked(tiles, 14 + k - 2), pairs[k]) for k in range(2, 4))
-            change7[rows, :] = sum(product(stacked(tiles, 4 + k), pairs[k]) for k in range(4))
-        change6[...] = top2[...] - sum(product(factor[TOP, columns(k)], pairs[k]) for k in range(4))
+            change7[rows, :] = state7[rows, :] + sum(product(stacked(tiles, 4 + k), pairs[k]) for k in range(1, 4))
+        value6[...] = state6[...] - sum(product(factor[TOP, columns(k)], pairs[k]) for k in range(1, 4))
 
 
 def fourth_kernel(
@@ -338,11 +354,11 @@
     middle2 = carried
     edge3 = edges(carried)
 
-    (early,) = call(early_kernel, [(3, *rows)])(past, prev_solution, edge1, edge2, middle2)
-    (send45,) = call(join_kernel, [(2 * tall[0], WIDTH)])(after(edge2, early), send5)
+    early, away = call(early_kernel, [(3, *rows), rows])(past, prev_solution, edge1, edge2, middle2)
+    (send45,) = call(join_kernel, [(2 * tall[0], WIDTH)])(edge2, send5)
     mine45 = move(send45, (1, 2))
-    away, keep = call(late_kernel, [(2, *rows)] * 2)(past, early, edge3, middle3)
-    one, other_low, other_top = call(sum_kernel, [rows, size, size])(keep, swap(away))
+    away, keep, total = call(late_kernel, [rows] * 3)(past, early, swap(away), edge3, middle3)
+    one, other_low, other_top = call(sum_kernel, [rows, size, size])(keep, swap(away), total)
     two_low, two_top = cross(other_low), cross(other_top)
     own8 = move(after(send8, one), (3, 2))
     (low,) = call(first_kernel, [size])(side, one, two_low, factor)
@@ -357,8 +373,9 @@
     second = move(low1, (1, 2))
     (top1,) = call(five_kernel, [size])(first, low1, top, factor)
     value5 = move(top1, (1, 2))
+    states = call(zero_kernel, [size] * 4)(zero, first, low, top, factor, mine, theirs)
     block2, block3, change4, change5, value6, change7 = call(third_kernel, [size] * 6, [pltpu.VMEM(size, jnp.float32)])(
-        first, zero, second, low, top, factor, mine, theirs
+        second, *states, factor, mine, theirs
     )
     last3 = move(block3, (2, 3))
     kept, block4, block5, sent = call(fourth_kernel, [size] * 4)(

time: 86 us -> 85.6 us (level)
    ppermute x17, waiting for transfers between devices: 35.2 us -> 33.6 us  [move(): return lax.ppermute(x, 'row', list(pairs))]
    ppermute x2 -> x3, waiting for transfers between devices: 1.9 us -> 3.05 us  [swap(): return lax.ppermute(x, 'col', [(0, 1), (1, 0), (2, 3), (3, 2)])]
    pallas_call x15 -> x16, Pallas kernels: 8.44 us -> 8.47 us  [run(): pl.pallas_call(kernel, out_shape=[(pltpu.VMEM if inside else jax.ShapeDty...]
  transfers between devices with their start and end apart: 21 -> 22, of which waited for: 9 -> 10; matrix products, arithmetic and copies ran while one was open for 0% -> 0% of each run, Pallas kernels for 9% -> 9%
where the time goes in v8:
time: 85.6 us; the launch traced here: 84.5 us
  waiting for transfers between devices  40.2 us (47%)
  starting transfers between devices  35.4 us (41%)
  Pallas kernels  8.47 us (10%)
    ppermute x17, waiting for transfers between devices, move(): return lax.ppermute(x, 'row', list(pairs))  33.6 us
    ppermute x17, starting transfers between devices, move(): return lax.ppermute(x, 'row', list(pairs))  33 us
    pallas_call x16, Pallas kernels, run(): pl.pallas_call(kernel, out_shape=[(pltpu.VMEM if inside else jax.ShapeDty...  8.47 us
    ppermute x2, waiting for transfers between devices, cross(): return lax.ppermute(x, 'col', [(0, 2), (2, 0), (1, 3), (3, 1)])  3.58 us
    ppermute x3, waiting for transfers between devices, swap(): return lax.ppermute(x, 'col', [(0, 1), (1, 0), (2, 3), (3, 2)])  3.05 us
    ppermute x2, starting transfers between devices, cross(): return lax.ppermute(x, 'col', [(0, 2), (2, 0), (1, 3), (3, 1)])  2.16 us
  transfers between devices with their start and end apart: 22, of which 10 were waited for; matrix products, arithmetic and copies ran while one was open for 0% of the time, Pallas kernels for 9%

profile of v8, /device:TPU:0, one launch (start us, length us, event | category | flops | bytes accessed | tf_op | source)
XLA Modules:
  0.0 84.5 jit_solution(11753674562650029902)
XLA Ops:
  0.0 3.0 %collective-permute-start.1 = (f32[1024,128]{1,0:T(8,128)}, f32[1024,128]{1,0:T(8,128)S(1)}, u32[]{:S(2)}, u32[]{:S(2)}) collective-permute-start(f32[1024,128]{1,0:T(8,128)} %own.1), channel_id=1, source_target_pairs={{0,4},{4,0},{8,12},{12,8},{1,5},{5,1},{9,13},{13,9},{2,6},{6,2},{1... | collective-permute-start | bytes 1572872 | tf_op jit(solution)/shard_map/ppermute | solution.py:323
  3.7 11.4 %collective-permute-done.1.edge1 = f32[1024,128]{1,0:T(8,128)S(1)} collective-permute-done((f32[1024,128]{1,0:T(8,128)}, f32[1024,128]{1,0:T(8,128)S(1)}, u32[]{:S(2)}, u32[]{:S(2)}) %collective-permute-start.1) | collective-permute-done | bytes 524320 | tf_op jit(solution)/shard_map/ppermute | solution.py:323
  15.9 1.2 %shard_map.46 = f32[1024,128]{1,0:T(8,128)S(1)} custom-call(f32[1024,128]{1,0:T(8,128)S(1)} %copy.7.x_in, f32[512,1536]{1,0:T(8,128)} %factor.3), custom_call_target="tpu_custom_call", output_to_operand_aliasing={{}: (0, {})} | custom-call | tf_op jit(solution)/shard_map/pallas_call | solution.py:77
  17.1 3.6 %collective-permute-start.2 = (f32[1024,128]{1,0:T(8,128)S(1)}, f32[1024,128]{1,0:T(8,128)S(1)}, u32[]{:S(2)}, u32[]{:S(2)}) collective-permute-start(f32[1024,128]{1,0:T(8,128)S(1)} %shard_map.46), channel_id=1, source_target_pairs={{0,4},{4,0},{8,12},{12,8},{1,5},{5,1},{9,13},{13,9},{2,6},{6,2},{1... | collective-permute-start | bytes 1572872 | tf_op jit(solution)/shard_map/ppermute | solution.py:323
  20.6 3.2 %shard_map.47 = (f32[512,1024]{1,0:T(8,128)S(1)}, f32[512,1536]{1,0:T(8,128)S(1)}, f32[512,128]{1,0:T(8,128)S(1)}, f32[1024,128]{1,0:T(8,128)S(1)}, f32[1024,128]{1,0:T(8,128)S(1)}, /*index=5*/f32[512,128]{1,0:T(8,128)S(1)}) custom-call(f32[512,1024]{1,0:T(8,128)} %past, f32[512,1536]{1,0:T(8,128)} %factor.3, f32[512,512]{1,0:T(8,128)} %side.1), custom_call_target="tpu_custom_call" | custom-call | tf_op jit(solution)/shard_map/pallas_call | solution.py:77
  23.8 7.7 %collective-permute-start.5 = (f32[1024,128]{1,0:T(8,128)S(1)}, f32[1024,128]{1,0:T(8,128)S(1)}, u32[]{:S(2)}, u32[]{:S(2)}) collective-permute-start(f32[1024,128]{1,0:T(8,128)S(1)} %shard_map.48.middle2), channel_id=1, source_target_pairs={{0,4},{4,0},{8,12},{12,8},{1,5},{5,1},{9,13},{13,9},{2,6},{6,2},{1... | collective-permute-start | bytes 1572872 | tf_op jit(solution)/shard_map/ppermute | solution.py:323
  31.6 0.7 collective-permute-done.2.edge2.refs_0_
  32.3 0.7 collective-permute-start.13
  33.1 1.8 %shard_map.49 = (f32[3,512,128]{2,1,0:T(8,128)S(1)}, f32[512,128]{1,0:T(8,128)S(1)}) custom-call(f32[512,1024]{1,0:T(8,128)S(1)} %get-tuple-element.39.past, f32[1024,128]{1,0:T(8,128)S(1)} %copy-done, f32[1024,128]{1,0:T(8,128)S(1)} %collective-permute-done.1.edge1, f32[1024,128]{1,0:T(8,128)S(1)} %collective-permute-done.2.edge2.refs_0_, ...), custom_call_target="tpu_custom_call" | custom-call | tf_op jit(solution)/shard_map/pallas_call | solution.py:77
  35.0 1.5 %collective-permute-done.4.came = f32[512,128]{1,0:T(8,128)S(1)} collective-permute-done((f32[512,128]{1,0:T(8,128)S(1)}, f32[512,128]{1,0:T(8,128)S(1)}, u32[]{:S(2)}, u32[]{:S(2)}) %collective-permute-start.4) | collective-permute-done | bytes 262176 | tf_op jit(solution)/shard_map/ppermute | solution.py:326
  36.5 6.1 %collective-permute-done.5.edge3.refs_1_ = f32[1024,128]{1,0:T(8,128)S(1)} collective-permute-done((f32[1024,128]{1,0:T(8,128)S(1)}, f32[1024,128]{1,0:T(8,128)S(1)}, u32[]{:S(2)}, u32[]{:S(2)}) %collective-permute-start.5) | collective-permute-done | bytes 524320 | tf_op jit(solution)/shard_map/ppermute | solution.py:323
  42.6 0.7 shard_map.50
  43.5 1.5 %collective-permute-done.6.came = f32[512,128]{1,0:T(8,128)S(1)} collective-permute-done((f32[512,128]{1,0:T(8,128)S(1)}, f32[512,128]{1,0:T(8,128)S(1)}, u32[]{:S(2)}, u32[]{:S(2)}) %collective-permute-start.6) | collective-permute-done | bytes 262176 | tf_op jit(solution)/shard_map/ppermute | solution.py:326
  45.0 1.6 %collective-permute-start.7 = (f32[256,128]{1,0:T(8,128)S(1)}, f32[256,128]{1,0:T(8,128)S(1)}, u32[]{:S(2)}, u32[]{:S(2)}) collective-permute-start(f32[256,128]{1,0:T(8,128)S(1)} %get-tuple-element.47), channel_id=1, source_target_pairs={{0,2},{2,0},{1,3},{3,1},{4,6},{6,4},{5,7},{7,5},{8,10},{10,8},{9,1... | collective-permute-start | bytes 393224 | tf_op jit(solution)/shard_map/ppermute | solution.py:329
  47.9 3.6 %collective-permute-done.7.two = f32[256,128]{1,0:T(8,128)S(1)} collective-permute-done((f32[256,128]{1,0:T(8,128)S(1)}, f32[256,128]{1,0:T(8,128)S(1)}, u32[]{:S(2)}, u32[]{:S(2)}) %collective-permute-start.7) | collective-permute-done | bytes 131104 | tf_op jit(solution)/shard_map/ppermute | solution.py:329
  51.7 3.4 %collective-permute-start.8 = (f32[256,128]{1,0:T(8,128)S(1)}, f32[256,128]{1,0:T(8,128)S(1)}, u32[]{:S(2)}, u32[]{:S(2)}) collective-permute-start(f32[256,128]{1,0:T(8,128)S(1)} %shard_map.52.low.low_in.low2), channel_id=1, source_target_pairs={{0,4},{12,8},{1,5},{13,9},{2,6},{14,10},{3,7},{15,11},{16,20},{28,... | collective-permute-start | bytes 393224 | tf_op jit(solution)/shard_map/ppermute | solution.py:323
  55.1 1.3 %collective-permute-start.11 = (f32[256,128]{1,0:T(8,128)S(1)}, f32[256,128]{1,0:T(8,128)S(1)}, u32[]{:S(2)}, u32[]{:S(2)}) collective-permute-start(f32[256,128]{1,0:T(8,128)S(1)} %shard_map.52.low.low_in.low2), channel_id=1, source_target_pairs={{0,8},{1,9},{2,10},{3,11},{16,24},{17,25},{18,26},{19,27}} | collective-permute-start | bytes 393224 | tf_op jit(solution)/shard_map/ppermute | solution.py:323
  56.7 1.8 %collective-permute-done.8.solved.first.zero = f32[256,128]{1,0:T(8,128)S(1)} collective-permute-done((f32[256,128]{1,0:T(8,128)S(1)}, f32[256,128]{1,0:T(8,128)S(1)}, u32[]{:S(2)}, u32[]{:S(2)}) %collective-permute-start.8) | collective-permute-done | bytes 131104 | tf_op jit(solution)/shard_map/ppermute | solution.py:323
  58.5 1.4 %collective-permute-done.11.zero = f32[256,128]{1,0:T(8,128)S(1)} collective-permute-done((f32[256,128]{1,0:T(8,128)S(1)}, f32[256,128]{1,0:T(8,128)S(1)}, u32[]{:S(2)}, u32[]{:S(2)}) %collective-permute-start.11) | collective-permute-done | bytes 131104 | tf_op jit(solution)/shard_map/ppermute | solution.py:323
  60.8 5.9 %collective-permute-start.16 = (f32[256,128]{1,0:T(8,128)S(1)}, f32[256,128]{1,0:T(8,128)S(1)}, u32[]{:S(2)}, u32[]{:S(2)}) collective-permute-start(f32[256,128]{1,0:T(8,128)S(1)} %shard_map.53.top2.top_in), channel_id=1, source_target_pairs={{0,8},{1,9},{2,10},{3,11},{16,24},{17,25},{18,26},{19,27}} | collective-permute-start | bytes 393224 | tf_op jit(solution)/shard_map/ppermute | solution.py:323
  68.2 1.9 %collective-permute-done.16.value4 = f32[256,128]{1,0:T(8,128)S(1)} collective-permute-done((f32[256,128]{1,0:T(8,128)S(1)}, f32[256,128]{1,0:T(8,128)S(1)}, u32[]{:S(2)}, u32[]{:S(2)}) %collective-permute-start.16) | collective-permute-done | bytes 131104 | tf_op jit(solution)/shard_map/ppermute | solution.py:323
  70.2 1.3 %collective-permute-start.18 = (f32[256,128]{1,0:T(8,128)S(1)}, f32[256,128]{1,0:T(8,128)S(1)}, u32[]{:S(2)}, u32[]{:S(2)}) collective-permute-start(f32[256,128]{1,0:T(8,128)S(1)} %get-tuple-element.63), channel_id=1, source_target_pairs={{8,0},{9,1},{10,2},{11,3},{24,16},{25,17},{26,18},{27,19}} | collective-permute-start | bytes 393224 | tf_op jit(solution)/shard_map/ppermute | solution.py:323
  73.5 10.2 %collective-permute-done.18.block4 = f32[256,128]{1,0:T(8,128)S(1)} collective-permute-done((f32[256,128]{1,0:T(8,128)S(1)}, f32[256,128]{1,0:T(8,128)S(1)}, u32[]{:S(2)}, u32[]{:S(2)}) %collective-permute-start.18) | collective-permute-done | bytes 131104 | tf_op jit(solution)/shard_map/ppermute | solution.py:323
  83.7 0.7 shard_map.61
  (39 shorter events, 7.8 us)
Async XLA Ops:
  0.0 15.2 %collective-permute-start.1 = (f32[1024,128]{1,0:T(8,128)}, f32[1024,128]{1,0:T(8,128)S(1)}, u32[]{:S(2)}, u32[]{:S(2)}) collective-permute-start(f32[1024,128]{1,0:T(8,128)} %own.1), channel_id=1, source_target_pairs={{0,4},{4,0},{8,12},{12,8},{1,5},{5,1},{9,13},{13,9},{2,6},{6,2},{1... | collective-permute-start | bytes 1572872 | tf_op jit(solution)/shard_map/ppermute | solution.py:323
  3.0 12.8 %collective-permute-start = (f32[1024,128]{1,0:T(8,128)}, f32[1024,128]{1,0:T(8,128)S(1)}, u32[]{:S(2)}, u32[]{:S(2)}) collective-permute-start(f32[1024,128]{1,0:T(8,128)} %own.1), channel_id=1, source_target_pairs={{4,8},{8,4},{5,9},{9,5},{6,10},{10,6},{7,11},{11,7},{20,24},{24,20... | collective-permute-start | bytes 1572872 | tf_op jit(solution)/shard_map/ppermute | solution.py:323
  15.2 8.6 %collective-permute-start.3 = (f32[1024,128]{1,0:T(8,128)S(1)}, f32[1024,128]{1,0:T(8,128)S(1)}, u32[]{:S(2)}, u32[]{:S(2)}) collective-permute-start(f32[1024,128]{1,0:T(8,128)S(1)} %collective-permute-done.1.edge1), channel_id=1, source_target_pairs={{4,8},{8,4},{5,9},{9,5},{6,10},{10,6},{7,11},{11,7},{20,24},{24,20... | collective-permute-start | bytes 1572872 | tf_op jit(solution)/shard_map/ppermute | solution.py:323
  17.1 15.2 %collective-permute-start.2 = (f32[1024,128]{1,0:T(8,128)S(1)}, f32[1024,128]{1,0:T(8,128)S(1)}, u32[]{:S(2)}, u32[]{:S(2)}) collective-permute-start(f32[1024,128]{1,0:T(8,128)S(1)} %shard_map.46), channel_id=1, source_target_pairs={{0,4},{4,0},{8,12},{12,8},{1,5},{5,1},{9,13},{13,9},{2,6},{6,2},{1... | collective-permute-start | bytes 1572872 | tf_op jit(solution)/shard_map/ppermute | solution.py:323
  23.8 9.3 %copy-start = (f32[1024,128]{1,0:T(8,128)S(1)}, f32[1024,128]{1,0:T(8,128)}, u32[]{:S(2)}) copy-start(f32[1024,128]{1,0:T(8,128)} %own.1) | copy-start | bytes 1572868
  23.8 18.8 %collective-permute-start.5 = (f32[1024,128]{1,0:T(8,128)S(1)}, f32[1024,128]{1,0:T(8,128)S(1)}, u32[]{:S(2)}, u32[]{:S(2)}) collective-permute-start(f32[1024,128]{1,0:T(8,128)S(1)} %shard_map.48.middle2), channel_id=1, source_target_pairs={{0,4},{4,0},{8,12},{12,8},{1,5},{5,1},{9,13},{13,9},{2,6},{6,2},{1... | collective-permute-start | bytes 1572872 | tf_op jit(solution)/shard_map/ppermute | solution.py:323
  32.3 27.6 %collective-permute-start.13 = (f32[2048,128]{1,0:T(8,128)S(1)}, f32[2048,128]{1,0:T(8,128)S(1)}, u32[]{:S(2)}, u32[]{:S(2)}) collective-permute-start(f32[2048,128]{1,0:T(8,128)S(1)} %shard_map.55), channel_id=1, source_target_pairs={{4,8},{5,9},{6,10},{7,11},{20,24},{21,25},{22,26},{23,27}} | collective-permute-start | bytes 3145736 | tf_op jit(solution)/shard_map/ppermute | solution.py:323
  34.9 1.6 %collective-permute-start.4 = (f32[512,128]{1,0:T(8,128)S(1)}, f32[512,128]{1,0:T(8,128)S(1)}, u32[]{:S(2)}, u32[]{:S(2)}) collective-permute-start(f32[512,128]{1,0:T(8,128)S(1)} %get-tuple-element.42), channel_id=1, source_target_pairs={{0,1},{1,0},{2,3},{3,2},{4,5},{5,4},{6,7},{7,6},{8,9},{9,8},{10,11... | collective-permute-start | bytes 786440 | tf_op jit(solution)/shard_map/ppermute | solution.py:326
  43.4 1.6 %collective-permute-start.6 = (f32[512,128]{1,0:T(8,128)S(1)}, f32[512,128]{1,0:T(8,128)S(1)}, u32[]{:S(2)}, u32[]{:S(2)}) collective-permute-start(f32[512,128]{1,0:T(8,128)S(1)} %get-tuple-element.44), channel_id=1, source_target_pairs={{0,1},{1,0},{2,3},{3,2},{4,5},{5,4},{6,7},{7,6},{8,9},{9,8},{10,11... | collective-permute-start | bytes 786440 | tf_op jit(solution)/shard_map/ppermute | solution.py:326
  45.0 6.4 %collective-permute-start.7 = (f32[256,128]{1,0:T(8,128)S(1)}, f32[256,128]{1,0:T(8,128)S(1)}, u32[]{:S(2)}, u32[]{:S(2)}) collective-permute-start(f32[256,128]{1,0:T(8,128)S(1)} %get-tuple-element.47), channel_id=1, source_target_pairs={{0,2},{2,0},{1,3},{3,1},{4,6},{6,4},{5,7},{7,5},{8,10},{10,8},{9,1... | collective-permute-start | bytes 393224 | tf_op jit(solution)/shard_map/ppermute | solution.py:329
  46.6 13.3 %collective-permute-start.12 = (f32[512,128]{1,0:T(8,128)S(1)}, f32[512,128]{1,0:T(8,128)S(1)}, u32[]{:S(2)}, u32[]{:S(2)}) collective-permute-start(f32[512,128]{1,0:T(8,128)S(1)} %get-tuple-element.52), channel_id=1, source_target_pairs={{12,8},{13,9},{14,10},{15,11},{28,24},{29,25},{30,26},{31,27}} | collective-permute-start | bytes 786440 | tf_op jit(solution)/shard_map/ppermute | solution.py:323
  47.3 9.2 %collective-permute-start.9 = (f32[256,128]{1,0:T(8,128)S(1)}, f32[256,128]{1,0:T(8,128)S(1)}, u32[]{:S(2)}, u32[]{:S(2)}) collective-permute-start(f32[256,128]{1,0:T(8,128)S(1)} %get-tuple-element.49), channel_id=1, source_target_pairs={{0,2},{2,0},{1,3},{3,1},{4,6},{6,4},{5,7},{7,5},{8,10},{10,8},{9,1... | collective-permute-start | bytes 393224 | tf_op jit(solution)/shard_map/ppermute | solution.py:329
  51.7 6.8 %collective-permute-start.8 = (f32[256,128]{1,0:T(8,128)S(1)}, f32[256,128]{1,0:T(8,128)S(1)}, u32[]{:S(2)}, u32[]{:S(2)}) collective-permute-start(f32[256,128]{1,0:T(8,128)S(1)} %shard_map.52.low.low_in.low2), channel_id=1, source_target_pairs={{0,4},{12,8},{1,5},{13,9},{2,6},{14,10},{3,7},{15,11},{16,20},{28,... | collective-permute-start | bytes 393224 | tf_op jit(solution)/shard_map/ppermute | solution.py:323
  55.1 4.8 %collective-permute-start.11 = (f32[256,128]{1,0:T(8,128)S(1)}, f32[256,128]{1,0:T(8,128)S(1)}, u32[]{:S(2)}, u32[]{:S(2)}) collective-permute-start(f32[256,128]{1,0:T(8,128)S(1)} %shard_map.52.low.low_in.low2), channel_id=1, source_target_pairs={{0,8},{1,9},{2,10},{3,11},{16,24},{17,25},{18,26},{19,27}} | collective-permute-start | bytes 393224 | tf_op jit(solution)/shard_map/ppermute | solution.py:323
  60.1 8.1 %collective-permute-start.14 = (f32[4608,128]{1,0:T(8,128)S(1)}, f32[4608,128]{1,0:T(8,128)S(1)}, u32[]{:S(2)}, u32[]{:S(2)}) collective-permute-start(f32[4608,128]{1,0:T(8,128)S(1)} %shard_map.56.mine), channel_id=1, source_target_pairs={{0,1},{1,0},{2,3},{3,2},{4,5},{5,4},{6,7},{7,6},{8,9},{9,8},{10,11... | collective-permute-start | bytes 7077896 | tf_op jit(solution)/shard_map/ppermute | solution.py:326
  60.2 8.0 %collective-permute-start.10 = (f32[256,128]{1,0:T(8,128)S(1)}, f32[256,128]{1,0:T(8,128)S(1)}, u32[]{:S(2)}, u32[]{:S(2)}) collective-permute-start(f32[256,128]{1,0:T(8,128)S(1)} %shard_map.54.one.low1), channel_id=1, source_target_pairs={{4,8},{5,9},{6,10},{7,11},{20,24},{21,25},{22,26},{23,27}} | collective-permute-start | bytes 393224 | tf_op jit(solution)/shard_map/ppermute | solution.py:323
  60.8 9.3 %collective-permute-start.16 = (f32[256,128]{1,0:T(8,128)S(1)}, f32[256,128]{1,0:T(8,128)S(1)}, u32[]{:S(2)}, u32[]{:S(2)}) collective-permute-start(f32[256,128]{1,0:T(8,128)S(1)} %shard_map.53.top2.top_in), channel_id=1, source_target_pairs={{0,8},{1,9},{2,10},{3,11},{16,24},{17,25},{18,26},{19,27}} | collective-permute-start | bytes 393224 | tf_op jit(solution)/shard_map/ppermute | solution.py:323
  66.8 3.4 %collective-permute-start.17 = (f32[256,128]{1,0:T(8,128)S(1)}, f32[256,128]{1,0:T(8,128)S(1)}, u32[]{:S(2)}, u32[]{:S(2)}) collective-permute-start(f32[256,128]{1,0:T(8,128)S(1)} %shard_map.53.top2.top_in), channel_id=1, source_target_pairs={{12,8},{13,9},{14,10},{15,11},{28,24},{29,25},{30,26},{31,27}} | collective-permute-start | bytes 393224 | tf_op jit(solution)/shard_map/ppermute | solution.py:323
  67.5 2.7 %collective-permute-start.15 = (f32[256,128]{1,0:T(8,128)S(1)}, f32[256,128]{1,0:T(8,128)S(1)}, u32[]{:S(2)}, u32[]{:S(2)}) collective-permute-start(f32[256,128]{1,0:T(8,128)S(1)} %shard_map.59), channel_id=1, source_target_pairs={{4,8},{5,9},{6,10},{7,11},{20,24},{21,25},{22,26},{23,27}} | collective-permute-start | bytes 393224 | tf_op jit(solution)/shard_map/ppermute | solution.py:323
  70.2 13.5 %collective-permute-start.18 = (f32[256,128]{1,0:T(8,128)S(1)}, f32[256,128]{1,0:T(8,128)S(1)}, u32[]{:S(2)}, u32[]{:S(2)}) collective-permute-start(f32[256,128]{1,0:T(8,128)S(1)} %get-tuple-element.63), channel_id=1, source_target_pairs={{8,0},{9,1},{10,2},{11,3},{24,16},{25,17},{26,18},{27,19}} | collective-permute-start | bytes 393224 | tf_op jit(solution)/shard_map/ppermute | solution.py:323
  71.5 12.3 %collective-permute-start.19 = (f32[256,128]{1,0:T(8,128)S(1)}, f32[256,128]{1,0:T(8,128)S(1)}, u32[]{:S(2)}, u32[]{:S(2)}) collective-permute-start(f32[256,128]{1,0:T(8,128)S(1)} %get-tuple-element.64), channel_id=1, source_target_pairs={{8,4},{9,5},{10,6},{11,7},{24,20},{25,21},{26,22},{27,23}} | collective-permute-start | bytes 393224 | tf_op jit(solution)/shard_map/ppermute | solution.py:323
  72.1 11.6 %collective-permute-start.21 = (f32[256,128]{1,0:T(8,128)S(1)}, f32[256,128]{1,0:T(8,128)S(1)}, u32[]{:S(2)}, u32[]{:S(2)}) collective-permute-start(f32[256,128]{1,0:T(8,128)S(1)} %get-tuple-element.66), channel_id=1, source_target_pairs={{8,12},{9,13},{10,14},{11,15},{24,28},{25,29},{26,30},{27,31}} | collective-permute-start | bytes 393224 | tf_op jit(solution)/shard_map/ppermute | solution.py:323
  72.8 10.9 %collective-permute-start.20 = (f32[256,128]{1,0:T(8,128)S(1)}, f32[256,128]{1,0:T(8,128)S(1)}, u32[]{:S(2)}, u32[]{:S(2)}) collective-permute-start(f32[256,128]{1,0:T(8,128)S(1)} %get-tuple-element.65), channel_id=1, source_target_pairs={{8,12},{9,13},{10,14},{11,15},{24,28},{25,29},{26,30},{27,31}} | collective-permute-start | bytes 393224 | tf_op jit(solution)/shard_map/ppermute | solution.py:323

commit v9 on v8

--- a/solution.py
+++ b/solution.py
@@ -64,6 +64,14 @@
     return both[:, :WIDTH] + both[:, WIDTH:]
 
 
+def square(one, two):
+    high, low = split(one)
+    pair = wide(two)
+    both = jnp.dot(high, pair, preferred_element_type=jnp.float32)
+    both = both + jnp.dot(low, pair, preferred_element_type=jnp.float32)
+    return both[:, :BLOCK] + both[:, BLOCK:]
+
+
 def columns(k):
     return slice(k * BLOCK, (k + 1) * BLOCK)
 
@@ -192,19 +200,29 @@
         low[...] = product(factor[LOW, columns(0)], wide(low[...]))
 
 
-def top_kernel(side, one, two, factor, low, top):
+def top_kernel(side, one, two, factor, low, top, base):
+    row_index = lax.axis_index("row")
     top[...] = side[TOP, :] - (one[TOP, :] + two[...])
 
+    @pl.when(row_index == 1)
+    def _():
+        base[...] = product(factor[LOW, columns(1)], wide(low[...]))
+
     @pl.when(lax.axis_index("row") == 0)
     def _():
         top[...] = top[...] - product(factor[TOP, columns(0)], wide(low[...]))
 
 
-def second_kernel(solved, low_in, factor, low):
+def joint_kernel(factor, joint):
     @pl.when(lax.axis_index("row") == 1)
     def _():
-        value = low_in[...] - product(factor[LOW, columns(0)], wide(solved[...]))
-        low[...] = product(factor[LOW, columns(1)], wide(value))
+        joint[...] = square(factor[LOW, columns(1)], factor[LOW, columns(0)])
+
+
+def second_kernel(solved, base, joint, low):
+    @pl.when(lax.axis_index("row") == 1)
+    def _():
+        low[...] = base[...] - product(joint[...], wide(solved[...]))
 
 
 def five_kernel(zero, one, top_in, factor, top):
@@ -256,7 +274,7 @@
         at += ref.shape[0]
 
 
-def zero_kernel(zero, first, low2, top2, factor, mine, theirs, state2, state3, state6, change7):
+def zero_kernel(zero, first, low2, top2, factor, mine, theirs, state2, state3, state6, change7, joint, tile):
     @pl.when(lax.axis_index("row") == 2)
     def _():
         own, other = halves()
@@ -266,6 +284,13 @@
         for rows, tiles in ((own, mine), (other, theirs)):
             state3[rows, :] = first[rows, :] - product(stacked(tiles, 0), pair)
             change7[rows, :] = product(stacked(tiles, 4), pair)
+        sides = ((own, mine), (other, theirs))
+        for rows, tiles in sides:
+            tile[0, rows, :] = stacked(tiles, 13)
+        for rows, tiles in sides:
+            tile[1, rows, :] = square(stacked(tiles, 16), tile[0])
+        for rows, tiles in sides:
+            joint[rows, :] = square(stacked(tiles, 17), tile[1])
 
 
 def third_kernel(
@@ -296,22 +321,18 @@
 
 
 def fourth_kernel(
-    change4, change5, value6, change7, factor, mine, theirs, value5, value4, top3, kept, block4, block5, sent
+    change4, change5, value6, change7, factor, mine, theirs, joint, value5, value4, top3, kept, block4, block5, sent
 ):
     @pl.when(lax.axis_index("row") == 2)
     def _():
         own, other = halves()
         sides = ((own, mine), (other, theirs))
-        pair = wide(value4[...] - change4[...])
-        for rows, tiles in sides:
-            block4[rows, :] = product(stacked(tiles, 13), pair)
-        four = wide(block4[...])
-        for rows, tiles in sides:
-            sent[rows, :] = value5[rows, :] - change5[rows, :] - product(stacked(tiles, 16), four)
-        pair = wide(sent[...])
-        for rows, tiles in sides:
-            block5[rows, :] = product(stacked(tiles, 17), pair)
-        five = wide(block5[...])
+        pair4 = wide(value4[...] - change4[...])
+        pair5 = wide(value5[...] - change5[...])
+        for rows, tiles in sides:
+            block4[rows, :] = product(stacked(tiles, 13), pair4)
+            block5[rows, :] = product(stacked(tiles, 17), pair5) - product(joint[rows, :], pair4)
+        four, five = wide(block4[...]), wide(block5[...])
         kept[...] = value6[...] - product(factor[TOP, columns(4)], four) - product(factor[TOP, columns(5)], five)
         for rows, tiles in sides:
             start = top3[rows, :] - change7[rows, :] - product(stacked(tiles, 8), four)
@@ -357,29 +378,31 @@
     early, away = call(early_kernel, [(3, *rows), rows])(past, prev_solution, edge1, edge2, middle2)
     (send45,) = call(join_kernel, [(2 * tall[0], WIDTH)])(edge2, send5)
     mine45 = move(send45, (1, 2))
-    away, keep, total = call(late_kernel, [rows] * 3)(past, early, swap(away), edge3, middle3)
+    tile = (BLOCK, BLOCK)
+    (joint1,) = call(joint_kernel, [tile])(after(factor, early))
+    away, keep, total = call(late_kernel, [rows] * 3)(past, after(early, joint1), swap(away), edge3, middle3)
     one, other_low, other_top = call(sum_kernel, [rows, size, size])(keep, swap(away), total)
     two_low, two_top = cross(other_low), cross(other_top)
     own8 = move(after(send8, one), (3, 2))
     (low,) = call(first_kernel, [size])(side, one, two_low, factor)
     first = move(low, (0, 1), (3, 2))
     zero = move(low, (0, 2))
-    (top,) = call(top_kernel, [size])(side, one, two_top, factor, low)
+    top, base = call(top_kernel, [size] * 2)(side, one, two_top, factor, low)
     value4 = move(top, (0, 2))
     top3 = move(top, (3, 2))
     (mine,) = call(join_kernel, [(4 * tall[0] + rows[0], WIDTH)])(edge2, edge3, own8, after(mine45, first, zero, top))
     theirs = swap(mine)
-    (low1,) = call(second_kernel, [size])(first, after(low, top), factor)
+    (low1,) = call(second_kernel, [size])(first, base, joint1)
     second = move(low1, (1, 2))
     (top1,) = call(five_kernel, [size])(first, low1, top, factor)
     value5 = move(top1, (1, 2))
-    states = call(zero_kernel, [size] * 4)(zero, first, low, top, factor, mine, theirs)
+    *states, joint5 = call(zero_kernel, [size] * 4 + [tile], [pltpu.VMEM((2, *tile), jnp.float32)])(zero, first, low, top, factor, mine, theirs)
     block2, block3, change4, change5, value6, change7 = call(third_kernel, [size] * 6, [pltpu.VMEM(size, jnp.float32)])(
         second, *states, factor, mine, theirs
     )
     last3 = move(block3, (2, 3))
     kept, block4, block5, sent = call(fourth_kernel, [size] * 4)(
-        change4, change5, value6, change7, factor, mine, theirs, value5, value4, top3
+        change4, change5, value6, change7, factor, mine, theirs, joint5, value5, value4, top3
     )
     last7 = move(sent, (2, 3))
     block5 = move(block5, (2, 1))

time: 85.6 us -> 85.3 us (level)
    pallas_call x16 -> x17, Pallas kernels: 8.47 us -> 8.49 us  [run(): pl.pallas_call(kernel, out_shape=[(pltpu.VMEM if inside else jax.ShapeDty...]
where the time goes in v9:
time: 85.3 us; the launch traced here: 84.1 us
  waiting for transfers between devices  39.9 us (47%)
  starting transfers between devices  35.4 us (42%)
  Pallas kernels  8.49 us (10%)
    ppermute x17, waiting for transfers between devices, move(): return lax.ppermute(x, 'row', list(pairs))  33.3 us
    ppermute x17, starting transfers between devices, move(): return lax.ppermute(x, 'row', list(pairs))  33 us
    pallas_call x17, Pallas kernels, run(): pl.pallas_call(kernel, out_shape=[(pltpu.VMEM if inside else jax.ShapeDty...  8.49 us
    ppermute x2, waiting for transfers between devices, cross(): return lax.ppermute(x, 'col', [(0, 2), (2, 0), (1, 3), (3, 1)])  3.58 us
    ppermute x3, waiting for transfers between devices, swap(): return lax.ppermute(x, 'col', [(0, 1), (1, 0), (2, 3), (3, 2)])  3.02 us
    ppermute x2, starting transfers between devices, cross(): return lax.ppermute(x, 'col', [(0, 2), (2, 0), (1, 3), (3, 1)])  2.16 us
  transfers between devices with their start and end apart: 22, of which 10 were waited for; matrix products, arithmetic and copies ran while one was open for 0% of the time, Pallas kernels for 9%

profile of v9, /device:TPU:0, one launch (start us, length us, event | category | flops | bytes accessed | tf_op | source)
XLA Modules:
  0.0 84.1 jit_solution(224614895415414007)
XLA Ops:
  0.0 3.0 %collective-permute-start.1 = (f32[1024,128]{1,0:T(8,128)}, f32[1024,128]{1,0:T(8,128)S(1)}, u32[]{:S(2)}, u32[]{:S(2)}) collective-permute-start(f32[1024,128]{1,0:T(8,128)} %own.1), channel_id=1, source_target_pairs={{0,4},{4,0},{8,12},{12,8},{1,5},{5,1},{9,13},{13,9},{2,6},{6,2},{1... | collective-permute-start | bytes 1572872 | tf_op jit(solution)/shard_map/ppermute | solution.py:344
  3.7 11.4 %collective-permute-done.1.edge1 = f32[1024,128]{1,0:T(8,128)S(1)} collective-permute-done((f32[1024,128]{1,0:T(8,128)}, f32[1024,128]{1,0:T(8,128)S(1)}, u32[]{:S(2)}, u32[]{:S(2)}) %collective-permute-start.1) | collective-permute-done | bytes 524320 | tf_op jit(solution)/shard_map/ppermute | solution.py:344
  15.9 1.2 %shard_map.46 = f32[1024,128]{1,0:T(8,128)S(1)} custom-call(f32[1024,128]{1,0:T(8,128)S(1)} %copy.7.x_in, f32[512,1536]{1,0:T(8,128)} %factor.3), custom_call_target="tpu_custom_call", output_to_operand_aliasing={{}: (0, {})} | custom-call | tf_op jit(solution)/shard_map/pallas_call | solution.py:85
  17.1 3.6 %collective-permute-start.2 = (f32[1024,128]{1,0:T(8,128)S(1)}, f32[1024,128]{1,0:T(8,128)S(1)}, u32[]{:S(2)}, u32[]{:S(2)}) collective-permute-start(f32[1024,128]{1,0:T(8,128)S(1)} %shard_map.46), channel_id=1, source_target_pairs={{0,4},{4,0},{8,12},{12,8},{1,5},{5,1},{9,13},{13,9},{2,6},{6,2},{1... | collective-permute-start | bytes 1572872 | tf_op jit(solution)/shard_map/ppermute | solution.py:344
  20.6 3.2 %shard_map.47 = (f32[512,1024]{1,0:T(8,128)S(1)}, f32[512,1536]{1,0:T(8,128)S(1)}, f32[512,128]{1,0:T(8,128)S(1)}, f32[1024,128]{1,0:T(8,128)S(1)}, f32[1024,128]{1,0:T(8,128)S(1)}, /*index=5*/f32[512,128]{1,0:T(8,128)S(1)}) custom-call(f32[512,1024]{1,0:T(8,128)} %past, f32[512,1536]{1,0:T(8,128)} %factor.3, f32[512,512]{1,0:T(8,128)} %side.1), custom_call_target="tpu_custom_call" | custom-call | tf_op jit(solution)/shard_map/pallas_call | solution.py:85
  23.8 7.7 %collective-permute-start.5 = (f32[1024,128]{1,0:T(8,128)S(1)}, f32[1024,128]{1,0:T(8,128)S(1)}, u32[]{:S(2)}, u32[]{:S(2)}) collective-permute-start(f32[1024,128]{1,0:T(8,128)S(1)} %shard_map.48.middle2), channel_id=1, source_target_pairs={{0,4},{4,0},{8,12},{12,8},{1,5},{5,1},{9,13},{13,9},{2,6},{6,2},{1... | collective-permute-start | bytes 1572872 | tf_op jit(solution)/shard_map/ppermute | solution.py:344
  31.6 0.7 collective-permute-done.2.edge2.refs_0_
  32.3 0.7 collective-permute-start.13
  33.1 1.8 %shard_map.49 = (f32[3,512,128]{2,1,0:T(8,128)S(1)}, f32[512,128]{1,0:T(8,128)S(1)}) custom-call(f32[512,1024]{1,0:T(8,128)S(1)} %get-tuple-element.43.past, f32[1024,128]{1,0:T(8,128)S(1)} %copy-done, f32[1024,128]{1,0:T(8,128)S(1)} %collective-permute-done.1.edge1, f32[1024,128]{1,0:T(8,128)S(1)} %collective-permute-done.2.edge2.refs_0_, ...), custom_call_target="tpu_custom_call" | custom-call | tf_op jit(solution)/shard_map/pallas_call | solution.py:85
  35.0 1.5 %collective-permute-done.4.came = f32[512,128]{1,0:T(8,128)S(1)} collective-permute-done((f32[512,128]{1,0:T(8,128)S(1)}, f32[512,128]{1,0:T(8,128)S(1)}, u32[]{:S(2)}, u32[]{:S(2)}) %collective-permute-start.4) | collective-permute-done | bytes 262176 | tf_op jit(solution)/shard_map/ppermute | solution.py:347
  36.5 6.1 %collective-permute-done.5.edge3.refs_1_ = f32[1024,128]{1,0:T(8,128)S(1)} collective-permute-done((f32[1024,128]{1,0:T(8,128)S(1)}, f32[1024,128]{1,0:T(8,128)S(1)}, u32[]{:S(2)}, u32[]{:S(2)}) %collective-permute-start.5) | collective-permute-done | bytes 524320 | tf_op jit(solution)/shard_map/ppermute | solution.py:344
  42.6 0.7 shard_map.51
  43.5 1.5 %collective-permute-done.6.came = f32[512,128]{1,0:T(8,128)S(1)} collective-permute-done((f32[512,128]{1,0:T(8,128)S(1)}, f32[512,128]{1,0:T(8,128)S(1)}, u32[]{:S(2)}, u32[]{:S(2)}) %collective-permute-start.6) | collective-permute-done | bytes 262176 | tf_op jit(solution)/shard_map/ppermute | solution.py:347
  45.0 1.6 %collective-permute-start.7 = (f32[256,128]{1,0:T(8,128)S(1)}, f32[256,128]{1,0:T(8,128)S(1)}, u32[]{:S(2)}, u32[]{:S(2)}) collective-permute-start(f32[256,128]{1,0:T(8,128)S(1)} %get-tuple-element.54), channel_id=1, source_target_pairs={{0,2},{2,0},{1,3},{3,1},{4,6},{6,4},{5,7},{7,5},{8,10},{10,8},{9,1... | collective-permute-start | bytes 393224 | tf_op jit(solution)/shard_map/ppermute | solution.py:350
  47.9 3.6 %collective-permute-done.7.two = f32[256,128]{1,0:T(8,128)S(1)} collective-permute-done((f32[256,128]{1,0:T(8,128)S(1)}, f32[256,128]{1,0:T(8,128)S(1)}, u32[]{:S(2)}, u32[]{:S(2)}) %collective-permute-start.7) | collective-permute-done | bytes 131104 | tf_op jit(solution)/shard_map/ppermute | solution.py:350
  51.7 3.4 %collective-permute-start.8 = (f32[256,128]{1,0:T(8,128)S(1)}, f32[256,128]{1,0:T(8,128)S(1)}, u32[]{:S(2)}, u32[]{:S(2)}) collective-permute-start(f32[256,128]{1,0:T(8,128)S(1)} %shard_map.53.low.low2), channel_id=1, source_target_pairs={{0,4},{12,8},{1,5},{13,9},{2,6},{14,10},{3,7},{15,11},{16,20},{28,... | collective-permute-start | bytes 393224 | tf_op jit(solution)/shard_map/ppermute | solution.py:344
  55.1 1.3 %collective-permute-start.11 = (f32[256,128]{1,0:T(8,128)S(1)}, f32[256,128]{1,0:T(8,128)S(1)}, u32[]{:S(2)}, u32[]{:S(2)}) collective-permute-start(f32[256,128]{1,0:T(8,128)S(1)} %shard_map.53.low.low2), channel_id=1, source_target_pairs={{0,8},{1,9},{2,10},{3,11},{16,24},{17,25},{18,26},{19,27}} | collective-permute-start | bytes 393224 | tf_op jit(solution)/shard_map/ppermute | solution.py:344
  56.7 1.8 %collective-permute-done.8.solved.first.zero = f32[256,128]{1,0:T(8,128)S(1)} collective-permute-done((f32[256,128]{1,0:T(8,128)S(1)}, f32[256,128]{1,0:T(8,128)S(1)}, u32[]{:S(2)}, u32[]{:S(2)}) %collective-permute-start.8) | collective-permute-done | bytes 131104 | tf_op jit(solution)/shard_map/ppermute | solution.py:344
  58.5 1.4 %collective-permute-done.11.zero = f32[256,128]{1,0:T(8,128)S(1)} collective-permute-done((f32[256,128]{1,0:T(8,128)S(1)}, f32[256,128]{1,0:T(8,128)S(1)}, u32[]{:S(2)}, u32[]{:S(2)}) %collective-permute-start.11) | collective-permute-done | bytes 131104 | tf_op jit(solution)/shard_map/ppermute | solution.py:344
  60.8 5.9 %collective-permute-start.16 = (f32[256,128]{1,0:T(8,128)S(1)}, f32[256,128]{1,0:T(8,128)S(1)}, u32[]{:S(2)}, u32[]{:S(2)}) collective-permute-start(f32[256,128]{1,0:T(8,128)S(1)} %get-tuple-element.57.top2.top_in), channel_id=1, source_target_pairs={{0,8},{1,9},{2,10},{3,11},{16,24},{17,25},{18,26},{19,27}} | collective-permute-start | bytes 393224 | tf_op jit(solution)/shard_map/ppermute | solution.py:344
  68.2 1.9 %collective-permute-done.16.value4 = f32[256,128]{1,0:T(8,128)S(1)} collective-permute-done((f32[256,128]{1,0:T(8,128)S(1)}, f32[256,128]{1,0:T(8,128)S(1)}, u32[]{:S(2)}, u32[]{:S(2)}) %collective-permute-start.16) | collective-permute-done | bytes 131104 | tf_op jit(solution)/shard_map/ppermute | solution.py:344
  70.2 1.3 %collective-permute-start.18 = (f32[256,128]{1,0:T(8,128)S(1)}, f32[256,128]{1,0:T(8,128)S(1)}, u32[]{:S(2)}, u32[]{:S(2)}) collective-permute-start(f32[256,128]{1,0:T(8,128)S(1)} %get-tuple-element.71), channel_id=1, source_target_pairs={{8,0},{9,1},{10,2},{11,3},{24,16},{25,17},{26,18},{27,19}} | collective-permute-start | bytes 393224 | tf_op jit(solution)/shard_map/ppermute | solution.py:344
  73.5 9.9 %collective-permute-done.18.block4 = f32[256,128]{1,0:T(8,128)S(1)} collective-permute-done((f32[256,128]{1,0:T(8,128)S(1)}, f32[256,128]{1,0:T(8,128)S(1)}, u32[]{:S(2)}, u32[]{:S(2)}) %collective-permute-start.18) | collective-permute-done | bytes 131104 | tf_op jit(solution)/shard_map/ppermute | solution.py:344
  83.4 0.7 shard_map.62
  (40 shorter events, 7.8 us)
Async XLA Ops:
  0.0 15.2 %collective-permute-start.1 = (f32[1024,128]{1,0:T(8,128)}, f32[1024,128]{1,0:T(8,128)S(1)}, u32[]{:S(2)}, u32[]{:S(2)}) collective-permute-start(f32[1024,128]{1,0:T(8,128)} %own.1), channel_id=1, source_target_pairs={{0,4},{4,0},{8,12},{12,8},{1,5},{5,1},{9,13},{13,9},{2,6},{6,2},{1... | collective-permute-start | bytes 1572872 | tf_op jit(solution)/shard_map/ppermute | solution.py:344
  3.0 12.8 %collective-permute-start = (f32[1024,128]{1,0:T(8,128)}, f32[1024,128]{1,0:T(8,128)S(1)}, u32[]{:S(2)}, u32[]{:S(2)}) collective-permute-start(f32[1024,128]{1,0:T(8,128)} %own.1), channel_id=1, source_target_pairs={{4,8},{8,4},{5,9},{9,5},{6,10},{10,6},{7,11},{11,7},{20,24},{24,20... | collective-permute-start | bytes 1572872 | tf_op jit(solution)/shard_map/ppermute | solution.py:344
  15.2 8.6 %collective-permute-start.3 = (f32[1024,128]{1,0:T(8,128)S(1)}, f32[1024,128]{1,0:T(8,128)S(1)}, u32[]{:S(2)}, u32[]{:S(2)}) collective-permute-start(f32[1024,128]{1,0:T(8,128)S(1)} %collective-permute-done.1.edge1), channel_id=1, source_target_pairs={{4,8},{8,4},{5,9},{9,5},{6,10},{10,6},{7,11},{11,7},{20,24},{24,20... | collective-permute-start | bytes 1572872 | tf_op jit(solution)/shard_map/ppermute | solution.py:344
  17.1 15.2 %collective-permute-start.2 = (f32[1024,128]{1,0:T(8,128)S(1)}, f32[1024,128]{1,0:T(8,128)S(1)}, u32[]{:S(2)}, u32[]{:S(2)}) collective-permute-start(f32[1024,128]{1,0:T(8,128)S(1)} %shard_map.46), channel_id=1, source_target_pairs={{0,4},{4,0},{8,12},{12,8},{1,5},{5,1},{9,13},{13,9},{2,6},{6,2},{1... | collective-permute-start | bytes 1572872 | tf_op jit(solution)/shard_map/ppermute | solution.py:344
  23.8 9.3 %copy-start = (f32[1024,128]{1,0:T(8,128)S(1)}, f32[1024,128]{1,0:T(8,128)}, u32[]{:S(2)}) copy-start(f32[1024,128]{1,0:T(8,128)} %own.1) | copy-start | bytes 1572868
  23.8 18.8 %collective-permute-start.5 = (f32[1024,128]{1,0:T(8,128)S(1)}, f32[1024,128]{1,0:T(8,128)S(1)}, u32[]{:S(2)}, u32[]{:S(2)}) collective-permute-start(f32[1024,128]{1,0:T(8,128)S(1)} %shard_map.48.middle2), channel_id=1, source_target_pairs={{0,4},{4,0},{8,12},{12,8},{1,5},{5,1},{9,13},{13,9},{2,6},{6,2},{1... | collective-permute-start | bytes 1572872 | tf_op jit(solution)/shard_map/ppermute | solution.py:344
  32.3 27.6 %collective-permute-start.13 = (f32[2048,128]{1,0:T(8,128)S(1)}, f32[2048,128]{1,0:T(8,128)S(1)}, u32[]{:S(2)}, u32[]{:S(2)}) collective-permute-start(f32[2048,128]{1,0:T(8,128)S(1)} %shard_map.56), channel_id=1, source_target_pairs={{4,8},{5,9},{6,10},{7,11},{20,24},{21,25},{22,26},{23,27}} | collective-permute-start | bytes 3145736 | tf_op jit(solution)/shard_map/ppermute | solution.py:344
  34.9 1.6 %collective-permute-start.4 = (f32[512,128]{1,0:T(8,128)S(1)}, f32[512,128]{1,0:T(8,128)S(1)}, u32[]{:S(2)}, u32[]{:S(2)}) collective-permute-start(f32[512,128]{1,0:T(8,128)S(1)} %get-tuple-element.49), channel_id=1, source_target_pairs={{0,1},{1,0},{2,3},{3,2},{4,5},{5,4},{6,7},{7,6},{8,9},{9,8},{10,11... | collective-permute-start | bytes 786440 | tf_op jit(solution)/shard_map/ppermute | solution.py:347
  43.4 1.6 %collective-permute-start.6 = (f32[512,128]{1,0:T(8,128)S(1)}, f32[512,128]{1,0:T(8,128)S(1)}, u32[]{:S(2)}, u32[]{:S(2)}) collective-permute-start(f32[512,128]{1,0:T(8,128)S(1)} %get-tuple-element.51), channel_id=1, source_target_pairs={{0,1},{1,0},{2,3},{3,2},{4,5},{5,4},{6,7},{7,6},{8,9},{9,8},{10,11... | collective-permute-start | bytes 786440 | tf_op jit(solution)/shard_map/ppermute | solution.py:347
  45.0 6.4 %collective-permute-start.7 = (f32[256,128]{1,0:T(8,128)S(1)}, f32[256,128]{1,0:T(8,128)S(1)}, u32[]{:S(2)}, u32[]{:S(2)}) collective-permute-start(f32[256,128]{1,0:T(8,128)S(1)} %get-tuple-element.54), channel_id=1, source_target_pairs={{0,2},{2,0},{1,3},{3,1},{4,6},{6,4},{5,7},{7,5},{8,10},{10,8},{9,1... | collective-permute-start | bytes 393224 | tf_op jit(solution)/shard_map/ppermute | solution.py:350
  46.6 13.3 %collective-permute-start.12 = (f32[512,128]{1,0:T(8,128)S(1)}, f32[512,128]{1,0:T(8,128)S(1)}, u32[]{:S(2)}, u32[]{:S(2)}) collective-permute-start(f32[512,128]{1,0:T(8,128)S(1)} %get-tuple-element.59), channel_id=1, source_target_pairs={{12,8},{13,9},{14,10},{15,11},{28,24},{29,25},{30,26},{31,27}} | collective-permute-start | bytes 786440 | tf_op jit(solution)/shard_map/ppermute | solution.py:344
  47.3 9.2 %collective-permute-start.9 = (f32[256,128]{1,0:T(8,128)S(1)}, f32[256,128]{1,0:T(8,128)S(1)}, u32[]{:S(2)}, u32[]{:S(2)}) collective-permute-start(f32[256,128]{1,0:T(8,128)S(1)} %get-tuple-element.55), channel_id=1, source_target_pairs={{0,2},{2,0},{1,3},{3,1},{4,6},{6,4},{5,7},{7,5},{8,10},{10,8},{9,1... | collective-permute-start | bytes 393224 | tf_op jit(solution)/shard_map/ppermute | solution.py:350
  51.7 6.8 %collective-permute-start.8 = (f32[256,128]{1,0:T(8,128)S(1)}, f32[256,128]{1,0:T(8,128)S(1)}, u32[]{:S(2)}, u32[]{:S(2)}) collective-permute-start(f32[256,128]{1,0:T(8,128)S(1)} %shard_map.53.low.low2), channel_id=1, source_target_pairs={{0,4},{12,8},{1,5},{13,9},{2,6},{14,10},{3,7},{15,11},{16,20},{28,... | collective-permute-start | bytes 393224 | tf_op jit(solution)/shard_map/ppermute | solution.py:344
  55.1 4.8 %collective-permute-start.11 = (f32[256,128]{1,0:T(8,128)S(1)}, f32[256,128]{1,0:T(8,128)S(1)}, u32[]{:S(2)}, u32[]{:S(2)}) collective-permute-start(f32[256,128]{1,0:T(8,128)S(1)} %shard_map.53.low.low2), channel_id=1, source_target_pairs={{0,8},{1,9},{2,10},{3,11},{16,24},{17,25},{18,26},{19,27}} | collective-permute-start | bytes 393224 | tf_op jit(solution)/shard_map/ppermute | solution.py:344
  60.1 8.1 %collective-permute-start.14 = (f32[4608,128]{1,0:T(8,128)S(1)}, f32[4608,128]{1,0:T(8,128)S(1)}, u32[]{:S(2)}, u32[]{:S(2)}) collective-permute-start(f32[4608,128]{1,0:T(8,128)S(1)} %shard_map.57.mine), channel_id=1, source_target_pairs={{0,1},{1,0},{2,3},{3,2},{4,5},{5,4},{6,7},{7,6},{8,9},{9,8},{10,11... | collective-permute-start | bytes 7077896 | tf_op jit(solution)/shard_map/ppermute | solution.py:347
  60.2 8.0 %collective-permute-start.10 = (f32[256,128]{1,0:T(8,128)S(1)}, f32[256,128]{1,0:T(8,128)S(1)}, u32[]{:S(2)}, u32[]{:S(2)}) collective-permute-start(f32[256,128]{1,0:T(8,128)S(1)} %shard_map.55.one.low1), channel_id=1, source_target_pairs={{4,8},{5,9},{6,10},{7,11},{20,24},{21,25},{22,26},{23,27}} | collective-permute-start | bytes 393224 | tf_op jit(solution)/shard_map/ppermute | solution.py:344
  60.8 9.3 %collective-permute-start.16 = (f32[256,128]{1,0:T(8,128)S(1)}, f32[256,128]{1,0:T(8,128)S(1)}, u32[]{:S(2)}, u32[]{:S(2)}) collective-permute-start(f32[256,128]{1,0:T(8,128)S(1)} %get-tuple-element.57.top2.top_in), channel_id=1, source_target_pairs={{0,8},{1,9},{2,10},{3,11},{16,24},{17,25},{18,26},{19,27}} | collective-permute-start | bytes 393224 | tf_op jit(solution)/shard_map/ppermute | solution.py:344
  66.8 3.4 %collective-permute-start.17 = (f32[256,128]{1,0:T(8,128)S(1)}, f32[256,128]{1,0:T(8,128)S(1)}, u32[]{:S(2)}, u32[]{:S(2)}) collective-permute-start(f32[256,128]{1,0:T(8,128)S(1)} %get-tuple-element.57.top2.top_in), channel_id=1, source_target_pairs={{12,8},{13,9},{14,10},{15,11},{28,24},{29,25},{30,26},{31,27}} | collective-permute-start | bytes 393224 | tf_op jit(solution)/shard_map/ppermute | solution.py:344
  67.5 2.7 %collective-permute-start.15 = (f32[256,128]{1,0:T(8,128)S(1)}, f32[256,128]{1,0:T(8,128)S(1)}, u32[]{:S(2)}, u32[]{:S(2)}) collective-permute-start(f32[256,128]{1,0:T(8,128)S(1)} %shard_map.60), channel_id=1, source_target_pairs={{4,8},{5,9},{6,10},{7,11},{20,24},{21,25},{22,26},{23,27}} | collective-permute-start | bytes 393224 | tf_op jit(solution)/shard_map/ppermute | solution.py:344
  70.2 13.2 %collective-permute-start.18 = (f32[256,128]{1,0:T(8,128)S(1)}, f32[256,128]{1,0:T(8,128)S(1)}, u32[]{:S(2)}, u32[]{:S(2)}) collective-permute-start(f32[256,128]{1,0:T(8,128)S(1)} %get-tuple-element.71), channel_id=1, source_target_pairs={{8,0},{9,1},{10,2},{11,3},{24,16},{25,17},{26,18},{27,19}} | collective-permute-start | bytes 393224 | tf_op jit(solution)/shard_map/ppermute | solution.py:344
  71.5 11.9 %collective-permute-start.19 = (f32[256,128]{1,0:T(8,128)S(1)}, f32[256,128]{1,0:T(8,128)S(1)}, u32[]{:S(2)}, u32[]{:S(2)}) collective-permute-start(f32[256,128]{1,0:T(8,128)S(1)} %get-tuple-element.72), channel_id=1, source_target_pairs={{8,4},{9,5},{10,6},{11,7},{24,20},{25,21},{26,22},{27,23}} | collective-permute-start | bytes 393224 | tf_op jit(solution)/shard_map/ppermute | solution.py:344
  72.1 11.2 %collective-permute-start.21 = (f32[256,128]{1,0:T(8,128)S(1)}, f32[256,128]{1,0:T(8,128)S(1)}, u32[]{:S(2)}, u32[]{:S(2)}) collective-permute-start(f32[256,128]{1,0:T(8,128)S(1)} %get-tuple-element.74), channel_id=1, source_target_pairs={{8,12},{9,13},{10,14},{11,15},{24,28},{25,29},{26,30},{27,31}} | collective-permute-start | bytes 393224 | tf_op jit(solution)/shard_map/ppermute | solution.py:344
  72.8 10.5 %collective-permute-start.20 = (f32[256,128]{1,0:T(8,128)S(1)}, f32[256,128]{1,0:T(8,128)S(1)}, u32[]{:S(2)}, u32[]{:S(2)}) collective-permute-start(f32[256,128]{1,0:T(8,128)S(1)} %get-tuple-element.73), channel_id=1, source_target_pairs={{8,12},{9,13},{10,14},{11,15},{24,28},{25,29},{26,30},{27,31}} | collective-permute-start | bytes 393224 | tf_op jit(solution)/shard_map/ppermute | solution.py:344

commit v10 on v9

--- a/solution.py
+++ b/solution.py
@@ -320,21 +320,24 @@
         value6[...] = state6[...] - sum(product(factor[TOP, columns(k)], pairs[k]) for k in range(1, 4))
 
 
-def fourth_kernel(
-    change4, change5, value6, change7, factor, mine, theirs, joint, value5, value4, top3, kept, block4, block5, sent
-):
+def fourth_kernel(change4, change5, mine, theirs, joint, value5, value4, block4, block5):
     @pl.when(lax.axis_index("row") == 2)
     def _():
         own, other = halves()
-        sides = ((own, mine), (other, theirs))
         pair4 = wide(value4[...] - change4[...])
         pair5 = wide(value5[...] - change5[...])
-        for rows, tiles in sides:
+        for rows, tiles in ((own, mine), (other, theirs)):
             block4[rows, :] = product(stacked(tiles, 13), pair4)
             block5[rows, :] = product(stacked(tiles, 17), pair5) - product(joint[rows, :], pair4)
+
+
+def fifth_kernel(block4, block5, value6, change7, factor, mine, theirs, top3, kept, sent):
+    @pl.when(lax.axis_index("row") == 2)
+    def _():
+        own, other = halves()
         four, five = wide(block4[...]), wide(block5[...])
         kept[...] = value6[...] - product(factor[TOP, columns(4)], four) - product(factor[TOP, columns(5)], five)
-        for rows, tiles in sides:
+        for rows, tiles in ((own, mine), (other, theirs)):
             start = top3[rows, :] - change7[rows, :] - product(stacked(tiles, 8), four)
             sent[rows, :] = start - product(stacked(tiles, 9), five)
 
@@ -401,9 +404,8 @@
         second, *states, factor, mine, theirs
     )
     last3 = move(block3, (2, 3))
-    kept, block4, block5, sent = call(fourth_kernel, [size] * 4)(
-        change4, change5, value6, change7, factor, mine, theirs, joint5, value5, value4, top3
-    )
+    block4, block5 = call(fourth_kernel, [size] * 2)(change4, change5, mine, theirs, joint5, value5, value4)
+    kept, sent = call(fifth_kernel, [size] * 2)(block4, block5, value6, change7, factor, mine, theirs, top3)
     last7 = move(sent, (2, 3))
     block5 = move(block5, (2, 1))
     block4 = move(block4, (2, 0))

time: 85.3 us -> 84 us (0.985)
  waiting for transfers between devices: 39.9 us -> 38.4 us
    ppermute x17, waiting for transfers between devices: 33.3 us -> 31.8 us  [move(): return lax.ppermute(x, 'row', list(pairs))]
    pallas_call x17 -> x18, Pallas kernels: 8.49 us -> 8.49 us  [run(): pl.pallas_call(kernel, out_shape=[(pltpu.VMEM if inside else jax.ShapeDty...]
where the time goes in v10:
time: 84 us; the launch traced here: 82.7 us
  waiting for transfers between devices  38.4 us (46%)
  starting transfers between devices  35.4 us (42%)
  Pallas kernels  8.49 us (10%)
    ppermute x17, starting transfers between devices, move(): return lax.ppermute(x, 'row', list(pairs))  33 us
    ppermute x17, waiting for transfers between devices, move(): return lax.ppermute(x, 'row', list(pairs))  31.8 us
    pallas_call x18, Pallas kernels, run(): pl.pallas_call(kernel, out_shape=[(pltpu.VMEM if inside else jax.ShapeDty...  8.49 us
    ppermute x2, waiting for transfers between devices, cross(): return lax.ppermute(x, 'col', [(0, 2), (2, 0), (1, 3), (3, 1)])  3.58 us
    ppermute x3, waiting for transfers between devices, swap(): return lax.ppermute(x, 'col', [(0, 1), (1, 0), (2, 3), (3, 2)])  3.02 us
    ppermute x2, starting transfers between devices, cross(): return lax.ppermute(x, 'col', [(0, 2), (2, 0), (1, 3), (3, 1)])  2.16 us
  transfers between devices with their start and end apart: 22, of which 10 were waited for; matrix products, arithmetic and copies ran while one was open for 0% of the time, Pallas kernels for 9%

profile of v10, /device:TPU:0, one launch (start us, length us, event | category | flops | bytes accessed | tf_op | source)
XLA Modules:
  0.0 82.7 jit_solution(10612625904130423393)
XLA Ops:
  0.0 3.0 %collective-permute-start.1 = (f32[1024,128]{1,0:T(8,128)}, f32[1024,128]{1,0:T(8,128)S(1)}, u32[]{:S(2)}, u32[]{:S(2)}) collective-permute-start(f32[1024,128]{1,0:T(8,128)} %own.1), channel_id=1, source_target_pairs={{0,4},{4,0},{8,12},{12,8},{1,5},{5,1},{9,13},{13,9},{2,6},{6,2},{1... | collective-permute-start | bytes 1572872 | tf_op jit(solution)/shard_map/ppermute | solution.py:347
  3.7 11.4 %collective-permute-done.1.edge1 = f32[1024,128]{1,0:T(8,128)S(1)} collective-permute-done((f32[1024,128]{1,0:T(8,128)}, f32[1024,128]{1,0:T(8,128)S(1)}, u32[]{:S(2)}, u32[]{:S(2)}) %collective-permute-start.1) | collective-permute-done | bytes 524320 | tf_op jit(solution)/shard_map/ppermute | solution.py:347
  15.9 1.2 %shard_map.46 = f32[1024,128]{1,0:T(8,128)S(1)} custom-call(f32[1024,128]{1,0:T(8,128)S(1)} %copy.7.x_in, f32[512,1536]{1,0:T(8,128)} %factor.3), custom_call_target="tpu_custom_call", output_to_operand_aliasing={{}: (0, {})} | custom-call | tf_op jit(solution)/shard_map/pallas_call | solution.py:85
  17.1 3.6 %collective-permute-start.2 = (f32[1024,128]{1,0:T(8,128)S(1)}, f32[1024,128]{1,0:T(8,128)S(1)}, u32[]{:S(2)}, u32[]{:S(2)}) collective-permute-start(f32[1024,128]{1,0:T(8,128)S(1)} %shard_map.46), channel_id=1, source_target_pairs={{0,4},{4,0},{8,12},{12,8},{1,5},{5,1},{9,13},{13,9},{2,6},{6,2},{1... | collective-permute-start | bytes 1572872 | tf_op jit(solution)/shard_map/ppermute | solution.py:347
  20.6 3.2 %shard_map.47 = (f32[512,1024]{1,0:T(8,128)S(1)}, f32[512,1536]{1,0:T(8,128)S(1)}, f32[512,128]{1,0:T(8,128)S(1)}, f32[1024,128]{1,0:T(8,128)S(1)}, f32[1024,128]{1,0:T(8,128)S(1)}, /*index=5*/f32[512,128]{1,0:T(8,128)S(1)}) custom-call(f32[512,1024]{1,0:T(8,128)} %past, f32[512,1536]{1,0:T(8,128)} %factor.3, f32[512,512]{1,0:T(8,128)} %side.1), custom_call_target="tpu_custom_call" | custom-call | tf_op jit(solution)/shard_map/pallas_call | solution.py:85
  23.8 7.7 %collective-permute-start.5 = (f32[1024,128]{1,0:T(8,128)S(1)}, f32[1024,128]{1,0:T(8,128)S(1)}, u32[]{:S(2)}, u32[]{:S(2)}) collective-permute-start(f32[1024,128]{1,0:T(8,128)S(1)} %shard_map.48.middle2), channel_id=1, source_target_pairs={{0,4},{4,0},{8,12},{12,8},{1,5},{5,1},{9,13},{13,9},{2,6},{6,2},{1... | collective-permute-start | bytes 1572872 | tf_op jit(solution)/shard_map/ppermute | solution.py:347
  31.6 0.7 collective-permute-done.2.edge2.refs_0_
  32.3 0.7 collective-permute-start.13
  33.1 1.8 %shard_map.49 = (f32[3,512,128]{2,1,0:T(8,128)S(1)}, f32[512,128]{1,0:T(8,128)S(1)}) custom-call(f32[512,1024]{1,0:T(8,128)S(1)} %get-tuple-element.43.past, f32[1024,128]{1,0:T(8,128)S(1)} %copy-done, f32[1024,128]{1,0:T(8,128)S(1)} %collective-permute-done.1.edge1, f32[1024,128]{1,0:T(8,128)S(1)} %collective-permute-done.2.edge2.refs_0_, ...), custom_call_target="tpu_custom_call" | custom-call | tf_op jit(solution)/shard_map/pallas_call | solution.py:85
  35.0 1.5 %collective-permute-done.4.came = f32[512,128]{1,0:T(8,128)S(1)} collective-permute-done((f32[512,128]{1,0:T(8,128)S(1)}, f32[512,128]{1,0:T(8,128)S(1)}, u32[]{:S(2)}, u32[]{:S(2)}) %collective-permute-start.4) | collective-permute-done | bytes 262176 | tf_op jit(solution)/shard_map/ppermute | solution.py:350
  36.5 6.1 %collective-permute-done.5.edge3.refs_1_ = f32[1024,128]{1,0:T(8,128)S(1)} collective-permute-done((f32[1024,128]{1,0:T(8,128)S(1)}, f32[1024,128]{1,0:T(8,128)S(1)}, u32[]{:S(2)}, u32[]{:S(2)}) %collective-permute-start.5) | collective-permute-done | bytes 524320 | tf_op jit(solution)/shard_map/ppermute | solution.py:347
  42.6 0.7 shard_map.51
  43.5 1.5 %collective-permute-done.6.came = f32[512,128]{1,0:T(8,128)S(1)} collective-permute-done((f32[512,128]{1,0:T(8,128)S(1)}, f32[512,128]{1,0:T(8,128)S(1)}, u32[]{:S(2)}, u32[]{:S(2)}) %collective-permute-start.6) | collective-permute-done | bytes 262176 | tf_op jit(solution)/shard_map/ppermute | solution.py:350
  45.0 1.6 %collective-permute-start.7 = (f32[256,128]{1,0:T(8,128)S(1)}, f32[256,128]{1,0:T(8,128)S(1)}, u32[]{:S(2)}, u32[]{:S(2)}) collective-permute-start(f32[256,128]{1,0:T(8,128)S(1)} %get-tuple-element.54), channel_id=1, source_target_pairs={{0,2},{2,0},{1,3},{3,1},{4,6},{6,4},{5,7},{7,5},{8,10},{10,8},{9,1... | collective-permute-start | bytes 393224 | tf_op jit(solution)/shard_map/ppermute | solution.py:353
  47.9 3.6 %collective-permute-done.7.two = f32[256,128]{1,0:T(8,128)S(1)} collective-permute-done((f32[256,128]{1,0:T(8,128)S(1)}, f32[256,128]{1,0:T(8,128)S(1)}, u32[]{:S(2)}, u32[]{:S(2)}) %collective-permute-start.7) | collective-permute-done | bytes 131104 | tf_op jit(solution)/shard_map/ppermute | solution.py:353
  51.7 3.4 %collective-permute-start.8 = (f32[256,128]{1,0:T(8,128)S(1)}, f32[256,128]{1,0:T(8,128)S(1)}, u32[]{:S(2)}, u32[]{:S(2)}) collective-permute-start(f32[256,128]{1,0:T(8,128)S(1)} %shard_map.53.low.low2), channel_id=1, source_target_pairs={{0,4},{12,8},{1,5},{13,9},{2,6},{14,10},{3,7},{15,11},{16,20},{28,... | collective-permute-start | bytes 393224 | tf_op jit(solution)/shard_map/ppermute | solution.py:347
  55.1 1.3 %collective-permute-start.11 = (f32[256,128]{1,0:T(8,128)S(1)}, f32[256,128]{1,0:T(8,128)S(1)}, u32[]{:S(2)}, u32[]{:S(2)}) collective-permute-start(f32[256,128]{1,0:T(8,128)S(1)} %shard_map.53.low.low2), channel_id=1, source_target_pairs={{0,8},{1,9},{2,10},{3,11},{16,24},{17,25},{18,26},{19,27}} | collective-permute-start | bytes 393224 | tf_op jit(solution)/shard_map/ppermute | solution.py:347
  56.7 1.8 %collective-permute-done.8.solved.first.zero = f32[256,128]{1,0:T(8,128)S(1)} collective-permute-done((f32[256,128]{1,0:T(8,128)S(1)}, f32[256,128]{1,0:T(8,128)S(1)}, u32[]{:S(2)}, u32[]{:S(2)}) %collective-permute-start.8) | collective-permute-done | bytes 131104 | tf_op jit(solution)/shard_map/ppermute | solution.py:347
  58.5 1.4 %collective-permute-done.11.zero = f32[256,128]{1,0:T(8,128)S(1)} collective-permute-done((f32[256,128]{1,0:T(8,128)S(1)}, f32[256,128]{1,0:T(8,128)S(1)}, u32[]{:S(2)}, u32[]{:S(2)}) %collective-permute-start.11) | collective-permute-done | bytes 131104 | tf_op jit(solution)/shard_map/ppermute | solution.py:347
  60.8 5.9 %collective-permute-start.16 = (f32[256,128]{1,0:T(8,128)S(1)}, f32[256,128]{1,0:T(8,128)S(1)}, u32[]{:S(2)}, u32[]{:S(2)}) collective-permute-start(f32[256,128]{1,0:T(8,128)S(1)} %get-tuple-element.57.top2.top_in), channel_id=1, source_target_pairs={{0,8},{1,9},{2,10},{3,11},{16,24},{17,25},{18,26},{19,27}} | collective-permute-start | bytes 393224 | tf_op jit(solution)/shard_map/ppermute | solution.py:347
  68.2 1.9 %collective-permute-done.16.value4 = f32[256,128]{1,0:T(8,128)S(1)} collective-permute-done((f32[256,128]{1,0:T(8,128)S(1)}, f32[256,128]{1,0:T(8,128)S(1)}, u32[]{:S(2)}, u32[]{:S(2)}) %collective-permute-start.16) | collective-permute-done | bytes 131104 | tf_op jit(solution)/shard_map/ppermute | solution.py:347
  70.2 1.3 %collective-permute-start.17 = (f32[256,128]{1,0:T(8,128)S(1)}, f32[256,128]{1,0:T(8,128)S(1)}, u32[]{:S(2)}, u32[]{:S(2)}) collective-permute-start(f32[256,128]{1,0:T(8,128)S(1)} %get-tuple-element.69.block4), channel_id=1, source_target_pairs={{8,0},{9,1},{10,2},{11,3},{24,16},{25,17},{26,18},{27,19}} | collective-permute-start | bytes 393224 | tf_op jit(solution)/shard_map/ppermute | solution.py:347
  73.5 8.4 %collective-permute-done.17.block4 = f32[256,128]{1,0:T(8,128)S(1)} collective-permute-done((f32[256,128]{1,0:T(8,128)S(1)}, f32[256,128]{1,0:T(8,128)S(1)}, u32[]{:S(2)}, u32[]{:S(2)}) %collective-permute-start.17) | collective-permute-done | bytes 131104 | tf_op jit(solution)/shard_map/ppermute | solution.py:347
  81.9 0.7 shard_map.63
  (41 shorter events, 7.8 us)
Async XLA Ops:
  0.0 15.2 %collective-permute-start.1 = (f32[1024,128]{1,0:T(8,128)}, f32[1024,128]{1,0:T(8,128)S(1)}, u32[]{:S(2)}, u32[]{:S(2)}) collective-permute-start(f32[1024,128]{1,0:T(8,128)} %own.1), channel_id=1, source_target_pairs={{0,4},{4,0},{8,12},{12,8},{1,5},{5,1},{9,13},{13,9},{2,6},{6,2},{1... | collective-permute-start | bytes 1572872 | tf_op jit(solution)/shard_map/ppermute | solution.py:347
  3.0 12.8 %collective-permute-start = (f32[1024,128]{1,0:T(8,128)}, f32[1024,128]{1,0:T(8,128)S(1)}, u32[]{:S(2)}, u32[]{:S(2)}) collective-permute-start(f32[1024,128]{1,0:T(8,128)} %own.1), channel_id=1, source_target_pairs={{4,8},{8,4},{5,9},{9,5},{6,10},{10,6},{7,11},{11,7},{20,24},{24,20... | collective-permute-start | bytes 1572872 | tf_op jit(solution)/shard_map/ppermute | solution.py:347
  15.2 8.6 %collective-permute-start.3 = (f32[1024,128]{1,0:T(8,128)S(1)}, f32[1024,128]{1,0:T(8,128)S(1)}, u32[]{:S(2)}, u32[]{:S(2)}) collective-permute-start(f32[1024,128]{1,0:T(8,128)S(1)} %collective-permute-done.1.edge1), channel_id=1, source_target_pairs={{4,8},{8,4},{5,9},{9,5},{6,10},{10,6},{7,11},{11,7},{20,24},{24,20... | collective-permute-start | bytes 1572872 | tf_op jit(solution)/shard_map/ppermute | solution.py:347
  17.1 15.2 %collective-permute-start.2 = (f32[1024,128]{1,0:T(8,128)S(1)}, f32[1024,128]{1,0:T(8,128)S(1)}, u32[]{:S(2)}, u32[]{:S(2)}) collective-permute-start(f32[1024,128]{1,0:T(8,128)S(1)} %shard_map.46), channel_id=1, source_target_pairs={{0,4},{4,0},{8,12},{12,8},{1,5},{5,1},{9,13},{13,9},{2,6},{6,2},{1... | collective-permute-start | bytes 1572872 | tf_op jit(solution)/shard_map/ppermute | solution.py:347
  23.8 9.3 %copy-start = (f32[1024,128]{1,0:T(8,128)S(1)}, f32[1024,128]{1,0:T(8,128)}, u32[]{:S(2)}) copy-start(f32[1024,128]{1,0:T(8,128)} %own.1) | copy-start | bytes 1572868
  23.8 18.8 %collective-permute-start.5 = (f32[1024,128]{1,0:T(8,128)S(1)}, f32[1024,128]{1,0:T(8,128)S(1)}, u32[]{:S(2)}, u32[]{:S(2)}) collective-permute-start(f32[1024,128]{1,0:T(8,128)S(1)} %shard_map.48.middle2), channel_id=1, source_target_pairs={{0,4},{4,0},{8,12},{12,8},{1,5},{5,1},{9,13},{13,9},{2,6},{6,2},{1... | collective-permute-start | bytes 1572872 | tf_op jit(solution)/shard_map/ppermute | solution.py:347
  32.3 27.6 %collective-permute-start.13 = (f32[2048,128]{1,0:T(8,128)S(1)}, f32[2048,128]{1,0:T(8,128)S(1)}, u32[]{:S(2)}, u32[]{:S(2)}) collective-permute-start(f32[2048,128]{1,0:T(8,128)S(1)} %shard_map.56), channel_id=1, source_target_pairs={{4,8},{5,9},{6,10},{7,11},{20,24},{21,25},{22,26},{23,27}} | collective-permute-start | bytes 3145736 | tf_op jit(solution)/shard_map/ppermute | solution.py:347
  34.9 1.6 %collective-permute-start.4 = (f32[512,128]{1,0:T(8,128)S(1)}, f32[512,128]{1,0:T(8,128)S(1)}, u32[]{:S(2)}, u32[]{:S(2)}) collective-permute-start(f32[512,128]{1,0:T(8,128)S(1)} %get-tuple-element.49), channel_id=1, source_target_pairs={{0,1},{1,0},{2,3},{3,2},{4,5},{5,4},{6,7},{7,6},{8,9},{9,8},{10,11... | collective-permute-start | bytes 786440 | tf_op jit(solution)/shard_map/ppermute | solution.py:350
  43.4 1.6 %collective-permute-start.6 = (f32[512,128]{1,0:T(8,128)S(1)}, f32[512,128]{1,0:T(8,128)S(1)}, u32[]{:S(2)}, u32[]{:S(2)}) collective-permute-start(f32[512,128]{1,0:T(8,128)S(1)} %get-tuple-element.51), channel_id=1, source_target_pairs={{0,1},{1,0},{2,3},{3,2},{4,5},{5,4},{6,7},{7,6},{8,9},{9,8},{10,11... | collective-permute-start | bytes 786440 | tf_op jit(solution)/shard_map/ppermute | solution.py:350
  45.0 6.4 %collective-permute-start.7 = (f32[256,128]{1,0:T(8,128)S(1)}, f32[256,128]{1,0:T(8,128)S(1)}, u32[]{:S(2)}, u32[]{:S(2)}) collective-permute-start(f32[256,128]{1,0:T(8,128)S(1)} %get-tuple-element.54), channel_id=1, source_target_pairs={{0,2},{2,0},{1,3},{3,1},{4,6},{6,4},{5,7},{7,5},{8,10},{10,8},{9,1... | collective-permute-start | bytes 393224 | tf_op jit(solution)/shard_map/ppermute | solution.py:353
  46.6 13.3 %collective-permute-start.12 = (f32[512,128]{1,0:T(8,128)S(1)}, f32[512,128]{1,0:T(8,128)S(1)}, u32[]{:S(2)}, u32[]{:S(2)}) collective-permute-start(f32[512,128]{1,0:T(8,128)S(1)} %get-tuple-element.59), channel_id=1, source_target_pairs={{12,8},{13,9},{14,10},{15,11},{28,24},{29,25},{30,26},{31,27}} | collective-permute-start | bytes 786440 | tf_op jit(solution)/shard_map/ppermute | solution.py:347
  47.3 9.2 %collective-permute-start.9 = (f32[256,128]{1,0:T(8,128)S(1)}, f32[256,128]{1,0:T(8,128)S(1)}, u32[]{:S(2)}, u32[]{:S(2)}) collective-permute-start(f32[256,128]{1,0:T(8,128)S(1)} %get-tuple-element.55), channel_id=1, source_target_pairs={{0,2},{2,0},{1,3},{3,1},{4,6},{6,4},{5,7},{7,5},{8,10},{10,8},{9,1... | collective-permute-start | bytes 393224 | tf_op jit(solution)/shard_map/ppermute | solution.py:353
  51.7 6.8 %collective-permute-start.8 = (f32[256,128]{1,0:T(8,128)S(1)}, f32[256,128]{1,0:T(8,128)S(1)}, u32[]{:S(2)}, u32[]{:S(2)}) collective-permute-start(f32[256,128]{1,0:T(8,128)S(1)} %shard_map.53.low.low2), channel_id=1, source_target_pairs={{0,4},{12,8},{1,5},{13,9},{2,6},{14,10},{3,7},{15,11},{16,20},{28,... | collective-permute-start | bytes 393224 | tf_op jit(solution)/shard_map/ppermute | solution.py:347
  55.1 4.8 %collective-permute-start.11 = (f32[256,128]{1,0:T(8,128)S(1)}, f32[256,128]{1,0:T(8,128)S(1)}, u32[]{:S(2)}, u32[]{:S(2)}) collective-permute-start(f32[256,128]{1,0:T(8,128)S(1)} %shard_map.53.low.low2), channel_id=1, source_target_pairs={{0,8},{1,9},{2,10},{3,11},{16,24},{17,25},{18,26},{19,27}} | collective-permute-start | bytes 393224 | tf_op jit(solution)/shard_map/ppermute | solution.py:347
  60.1 8.1 %collective-permute-start.14 = (f32[4608,128]{1,0:T(8,128)S(1)}, f32[4608,128]{1,0:T(8,128)S(1)}, u32[]{:S(2)}, u32[]{:S(2)}) collective-permute-start(f32[4608,128]{1,0:T(8,128)S(1)} %shard_map.57.mine), channel_id=1, source_target_pairs={{0,1},{1,0},{2,3},{3,2},{4,5},{5,4},{6,7},{7,6},{8,9},{9,8},{10,11... | collective-permute-start | bytes 7077896 | tf_op jit(solution)/shard_map/ppermute | solution.py:350
  60.2 8.0 %collective-permute-start.10 = (f32[256,128]{1,0:T(8,128)S(1)}, f32[256,128]{1,0:T(8,128)S(1)}, u32[]{:S(2)}, u32[]{:S(2)}) collective-permute-start(f32[256,128]{1,0:T(8,128)S(1)} %shard_map.55.one.low1), channel_id=1, source_target_pairs={{4,8},{5,9},{6,10},{7,11},{20,24},{21,25},{22,26},{23,27}} | collective-permute-start | bytes 393224 | tf_op jit(solution)/shard_map/ppermute | solution.py:347
  60.8 9.3 %collective-permute-start.16 = (f32[256,128]{1,0:T(8,128)S(1)}, f32[256,128]{1,0:T(8,128)S(1)}, u32[]{:S(2)}, u32[]{:S(2)}) collective-permute-start(f32[256,128]{1,0:T(8,128)S(1)} %get-tuple-element.57.top2.top_in), channel_id=1, source_target_pairs={{0,8},{1,9},{2,10},{3,11},{16,24},{17,25},{18,26},{19,27}} | collective-permute-start | bytes 393224 | tf_op jit(solution)/shard_map/ppermute | solution.py:347
  66.8 3.4 %collective-permute-start.15 = (f32[256,128]{1,0:T(8,128)S(1)}, f32[256,128]{1,0:T(8,128)S(1)}, u32[]{:S(2)}, u32[]{:S(2)}) collective-permute-start(f32[256,128]{1,0:T(8,128)S(1)} %shard_map.60), channel_id=1, source_target_pairs={{4,8},{5,9},{6,10},{7,11},{20,24},{21,25},{22,26},{23,27}} | collective-permute-start | bytes 393224 | tf_op jit(solution)/shard_map/ppermute | solution.py:347
  67.5 4.0 %collective-permute-start.20 = (f32[256,128]{1,0:T(8,128)S(1)}, f32[256,128]{1,0:T(8,128)S(1)}, u32[]{:S(2)}, u32[]{:S(2)}) collective-permute-start(f32[256,128]{1,0:T(8,128)S(1)} %get-tuple-element.57.top2.top_in), channel_id=1, source_target_pairs={{12,8},{13,9},{14,10},{15,11},{28,24},{29,25},{30,26},{31,27}} | collective-permute-start | bytes 393224 | tf_op jit(solution)/shard_map/ppermute | solution.py:347
  70.2 11.8 %collective-permute-start.17 = (f32[256,128]{1,0:T(8,128)S(1)}, f32[256,128]{1,0:T(8,128)S(1)}, u32[]{:S(2)}, u32[]{:S(2)}) collective-permute-start(f32[256,128]{1,0:T(8,128)S(1)} %get-tuple-element.69.block4), channel_id=1, source_target_pairs={{8,0},{9,1},{10,2},{11,3},{24,16},{25,17},{26,18},{27,19}} | collective-permute-start | bytes 393224 | tf_op jit(solution)/shard_map/ppermute | solution.py:347
  71.5 2.0 %collective-permute-start.21 = (f32[256,128]{1,0:T(8,128)S(1)}, f32[256,128]{1,0:T(8,128)S(1)}, u32[]{:S(2)}, u32[]{:S(2)}) collective-permute-start(f32[256,128]{1,0:T(8,128)S(1)} %get-tuple-element.74), channel_id=1, source_target_pairs={{8,12},{9,13},{10,14},{11,15},{24,28},{25,29},{26,30},{27,31}} | collective-permute-start | bytes 393224 | tf_op jit(solution)/shard_map/ppermute | solution.py:347
  72.2 9.8 %collective-permute-start.18 = (f32[256,128]{1,0:T(8,128)S(1)}, f32[256,128]{1,0:T(8,128)S(1)}, u32[]{:S(2)}, u32[]{:S(2)}) collective-permute-start(f32[256,128]{1,0:T(8,128)S(1)} %get-tuple-element.70.block5), channel_id=1, source_target_pairs={{8,4},{9,5},{10,6},{11,7},{24,20},{25,21},{26,22},{27,23}} | collective-permute-start | bytes 393224 | tf_op jit(solution)/shard_map/ppermute | solution.py:347
  72.9 9.1 %collective-permute-start.19 = (f32[256,128]{1,0:T(8,128)S(1)}, f32[256,128]{1,0:T(8,128)S(1)}, u32[]{:S(2)}, u32[]{:S(2)}) collective-permute-start(f32[256,128]{1,0:T(8,128)S(1)} %get-tuple-element.71), channel_id=1, source_target_pairs={{8,12},{9,13},{10,14},{11,15},{24,28},{25,29},{26,30},{27,31}} | collective-permute-start | bytes 393224 | tf_op jit(solution)/shard_map/ppermute | solution.py:347
